TPU v7x, 128 devices: a whole 4x4x4 slice. The times are simulated.
128 devices in a mesh: seq: 16 (over x, z), hx: 8 (over y, core).
Axes of the slice: x: 4, y: 4, z: 4, core: 2. Of those that a mesh axis runs over, the one named last changes fastest.
Arguments:
- query: bfloat16 [16384, 8192], P('seq', 'hx'), may hold values from -6 to 6
- key_in: bfloat16 [16384, 8192], P('seq', 'hx'), may hold values from -6 to 6
- value: bfloat16 [16384, 8192], P('seq', 'hx'), may hold values from -6 to 6
- head_gain: float32 [8192], P('hx'), may hold values from 0.1 to 1.9
- out_weight: bfloat16 [8192, 6144], P('hx', 'seq'), may hold values from -0.0625 to 0.0625
- residual: bfloat16 [16384, 6144], P(('seq', 'hx')), may hold values from -6 to 6
Outputs:
- mixed: bfloat16 [16384, 6144], P(('seq', 'hx'))
All inputs are finite; a program needn't handle non-finite values.
Results may differ from a plain program's by a relative error of at most 0.014.
Values may be sent and summed in bfloat16 or wider, within the bound.
No kernel may reach another device: no remote copies, remote signals or barrier semaphores. Data moves between devices by JAX's collectives and lax.ppermute only.
A program may use at most 128 MiB of HBM per device.

v0:
```python
import jax
import jax.numpy as jnp
from jax import lax
from jax.sharding import PartitionSpec as P

DH = 128


def activate(array):
    return jax.nn.silu(array.astype(jnp.float32)).astype(jnp.bfloat16)


def per_device(query, key_in, value, head_gain, out_weight, residual):
    highest = lax.Precision.HIGHEST
    tokens_here, width = query.shape
    heads = width // DH
    q_act = activate(query).reshape(tokens_here, heads, DH)
    k_act = activate(key_in).reshape(tokens_here, heads, DH)
    v_heads = value.reshape(tokens_here, heads, DH)
    blocks = min(512, tokens_here)
    count = tokens_here // blocks
    rows = jnp.arange(blocks, dtype=jnp.int32)
    lower = rows[:, None] >= rows[None, :]
    running = jnp.zeros((heads, DH, DH), jnp.float32)
    pieces = []
    for index in range(count):
        q_part = q_act[index * blocks : (index + 1) * blocks]
        k_part = k_act[index * blocks : (index + 1) * blocks]
        v_part = v_heads[index * blocks : (index + 1) * blocks]
        scores = jnp.einsum("thd,shd->hts", q_part, k_part, preferred_element_type=jnp.float32)
        scores = jnp.where(lower[None, :, :], scores, jnp.zeros_like(scores))
        inner = jnp.einsum("hts,she->the", scores, v_part.astype(jnp.float32), precision=highest)
        if index > 0:
            inner = inner + jnp.einsum(
                "thd,hde->the", q_part.astype(jnp.float32), running, precision=highest
            )
        pieces.append(inner)
        running = running + jnp.einsum(
            "thd,the->hde", k_part, v_part, preferred_element_type=jnp.float32
        )
    local_part = jnp.concatenate(pieces, axis=0)
    empty = jnp.zeros((heads, DH, DH), jnp.float32)
    position = lax.axis_index("seq")
    piece = lax.all_gather(running[None].astype(jnp.bfloat16), "seq", axis=0, tiled=True).astype(
        jnp.float32
    )
    ranks = jnp.arange(piece.shape[0], dtype=jnp.int32)
    keep = (ranks < position)[:, None, None, None]
    prefix = empty + jnp.sum(jnp.where(keep, piece, jnp.zeros_like(piece)), axis=0)
    attended = local_part + jnp.einsum(
        "thd,hde->the", q_act.astype(jnp.float32), prefix, precision=highest
    )
    meansq = jnp.mean(attended * attended, axis=-1, keepdims=True)
    normed = attended * lax.rsqrt(meansq + 1e-06) * head_gain.reshape(heads, DH)
    normed = normed.astype(jnp.bfloat16).reshape(tokens_here, width)
    full_weight = lax.all_gather(out_weight, "seq", axis=1, tiled=True)
    summed = lax.psum_scatter(
        jnp.dot(normed, full_weight, preferred_element_type=jnp.float32).astype(jnp.bfloat16),
        "hx",
        scatter_dimension=0,
        tiled=True,
    ).astype(jnp.float32)
    return (summed + residual.astype(jnp.float32)).astype(jnp.bfloat16)


def solution(mesh):
    return jax.shard_map(
        per_device,
        mesh=mesh,
        in_specs=(
            P("seq", "hx"),
            P("seq", "hx"),
            P("seq", "hx"),
            P("hx"),
            P("hx", "seq"),
            P(("seq", "hx"), None),
        ),
        out_specs=P(("seq", "hx"), None),
        check_vma=False,
    )
```

profile of v0, /device:TPU:1, one launch (start us, length us, event | category | flops | bytes accessed | tf_op | source)
XLA Modules:
  0.0 277.5 jit_solution(6667149055458355304)
XLA Ops:
  6.5 0.0 all-gather.6.cloned.1.call-start
  6.5 2.9 %copy.46 = bf16[1024,1024]{0,1:T(8,128)(2,1)S(1)} copy(bf16[1024,1024]{1,0:T(8,128)(2,1)} %param.7) | data formatting | bytes 4194304 | tf_op args[1]
  9.4 0.0 copy-start.9
  9.4 1.2 fusion.12
  10.6 1.1 fusion.25
  11.8 0.0 copy-done.9
  11.8 1.3 fusion.24
  13.1 0.5 copy.79
  13.6 0.0 copy-start.2
  13.6 1.9 copy.78
  15.5 0.0 copy-done
  15.5 0.4 fusion.28
  16.0 0.0 copy-start.7
  16.0 0.8 copy-done.7
  16.8 2.4 fusion.20
  19.2 0.0 all-gather.6.cloned.1.call-update
  19.2 0.0 all-gather.4.cloned.1.call-start
  19.2 0.7 all-gather.4.cloned.1.call-update
  19.9 0.0 copy-done.2
  19.9 0.0 reduce-scatter.2.cloned.1.call-start
  20.0 4.0 %copy.45 = bf16[1024,1024]{0,1:T(8,128)(2,1)} copy(bf16[1024,1024]{1,0:T(8,128)(2,1)} %param.6) | data formatting | bytes 4194304 | tf_op args[0]
  24.0 0.1 iota_compare_fusion
  24.0 0.0 copy-start.4
  24.1 2.9 %fusion.8 = bf16[1024,1024]{0,1:T(8,128)(2,1)S(1)} fusion(bf16[1024,1024]{0,1:T(8,128)(2,1)} %copy.45), kind=kLoop, calls=%fused_computation.14 | loop fusion | flops 6291456 | bytes 4194304 | tf_op jit(solution)/shard_map/convert_element_type | solution.py:10
  27.0 0.1 fusion.23
  27.1 0.0 copy-done.4
  27.1 0.0 copy-start.3
  27.1 1.3 fusion.27
  28.4 0.0 copy-done.3
  28.4 0.0 copy-start.8
  28.4 4.5 %fusion.1 = f32[8,512,128]{2,1,0:T(8,128)S(1)} fusion(bf16[512,8,128]{0,2,1:T(8,128)(2,1)S(1)} %bitcast.41, f32[8,512,512]{2,1,0:T(8,128)S(1)} %fusion.27, pred[512,512]{1,0:T(8,128)(4,1)S(1)} %iota_compare_fusion), kind=kOutput, calls=%fused_computation.3 | convolution fusion | flops 3223322624 | bytes 11796480 | tf_op jit(solution)/shard_map/hts,she->the/dot_general | solution.py:32
  33.0 0.0 copy-done.8
  33.0 0.0 copy-start.1
  33.0 2.5 bitcast_add_fusion
  35.5 0.0 copy-done.1
  35.5 1.3 fusion.26
  36.8 6.0 %fusion.17 = f32[512,8,128]{2,0,1:T(8,128)} fusion(bf16[512,8,128]{0,2,1:T(8,128)(2,1)S(1)} %bitcast.37, f32[8,512,512]{2,1,0:T(8,128)S(1)} %fusion.26, pred[512,512]{1,0:T(8,128)(4,1)S(1)} %iota_compare_fusion), kind=kOutput, calls=%fused_computation.28 | convolution fusion | flops 3223322624 | bytes 11796480 | tf_op jit(solution)/shard_map/hts,she->the/dot_general | solution.py:32
  42.8 31.4 %all-gather.6.cloned.1.call-done = bf16[128,128,128]{2,1,0:T(8,128)(2,1)} async-done(((bf16[8,128,128]{2,1,0:T(8,128)(2,1)}), bf16[128,128,128]{2,1,0:T(8,128)(2,1)}) %all-gather.6.cloned.1.call-update) | async-done | bytes 4194320 | tf_op jit(solution)/shard_map/all_gather | solution.py:44
  74.2 3.3 %fusion = f32[8,128,128]{2,1,0:T(8,128)S(1)} fusion(bf16[16,8,128,128]{3,2,1,0:T(8,128)(2,1)} %bitcast.46, pred[16]{0:T(512)(128)(4,1)S(1)} %iota_compare_fusion.1), kind=kLoop, calls=%fused_computation.2 | loop fusion | flops 6160384 | bytes 4718608 | tf_op jit(solution)/shard_map/reduce_sum | solution.py:49
  77.6 0.1 copy-done.6
  77.7 3.3 %multiply_reduce_fusion = (f32[1024,8]{0,1:T(8,128)S(1)}, f32[1024,8,128]{2,0,1:T(8,128)S(1)}) fusion(f32[8,128,128]{2,1,0:T(8,128)S(1)} %fusion, bf16[1024,8,128]{0,2,1:T(8,128)(2,1)S(1)} %bitcast.35, f32[512,8,128]{2,0,1:T(8,128)S(1)} %copy-done.5, f32[512,8,128]{2,0,1:T(8,128)S(1)} %copy-done.6), kind=kOutput, calls=%fused_computation.21 | convolution fusion | flops 1614798848 | bytes 11042816 | tf_op jit(solution)/shard_map/thd,hde->the/dot_general | solution.py:50
  81.0 1.4 multiply_convert_fusion
  82.4 2.7 copy.63
  85.2 89.7 %all-gather.4.cloned.1.call-done = bf16[1024,6144]{1,0:T(8,128)(2,1)} async-done(((bf16[1024,384]{1,0:T(8,128)(2,1)}), bf16[1024,6144]{1,0:T(8,128)(2,1)}) %all-gather.4.cloned.1.call-update) | async-done | bytes 12582928 | tf_op jit(solution)/shard_map/all_gather | solution.py:56
  174.9 21.1 %convolution_convert_fusion = bf16[1024,6144]{1,0:T(8,128)(2,1)} fusion(bf16[1024,1024]{0,1:T(8,128)(2,1)} %bitcast.48, bf16[1024,6144]{1,0:T(8,128)(2,1)} %all-gather.4.cloned.1.call-done), kind=kOutput, calls=%fused_computation | convolution fusion | flops 12891193344 | bytes 27262976 | tf_op jit(solution)/shard_map/dot_general | solution.py:58
  195.9 0.0 reduce-scatter.2.cloned.1.call-update
  195.9 72.1 %reduce-scatter.2.cloned.1.call-done = bf16[128,6144]{1,0:T(8,128)(2,1)} async-done(((bf16[1024,6144]{1,0:T(8,128)(2,1)}), bf16[128,6144]{1,0:T(8,128)(2,1)}) %reduce-scatter.2.cloned.1.call-update) | async-done | bytes 1572880 | tf_op jit(solution)/shard_map/reduce_scatter | solution.py:57
  268.0 2.9 %add_convert_fusion = bf16[128,6144]{1,0:T(8,128)(2,1)} fusion(bf16[128,6144]{1,0:T(8,128)(2,1)S(1)} %copy-done.10, bf16[128,6144]{1,0:T(8,128)(2,1)} %reduce-scatter.2.cloned.1.call-done), kind=kLoop, calls=%fused_computation.26 | loop fusion | flops 3145728 | bytes 4718592 | tf_op jit(solution)/shard_map/convert_element_type | solution.py:63
  (10 shorter events, 0.0 us)
Async XLA Ops:
  6.5 67.7 %all-gather.6.cloned.1.call-start = ((), (), s32[]{:S(2)}) async-start(), calls=%async_computation.3 | async-start | bytes 4456448 | tf_op jit(solution)/shard_map/all_gather | solution.py:44
  9.4 2.4 copy-start.9
  11.8 3.8 %copy-start = (bf16[512,1024]{0,1:T(8,128)(2,1)}, bf16[512,1024]{0,1:T(8,128)(2,1)S(1)}, u32[]{:S(2)}) copy-start(bf16[512,1024]{0,1:T(8,128)(2,1)S(1)} %get-tuple-element.9) | copy-start | bytes 3145732
  13.6 6.3 %copy-start.2 = (bf16[512,1024]{0,1:T(8,128)(2,1)}, bf16[512,1024]{0,1:T(8,128)(2,1)S(1)}, u32[]{:S(2)}) copy-start(bf16[512,1024]{0,1:T(8,128)(2,1)S(1)} %copy.79) | copy-start | bytes 3145732
  16.0 0.8 copy-start.7
  19.2 155.7 %all-gather.4.cloned.1.call-start = ((), (), s32[]{:S(2)}) async-start(), calls=%async_computation.1 | async-start | bytes 13369344 | tf_op jit(solution)/shard_map/all_gather | solution.py:56
  19.9 248.1 %reduce-scatter.2.cloned.1.call-start = ((), (), s32[]{:S(2)}) async-start(), calls=%async_computation.2 | async-start | bytes 14155776 | tf_op jit(solution)/shard_map/reduce_scatter | solution.py:57
  24.0 3.1 %copy-start.4 = (bf16[512,1024]{0,1:T(8,128)(2,1)S(1)}, bf16[512,1024]{0,1:T(8,128)(2,1)}, u32[]{:S(2)}) copy-start(bf16[512,1024]{0,1:T(8,128)(2,1)} %get-tuple-element.10) | copy-start | bytes 3145732
  27.1 1.3 copy-start.3
  28.4 4.6 %copy-start.8 = (f32[8,128,128]{2,1,0:T(8,128)S(1)}, f32[8,128,128]{2,1,0:T(8,128)}, u32[]{:S(2)}) copy-start(f32[8,128,128]{2,1,0:T(8,128)} %copy-done.7) | copy-start | bytes 1572868
  33.0 2.5 copy-start.1
  74.2 3.4 %copy-start.5 = (f32[512,8,128]{2,0,1:T(8,128)S(1)}, f32[512,8,128]{2,0,1:T(8,128)}, u32[]{:S(2)}) copy-start(f32[512,8,128]{2,0,1:T(8,128)} %bitcast_add_fusion) | copy-start | bytes 6291460
  74.2 3.5 %copy-start.6 = (f32[512,8,128]{2,0,1:T(8,128)S(1)}, f32[512,8,128]{2,0,1:T(8,128)}, u32[]{:S(2)}) copy-start(f32[512,8,128]{2,0,1:T(8,128)} %fusion.17) | copy-start | bytes 6291460
  77.7 3.3 %copy-start.11 = (f32[1024]{0:T(1024)S(1)}, f32[1024]{0:T(1024)}, u32[]{:S(2)}) copy-start(f32[1024]{0:T(1024)} %param.9) | copy-start | bytes 12292
  195.9 72.1 %copy-start.10 = (bf16[128,6144]{1,0:T(8,128)(2,1)S(1)}, bf16[128,6144]{1,0:T(8,128)(2,1)}, u32[]{:S(2)}) copy-start(bf16[128,6144]{1,0:T(8,128)(2,1)} %param.11) | copy-start | bytes 4718596
Sparse Core Ops, SparseCore 0:
  19.3 54.8 all-gather.5
  76.3 98.4 all-gather.3
  196.1 71.9 reduce-scatter.1
where the time goes:
time: 278 us; the launch traced here: 277 us
  waiting for transfers between devices  194 us (70%)
  matrix products  42.7 us (15%)
  local copies, waits for them, and re-layouts  15.5 us (6%)
  between operations  13.3 us (5%)
  other arithmetic  11.9 us (4%)
    all_gather x1, waiting for transfers between devices, per_device(): full_weight = lax.all_gather(out_weight, 'seq', axis=1, tiled=True)  89.7 us
    reduce_scatter x1, waiting for transfers between devices, per_device(): lax.psum_scatter(jnp.dot(normed, full_weight, preferred_element_type=jnp....  72.1 us
    all_gather x1, waiting for transfers between devices, per_device(): lax.all_gather(running[None].astype(jnp.bfloat16), 'seq', axis=0, tiled=T...  31.4 us
    dot_general x1, matrix products, per_device(): jnp.dot(normed, full_weight, preferred_element_type=jnp.float32)  21.1 us
    dot_general x2, matrix products, per_device(): jnp.einsum('hts,she->the', scores, v_part.astype(jnp.float32), precision=...  10.5 us
    unnamed x28, local copies, waits for them, and re-layouts  10.2 us
  transfers between devices with their start and end apart: 3, of which 3 were waited for; matrix products, arithmetic and copies ran while one was open for 12% of the time, Pallas kernels for 0%

commit v1 on v0

v1 whole, which is shorter than its diff:
```python
import functools

import jax
import jax.numpy as jnp
from jax import lax
from jax.experimental import pallas as pl
from jax.experimental.pallas import tpu as pltpu
from jax.sharding import Mesh, PartitionSpec as P

DH = 128
F32 = jnp.float32
BF16 = jnp.bfloat16
REL = (0, 1, 3, 2)
YREL = (2, 1, 3, 0)
CHUNK = 256


def silu(block):
    wide = block.astype(F32)
    return (0.5 * wide * (1.0 + jnp.tanh(0.5 * wide))).astype(BF16)


def after(value, *others):
    return lax.optimization_barrier((value, *others))[0]


def cost(flops, moved):
    return pl.CostEstimate(flops=int(flops), transcendentals=0, bytes_accessed=int(moved))


def contract(left, right, dims):
    return lax.dot_general(left, right, (dims, ((), ())), preferred_element_type=F32)


def state_body(k_ref, v_ref, kact_ref, state_ref):
    k_act = silu(k_ref[...])
    kact_ref[...] = k_act
    both = contract(k_act, v_ref[...], ((0,), (0,))).astype(BF16)
    state_ref[:DH, :] = both[:DH, :DH]
    state_ref[DH:, :] = both[DH:, DH:]


def span_state(key_in, value):
    tokens, width = key_in.shape
    column = pl.BlockSpec((tokens, 2 * DH), lambda h: (0, h))
    return pl.pallas_call(
        state_body,
        grid=(width // (2 * DH),),
        in_specs=[column, column],
        out_specs=[column, pl.BlockSpec((2 * DH, DH), lambda h: (h, 0))],
        out_shape=[
            jax.ShapeDtypeStruct((tokens, width), BF16),
            jax.ShapeDtypeStruct((width, DH), BF16),
        ],
        cost_estimate=cost(2 * tokens * width * DH, 24e6),
        name="span_state",
    )(key_in, value)


def local_body(q_ref, kact_ref, v_ref, qact_ref, local_ref):
    q_act = silu(q_ref[...])
    qact_ref[...] = q_act
    tokens = q_act.shape[0]
    rows = lax.broadcasted_iota(jnp.int32, (CHUNK, CHUNK), 0)
    cols = lax.broadcasted_iota(jnp.int32, (CHUNK, CHUNK), 1)
    running = None
    for start in range(0, tokens, CHUNK):
        q_part = q_act[start : start + CHUNK]
        k_part = kact_ref[start : start + CHUNK, :]
        v_part = v_ref[start : start + CHUNK, :]
        scores = contract(q_part, k_part, ((1,), (1,)))
        scores = jnp.where(rows >= cols, scores, 0.0).astype(BF16)
        inner = contract(scores, v_part, ((1,), (0,)))
        if running is not None:
            inner = inner + contract(q_part, running.astype(BF16), ((1,), (0,)))
        local_ref[start : start + CHUNK, :] = inner
        if start + CHUNK < tokens:
            update = contract(k_part, v_part, ((0,), (0,)))
            running = update if running is None else running + update


def local_attention(query, k_act, value, first, heads):
    tokens, width = query.shape[0], heads * DH
    source = pl.BlockSpec((tokens, DH), lambda h: (0, h + first))
    column = pl.BlockSpec((tokens, DH), lambda h: (0, h))
    return pl.pallas_call(
        local_body,
        grid=(heads,),
        in_specs=[source, source, source],
        out_specs=[column, column],
        out_shape=[
            jax.ShapeDtypeStruct((tokens, width), BF16),
            jax.ShapeDtypeStruct((tokens, width), F32),
        ],
        cost_estimate=cost(8 * tokens * width * DH, 36e6 * width / 1024),
        name="local_attention",
    )(query, k_act, value)


def norm_body(
    tab_ref, qa_ref, la_ref, qb_ref, lb_ref, gain_ref, z1, z2, z3, x1, x2, x3, theirs_ref, mine_ref
):
    def part(q_ref, local_ref):
        prefix = x1[...].astype(F32) + x2[...].astype(F32) + x3[...].astype(F32)
        for index, piece in enumerate((z1, z2, z3)):
            prefix = prefix + jnp.where(tab_ref[8 + index] > 0, piece[...].astype(F32), 0.0)
        prefix = prefix.astype(BF16)
        zero = jnp.zeros((DH, DH), BF16)
        prefix = jnp.concatenate(
            [
                jnp.concatenate([prefix[:DH], zero], axis=1),
                jnp.concatenate([zero, prefix[DH:]], axis=1),
            ],
            axis=0,
        )
        head = lax.broadcasted_iota(jnp.int32, (2 * DH, 2 * DH), 0) // DH
        other = lax.broadcasted_iota(jnp.int32, (2 * DH, 2 * DH), 1) // DH
        average = jnp.where(head == other, 1.0 / DH, 0.0).astype(BF16)
        gain = gain_ref[...]
        for place in range(8):
            source = pl.ds(pl.multiple_of(tab_ref[place] * 128, 128), 128)
            attended = local_ref[source, :] + contract(q_ref[source, :], prefix, ((1,), (0,)))
            square = attended * attended
            high = square.astype(BF16)
            low = (square - high.astype(F32)).astype(BF16)
            meansq = contract(high, average, ((1,), (0,))) + contract(low, average, ((1,), (0,)))
            normed = (attended * lax.rsqrt(meansq + 1e-06) * gain).astype(BF16)
            out = theirs_ref if place < 4 else mine_ref
            out[(place % 4) * 128 : (place % 4 + 1) * 128, :] = normed

    early = pl.program_id(0) < pl.num_programs(0) // 2
    pl.when(early)(lambda: part(qa_ref, la_ref))
    pl.when(jnp.logical_not(early))(lambda: part(qb_ref, lb_ref))


def norm(table, halves, gain, z_pieces, x_pieces):
    (qa, la), (qb, lb) = halves
    tokens, width = qa.shape[0], qa.shape[1] * 2
    steps = width // (2 * DH)
    first = pl.BlockSpec((tokens, 2 * DH), lambda h, t: (0, jnp.minimum(h, steps // 2 - 1)))
    second = pl.BlockSpec((tokens, 2 * DH), lambda h, t: (0, jnp.maximum(h - steps // 2, 0)))
    half = pl.BlockSpec((tokens // 2, 2 * DH), lambda h, t: (0, h))
    square = pl.BlockSpec((2 * DH, DH), lambda h, t: (h, 0))
    return pl.pallas_call(
        norm_body,
        grid_spec=pltpu.PrefetchScalarGridSpec(
            num_scalar_prefetch=1,
            grid=(steps,),
            in_specs=[first, first, second, second, pl.BlockSpec((1, 2 * DH), lambda h, t: (0, h))]
            + [square] * 6,
            out_specs=[half, half],
        ),
        out_shape=[jax.ShapeDtypeStruct((tokens // 2, width), BF16)] * 2,
        cost_estimate=cost(2 * tokens * width * DH, 28e6),
        name="norm",
    )(table, qa, la, qb, lb, gain, *z_pieces, *x_pieces)


def project_body(counts, split, n_ref, *refs):
    weights = refs[: len(counts)]
    rest = refs[len(counts) :]
    step = pl.program_id(0)
    first = 0
    for w_ref, count in zip(weights, counts):

        @pl.when((step >= first) & (step < first + count))
        def _(w_ref=w_ref):
            total = contract(n_ref[...], w_ref[...], ((1,), (1,)))
            if not split:
                rest[0][...] = total.astype(BF16)
            else:
                total = total + rest[0][...].astype(F32)
                for index, out in enumerate(rest[1:]):
                    out[...] = total[index * 128 : (index + 1) * 128].astype(out.dtype)

        first += count


def project(normed, weights, tile, received=None):
    rows, depth = normed.shape
    counts = tuple(w.shape[0] // tile for w in weights)
    columns = tile * sum(counts)
    specs, first = [], 0
    for count in counts:
        specs.append(
            pl.BlockSpec(
                (tile, depth),
                lambda g, first=first, count=count: (jnp.clip(g - first, 0, count - 1), 0),
            )
        )
        first += count
    split = received is not None
    in_specs = [pl.BlockSpec((rows, depth), lambda g: (0, 0))] + specs
    args = [normed, *weights]
    if split:
        in_specs.append(pl.BlockSpec((rows, tile), lambda g: (0, g)))
        args.append(received)
        out_specs = [pl.BlockSpec((128, tile), lambda g: (0, g))] * 4
        out_shape = [jax.ShapeDtypeStruct((128, columns), BF16)] * 3 + [
            jax.ShapeDtypeStruct((128, columns), F32)
        ]
    else:
        out_specs = pl.BlockSpec((rows, tile), lambda g: (0, g))
        out_shape = jax.ShapeDtypeStruct((rows, columns), BF16)
    return pl.pallas_call(
        functools.partial(project_body, counts, split),
        grid=(sum(counts),),
        in_specs=in_specs,
        out_specs=out_specs,
        out_shape=out_shape,
        compiler_params=pltpu.CompilerParams(vmem_limit_bytes=40 * 1024 * 1024),
        cost_estimate=cost(2 * rows * depth * columns, 2 * depth * (rows + columns) + 2 * rows * columns),
        name="project",
    )(*args)


def finish_body(layout, counts, tab_ref, res_ref, *refs):
    out_ref = refs[-1]
    sums, index = [], 0
    for count in counts:
        total = refs[index][...]
        for other in refs[index + 1 : index + count]:
            total = total + other[...].astype(F32)
        sums.append(total)
        index += count
    for place, (first, second) in enumerate(layout):
        (c0, o0), (c1, o1) = first, second
        both = jnp.concatenate([sums[c0][:, o0 : o0 + 192], sums[c1][:, o1 : o1 + 192]], axis=1)
        target = pl.ds(pl.multiple_of(tab_ref[place] * 384, 128), 384)
        out_ref[:, target] = (both + res_ref[:, target].astype(F32)).astype(BF16)


def finish(layout, table, residual, parts):
    flat = [array for part in parts for array in part]
    return pl.pallas_call(
        functools.partial(finish_body, layout, tuple(len(part) for part in parts)),
        in_specs=[pl.BlockSpec(memory_space=pltpu.SMEM)]
        + [pl.BlockSpec(memory_space=pltpu.VMEM)] * (1 + len(flat)),
        out_specs=pl.BlockSpec(memory_space=pltpu.VMEM),
        out_shape=jax.ShapeDtypeStruct(residual.shape, BF16),
        compiler_params=pltpu.CompilerParams(vmem_limit_bytes=40 * 1024 * 1024),
        cost_estimate=cost(0, 12e6),
        name="finish",
    )(table, residual, *flat)


def fetch(array, axis, offset):
    return lax.ppermute(array, axis, [((i + offset) % 4, i) for i in range(4)])


def earlier(array, axis, offset):
    return lax.ppermute(array, axis, [(i, i + offset) for i in range(4 - offset)])


def swap(array):
    return lax.ppermute(array, "c", [(0, 1), (1, 0)])


def scatter_chunk(theirs, mine, a_parts, b_parts, tile, direct):
    weights = a_parts + b_parts
    a_columns = sum(w.shape[0] for w in a_parts)
    received = swap(project(theirs, weights, tile))
    far, right, left, own = project(mine, weights, tile, received)
    if direct:
        return own, fetch(right, "y", 3), fetch(left, "y", 1), fetch(far, "y", 2)
    far_right = fetch(far[:, :a_columns], "y", 3)
    far_left = fetch(far[:, a_columns:], "y", 1)
    right = jnp.concatenate(
        [(right[:, :a_columns].astype(F32) + far_right.astype(F32)).astype(BF16), right[:, a_columns:]],
        axis=1,
    )
    left = jnp.concatenate(
        [left[:, :a_columns], (left[:, a_columns:].astype(F32) + far_left.astype(F32)).astype(BF16)],
        axis=1,
    )
    return own, fetch(right, "y", 3), fetch(left, "y", 1)


def per_device(query, key_in, value, head_gain, out_weight, residual):
    x, z, y, c = (lax.axis_index(name) for name in ("x", "z", "y", "c"))
    blocks = [(y + offset) % 4 * 2 + 1 - c for offset in YREL]
    blocks += [(y + offset) % 4 * 2 + c for offset in YREL]
    flags = [((z + offset) % 4 < z).astype(jnp.int32) for offset in REL[1:]]
    table = jnp.stack([jnp.asarray(entry, jnp.int32) for entry in blocks + flags])

    turned = out_weight.T
    half = turned.shape[0] // 2
    a_own, b_own = turned[:half], turned[half:]
    a_near = [fetch(a_own, "z", offset) for offset in (1, 3)]
    b_near = [fetch(b_own, "x", offset) for offset in (1, 3)]

    k_act, state = span_state(after(key_in, turned), value)
    z_pieces = [fetch(state, "z", offset) for offset in REL[1:]]
    a_far = fetch(after(a_own, state), "z", 2)
    b_far = fetch(after(b_own, state), "x", 2)

    heads = query.shape[1] // DH // 2
    early = local_attention(query, k_act, value, 0, heads)
    z_pieces = [after(piece, early[0]) for piece in z_pieces]
    row = state.astype(F32)
    for piece in z_pieces:
        row = row + piece.astype(F32)
    row = row.astype(BF16)
    x_pieces = [earlier(row, "x", offset) for offset in (1, 2, 3)]
    late = local_attention(after(query, row), k_act, value, heads, heads)

    b0 = jnp.concatenate([b_own] + b_near + [b_far], axis=0)
    b1, b3 = fetch(b0, "z", 1), fetch(b0, "z", 3)
    a0 = jnp.concatenate([a_own] + a_near + [a_far], axis=0)
    ready = after(a0, *x_pieces)
    a1, a3 = fetch(ready, "x", 1), fetch(ready, "x", 3)
    theirs, mine = norm(table, (early, late), head_gain.reshape(1, -1), z_pieces, x_pieces)
    first = scatter_chunk(theirs, mine, [a0], [b0], 4 * half, True)
    a2 = [fetch(a1[: 2 * half], "x", 1), fetch(a3[2 * half :], "x", 3)]
    b2 = [fetch(b1[: 2 * half], "z", 1), fetch(b3[2 * half :], "z", 3)]
    second = scatter_chunk(after(theirs, first[0]), mine, [a1, a3], [b1, b3], 4 * half, False)
    third = scatter_chunk(after(theirs, second[0]), mine, a2, b2, 2 * half, True)
    parts = [first, second, third]
    a_group = ((0, 0), (1, 0), (1, 4 * half), (2, 0))
    b_group = ((0, 4 * half), (1, 8 * half), (1, 12 * half), (2, 4 * half))
    layout, shards = [], []
    for i, x_off in enumerate(REL):
        for j, z_off in enumerate(REL):
            layout.append(
                (
                    (a_group[i][0], a_group[i][1] + j * half),
                    (b_group[j][0], b_group[j][1] + i * half),
                )
            )
            shards.append((x + x_off) % 4 * 4 + (z + z_off) % 4)
    shard_table = jnp.stack([jnp.asarray(entry, jnp.int32) for entry in shards])
    return finish(tuple(layout), shard_table, residual, parts)


def solution(mesh):
    torus = Mesh(mesh.devices.reshape(4, 4, 4, 2), ("x", "z", "y", "c"))
    seq, hx = ("x", "z"), ("y", "c")
    return jax.shard_map(
        per_device,
        mesh=torus,
        in_specs=(P(seq, hx), P(seq, hx), P(seq, hx), P(hx), P(hx, seq), P(seq + hx, None)),
        out_specs=P(seq + hx, None),
        check_vma=False,
    )
```

time: 278 us -> 224 us (0.81)
  the two profiles are of different devices: /device:TPU:1 before, /device:TPU:24 now
where the time goes in v1:
time: 224 us; the launch traced here: 223 us
  waiting for transfers between devices  104 us (46%)
  Pallas kernels  50.2 us (22%)
  starting transfers between devices  47 us (21%)
  local copies, waits for them, and re-layouts  15.6 us (7%)
  other arithmetic  5.56 us (2%)
    ppermute x27, waiting for transfers between devices, fetch(): return lax.ppermute(array, axis, [((i + offset) % 4, i) for i in range(4)])  102 us
    ppermute x27, starting transfers between devices, fetch(): return lax.ppermute(array, axis, [((i + offset) % 4, i) for i in range(4)])  38.8 us
    pallas_call x6, Pallas kernels, project(): pl.pallas_call(functools.partial(project_body, counts, split), grid=(sum(...  21.6 us
    unnamed x53, local copies, waits for them, and re-layouts  11.8 us
    pallas_call x2, Pallas kernels, local_attention(): pl.pallas_call(local_body, grid=(heads,), in_specs=[source, source, sourc...  11.5 us
    pallas_call x1, Pallas kernels, norm(): pl.pallas_call(norm_body, grid_spec=pltpu.PrefetchScalarGridSpec(num_scal...  8.47 us
    ppermute x3, starting transfers between devices, earlier(): lax.ppermute(array, axis, [(i, i + offset) for i in range(4 - offset)])  8.03 us
    pallas_call x1, Pallas kernels, span_state(): pl.pallas_call(state_body, grid=(width // (2 * DH),), in_specs=[column, c...  4.71 us
  transfers between devices with their start and end apart: 33, of which 13 were waited for; matrix products, arithmetic and copies ran while one was open for 4% of the time, Pallas kernels for 12%

profile of v1, /device:TPU:24, one launch (start us, length us, event | category | flops | bytes accessed | tf_op | source)
XLA Modules:
  0.0 223.2 jit_solution(7168440953072262896)
XLA Ops:
  0.0 1.4 copy.7
  1.5 4.7 %span_state.1 = (bf16[1024,1024]{1,0:T(8,128)(2,1)}, bf16[1024,128]{1,0:T(8,128)(2,1)}) custom-call(bf16[1024,1024]{1,0:T(8,128)(2,1)} %k_ref, bf16[1024,1024]{1,0:T(8,128)(2,1)} %v_ref.5), custom_call_target="tpu_custom_call" | custom-call | flops 268435456 | bytes 24000000 | tf_op jit(solution)/shard_map/span_state/pallas_call | solution.py:46
  6.2 3.9 %collective-permute-start.8 = (bf16[192,1024]{1,0:T(8,128)(2,1)S(1)}, bf16[192,1024]{1,0:T(8,128)(2,1)S(1)}, u32[]{:S(2)}, u32[]{:S(2)}) collective-permute-start(bf16[192,1024]{1,0:T(8,128)(2,1)S(1)} %get-tuple-element.47), channel_id=1, source_target_pairs={{16,0},{24,8},{0,16},{8,24},{17,1},{25,9},{1,17},{9,25},{18,2},{26... | collective-permute-start | bytes 1179656 | tf_op jit(solution)/shard_map/ppermute | solution.py:248
  10.1 1.5 collective-permute-start.1
  11.6 2.1 collective-permute-start
  13.8 11.9 %collective-permute-done.2.z3 = bf16[1024,128]{1,0:T(8,128)(2,1)S(1)} collective-permute-done((bf16[1024,128]{1,0:T(8,128)(2,1)}, bf16[1024,128]{1,0:T(8,128)(2,1)S(1)}, u32[]{:S(2)}, u32[]{:S(2)}) %collective-permute-start.2) | collective-permute-done | bytes 262176 | tf_op jit(solution)/shard_map/ppermute | solution.py:248
  25.7 3.7 %collective-permute-start.6 = (bf16[192,1024]{1,0:T(8,128)(2,1)S(1)}, bf16[192,1024]{1,0:T(8,128)(2,1)}, u32[]{:S(2)}, u32[]{:S(2)}) collective-permute-start(bf16[192,1024]{1,0:T(8,128)(2,1)S(1)} %get-tuple-element.47), channel_id=1, source_target_pairs={{8,0},{16,8},{24,16},{0,24},{9,1},{17,9},{25,17},{1,25},{10,2},{18... | collective-permute-start | bytes 1179656 | tf_op jit(solution)/shard_map/ppermute | solution.py:248
  29.4 1.6 collective-permute-done.1.z2
  31.0 3.0 %collective-permute-start.11 = (bf16[192,1024]{1,0:T(8,128)(2,1)S(1)}, bf16[192,1024]{1,0:T(8,128)(2,1)S(1)}, u32[]{:S(2)}, u32[]{:S(2)}) collective-permute-start(bf16[192,1024]{1,0:T(8,128)(2,1)S(1)} %get-tuple-element.48), channel_id=1, source_target_pairs={{64,0},{96,32},{0,64},{32,96},{65,1},{97,33},{1,65},{33,97},{66,2}... | collective-permute-start | bytes 1179656 | tf_op jit(solution)/shard_map/ppermute | solution.py:248
  34.6 5.8 %local_attention.2 = (bf16[1024,512]{1,0:T(8,128)(2,1)}, f32[1024,512]{1,0:T(8,128)}) custom-call(bf16[1024,1024]{1,0:T(8,128)(2,1)} %q_ref.2, bf16[1024,1024]{1,0:T(8,128)(2,1)} %get-tuple-element.36.kact_ref, bf16[1024,1024]{1,0:T(8,128)(2,1)} %v_ref.5), custom_call_target="tpu_custom_call" | custom-call | flops 536870912 | bytes 18000000 | tf_op jit(solution)/shard_map/local_attention/pallas_call | solution.py:86
  41.1 2.6 %collective-permute-start.9 = (bf16[192,1024]{1,0:T(8,128)(2,1)S(1)}, bf16[192,1024]{1,0:T(8,128)(2,1)}, u32[]{:S(2)}, u32[]{:S(2)}) collective-permute-start(bf16[192,1024]{1,0:T(8,128)(2,1)S(1)} %get-tuple-element.48), channel_id=1, source_target_pairs={{32,0},{64,32},{96,64},{0,96},{33,1},{65,33},{97,65},{1,97},{34,2}... | collective-permute-start | bytes 1179656 | tf_op jit(solution)/shard_map/ppermute | solution.py:248
  44.6 5.7 %local_attention.3 = (bf16[1024,512]{1,0:T(8,128)(2,1)}, f32[1024,512]{1,0:T(8,128)}) custom-call(bf16[1024,1024]{1,0:T(8,128)(2,1)} %q_ref.2, bf16[1024,1024]{1,0:T(8,128)(2,1)} %get-tuple-element.36.kact_ref, bf16[1024,1024]{1,0:T(8,128)(2,1)} %v_ref.5), custom_call_target="tpu_custom_call" | custom-call | flops 536870912 | bytes 18000000 | tf_op jit(solution)/shard_map/local_attention/pallas_call | solution.py:86
  50.3 2.0 collective-permute-start.3
  52.3 4.0 %collective-permute-start.4 = (bf16[1024,128]{1,0:T(8,128)(2,1)}, bf16[1024,128]{1,0:T(8,128)(2,1)}, u32[]{:S(2)}, u32[]{:S(2)}) collective-permute-start(bf16[1024,128]{1,0:T(8,128)(2,1)} %add_convert_fusion.2), channel_id=1, source_target_pairs={{0,64},{32,96},{1,65},{33,97},{2,66},{34,98},{3,67},{35,99},{4,68}... | collective-permute-start | bytes 786440 | tf_op jit(solution)/shard_map/ppermute | solution.py:252
  57.1 2.0 collective-permute-start.5
  59.1 1.3 pad_maximum_fusion.refs_0_
  60.4 1.3 pad_maximum_fusion.1.refs_1_
  62.2 2.2 %collective-permute-done.5.x3 = bf16[1024,128]{1,0:T(8,128)(2,1)} collective-permute-done((bf16[1024,128]{1,0:T(8,128)(2,1)}, bf16[1024,128]{1,0:T(8,128)(2,1)}, u32[]{:S(2)}, u32[]{:S(2)}) %collective-permute-start.5) | collective-permute-done | bytes 262176 | tf_op jit(solution)/shard_map/ppermute | solution.py:252
  64.4 8.5 %norm.1 = (bf16[512,1024]{1,0:T(8,128)(2,1)}, bf16[512,1024]{1,0:T(8,128)(2,1)}) custom-call(s32[11]{0:T(128)} %stack.127.tab_ref, bf16[1024,512]{1,0:T(8,128)(2,1)} %get-tuple-element.37.qa_ref, f32[1024,512]{1,0:T(8,128)} %get-tuple-element.38.la_ref, bf16[1024,512]{1,0:T(8,128)(2,1)} %get-tuple-element.44.qb_ref, f32[1024,512]{1,0:T(8,128)} %get-tuple-element.45.lb_ref, ...), custom_call_target="tpu_custom_call" | custom-call | flops 268435456 | bytes 28000000 | tf_op jit(solution)/shard_map/norm/pallas_call | solution.py:144
  72.9 1.2 copy-done.11
  74.1 2.2 project.6
  76.6 1.9 collective-permute-start.19
  78.5 3.7 %collective-permute-start.16 = (bf16[768,1024]{1,0:T(8,128)(2,1)S(1)}, bf16[768,1024]{1,0:T(8,128)(2,1)S(1)}, u32[]{:S(2)}, u32[]{:S(2)}) collective-permute-start(bf16[768,1024]{1,0:T(8,128)(2,1)S(1)} %pad_maximum_fusion.refs_0_), channel_id=1, source_target_pairs={{32,0},{64,32},{96,64},{0,96},{33,1},{65,33},{97,65},{1,97},{34,2}... | collective-permute-start | bytes 4718600 | tf_op jit(solution)/shard_map/ppermute | solution.py:248
  82.2 3.1 %project.7 = (bf16[128,1536]{1,0:T(8,128)(2,1)S(1)}, bf16[128,1536]{1,0:T(8,128)(2,1)}, bf16[128,1536]{1,0:T(8,128)(2,1)}, f32[128,1536]{1,0:T(8,128)S(1)}) custom-call(bf16[512,1024]{1,0:T(8,128)(2,1)S(1)} %copy-done.9, bf16[768,1024]{1,0:T(8,128)(2,1)S(1)} %pad_maximum_fusion.refs_0_, bf16[768,1024]{1,0:T(8,128)(2,1)S(1)} %pad_maximum_fusion.1.refs_1_, ...), custom_call_target="tpu_custom_call" | custom-call | flops 1610612736 | bytes 5767168 | tf_op jit(solution)/shard_map/project/pallas_call | solution.py:205
  86.1 27.1 %collective-permute-done.18.refs_2_ = bf16[768,1024]{1,0:T(8,128)(2,1)S(1)} collective-permute-done((bf16[768,1024]{1,0:T(8,128)(2,1)S(1)}, bf16[768,1024]{1,0:T(8,128)(2,1)S(1)}, u32[]{:S(2)}, u32[]{:S(2)}) %collective-permute-start.18) | collective-permute-done | bytes 1572896 | tf_op jit(solution)/shard_map/ppermute | solution.py:248
  113.2 1.9 collective-permute-done.19.refs_3_
  115.9 3.4 %collective-permute-done.17.refs_1_ = bf16[768,1024]{1,0:T(8,128)(2,1)S(1)} collective-permute-done((bf16[768,1024]{1,0:T(8,128)(2,1)S(1)}, bf16[768,1024]{1,0:T(8,128)(2,1)S(1)}, u32[]{:S(2)}, u32[]{:S(2)}) %collective-permute-start.17) | collective-permute-done | bytes 1572896 | tf_op jit(solution)/shard_map/ppermute | solution.py:248
  119.3 4.4 %project.8 = bf16[512,3072]{1,0:T(8,128)(2,1)S(1)} custom-call(bf16[512,1024]{1,0:T(8,128)(2,1)S(1)} %copy-done.11, bf16[768,1024]{1,0:T(8,128)(2,1)S(1)} %collective-permute-done.16.refs_0_, bf16[768,1024]{1,0:T(8,128)(2,1)S(1)} %collective-permute-done.17.refs_1_, bf16[768,1024]{1,0:T(8,128)(2,1)S(1)} %collective-permute-done.18.refs_2_, ...), custom_call_target="tpu_custom_call" | custom-call | flops 3221225472 | bytes 10485760 | tf_op jit(solution)/shard_map/project/pallas_call | solution.py:205
  124.7 2.2 collective-permute-start.27
  129.1 1.8 collective-permute-start.26
  130.9 4.7 %project.9 = (bf16[128,3072]{1,0:T(8,128)(2,1)S(1)}, bf16[128,3072]{1,0:T(8,128)(2,1)S(1)}, bf16[128,3072]{1,0:T(8,128)(2,1)S(1)}, f32[128,3072]{1,0:T(8,128)S(1)}) custom-call(bf16[512,1024]{1,0:T(8,128)(2,1)S(1)} %copy-done.9, bf16[768,1024]{1,0:T(8,128)(2,1)S(1)} %collective-permute-done.16.refs_0_, ...), custom_call_target="tpu_custom_call" | custom-call | flops 3221225472 | bytes 10485760 | tf_op jit(solution)/shard_map/project/pallas_call | solution.py:205
  136.1 8.8 %collective-permute-done.27.refs_2_ = bf16[384,1024]{1,0:T(8,128)(2,1)S(1)} collective-permute-done((bf16[384,1024]{1,0:T(8,128)(2,1)}, bf16[384,1024]{1,0:T(8,128)(2,1)S(1)}, u32[]{:S(2)}, u32[]{:S(2)}) %collective-permute-start.27) | collective-permute-done | bytes 786464 | tf_op jit(solution)/shard_map/ppermute | solution.py:248
  145.1 3.8 %collective-permute-done.28.refs_3_ = bf16[384,1024]{1,0:T(8,128)(2,1)S(1)} collective-permute-done((bf16[384,1024]{1,0:T(8,128)(2,1)}, bf16[384,1024]{1,0:T(8,128)(2,1)S(1)}, u32[]{:S(2)}, u32[]{:S(2)}) %collective-permute-start.28) | collective-permute-done | bytes 786464 | tf_op jit(solution)/shard_map/ppermute | solution.py:248
  150.2 3.2 %project.10 = bf16[512,1536]{1,0:T(8,128)(2,1)S(1)} custom-call(bf16[512,1024]{1,0:T(8,128)(2,1)S(1)} %copy-done.11, bf16[384,1024]{1,0:T(8,128)(2,1)S(1)} %collective-permute-done.25.refs_0_, bf16[384,1024]{1,0:T(8,128)(2,1)S(1)} %collective-permute-done.26.refs_1_, bf16[384,1024]{1,0:T(8,128)(2,1)S(1)} %collective-permute-done.27.refs_2_, ...), custom_call_target="tpu_custom_call" | custom-call | flops 1610612736 | bytes 5767168 | tf_op jit(solution)/shard_map/project/pallas_call | solution.py:205
  155.3 2.7 %collective-permute-start.22 = (bf16[128,3072]{1,0:T(8,128)(2,1)}, bf16[128,3072]{1,0:T(8,128)(2,1)}, u32[]{:S(2)}, u32[]{:S(2)}) collective-permute-start(bf16[128,3072]{1,0:T(8,128)(2,1)} %pad_maximum_fusion.2), channel_id=1, source_target_pairs={{6,0},{0,2},{2,4},{4,6},{7,1},{1,3},{3,5},{5,7},{14,8},{8,10},{10,... | collective-permute-start | bytes 2359304 | tf_op jit(solution)/shard_map/ppermute | solution.py:248
  158.1 11.1 %collective-permute-done.23 = bf16[128,1536]{1,0:T(8,128)(2,1)S(1)} collective-permute-done((bf16[128,1536]{1,0:T(8,128)(2,1)S(1)}, bf16[128,1536]{1,0:T(8,128)(2,1)S(1)}, u32[]{:S(2)}, u32[]{:S(2)}) %collective-permute-start.23) | collective-permute-done | bytes 393248 | tf_op jit(solution)/shard_map/ppermute | solution.py:248
  169.3 1.0 pad_maximum_fusion.3
  170.3 1.0 collective-permute-start.15
  171.3 4.1 %project.11 = (bf16[128,1536]{1,0:T(8,128)(2,1)}, bf16[128,1536]{1,0:T(8,128)(2,1)}, bf16[128,1536]{1,0:T(8,128)(2,1)}, f32[128,1536]{1,0:T(8,128)S(1)}) custom-call(bf16[512,1024]{1,0:T(8,128)(2,1)S(1)} %copy-done.10, bf16[384,1024]{1,0:T(8,128)(2,1)S(1)} %copy-done.17, bf16[384,1024]{1,0:T(8,128)(2,1)S(1)} %copy-done.19, bf16[384,1024]{1,0:T(8,128)(2,1)S(1)} %copy-done.13, ...), custom_call_target="tpu_custom_call" | custom-call | flops 1610612736 | bytes 5767168 | tf_op jit(solution)/shard_map/project/pallas_call | solution.py:205
  176.3 2.3 %collective-permute-start.30 = (bf16[128,1536]{1,0:T(8,128)(2,1)}, bf16[128,1536]{1,0:T(8,128)(2,1)}, u32[]{:S(2)}, u32[]{:S(2)}) collective-permute-start(bf16[128,1536]{1,0:T(8,128)(2,1)} %get-tuple-element.62), channel_id=1, source_target_pairs={{6,0},{0,2},{2,4},{4,6},{7,1},{1,3},{3,5},{5,7},{14,8},{8,10},{10,... | collective-permute-start | bytes 1179656 | tf_op jit(solution)/shard_map/ppermute | solution.py:248
  180.1 18.3 %collective-permute-done.15.refs_3_ = bf16[128,1536]{1,0:T(8,128)(2,1)S(1)} collective-permute-done((bf16[128,1536]{1,0:T(8,128)(2,1)S(1)}, bf16[128,1536]{1,0:T(8,128)(2,1)S(1)}, u32[]{:S(2)}, u32[]{:S(2)}) %collective-permute-start.15) | collective-permute-done | bytes 393248 | tf_op jit(solution)/shard_map/ppermute | solution.py:248
  199.2 2.5 %collective-permute-start.32 = (bf16[128,1536]{1,0:T(8,128)(2,1)}, bf16[128,1536]{1,0:T(8,128)(2,1)}, u32[]{:S(2)}, u32[]{:S(2)}) collective-permute-start(bf16[128,1536]{1,0:T(8,128)(2,1)} %get-tuple-element.64), channel_id=1, source_target_pairs={{4,0},{6,2},{0,4},{2,6},{5,1},{7,3},{1,5},{3,7},{12,8},{14,10},{8,... | collective-permute-start | bytes 1179656 | tf_op jit(solution)/shard_map/ppermute | solution.py:248
  201.8 13.2 %collective-permute-done.31.refs_9_ = bf16[128,1536]{1,0:T(8,128)(2,1)} collective-permute-done((bf16[128,1536]{1,0:T(8,128)(2,1)}, bf16[128,1536]{1,0:T(8,128)(2,1)}, u32[]{:S(2)}, u32[]{:S(2)}) %collective-permute-start.31) | collective-permute-done | bytes 393248 | tf_op jit(solution)/shard_map/ppermute | solution.py:248
  215.0 1.1 copy-done.2
  216.1 1.1 copy-done.4
  217.3 1.0 copy-done.6
  218.3 1.0 copy-done.8
  219.3 3.9 %finish.1 = bf16[128,6144]{1,0:T(8,128)(2,1)} custom-call(s32[16]{0:T(128)S(1)} %stack.112.tab_ref, bf16[128,6144]{1,0:T(8,128)(2,1)S(1)} %copy-done, f32[128,1536]{1,0:T(8,128)S(1)} %copy-done.2, bf16[128,1536]{1,0:T(8,128)(2,1)S(1)} %collective-permute-done.13.refs_1_, bf16[128,1536]{1,0:T(8,128)(2,1)S(1)} %copy-done.6, bf16[128,1536]{1,0:T(8,128)(2,1)S(1)} %copy-done.8, ...), custom_call_target="tpu_custom_call" | custom-call | bytes 12000000 | tf_op jit(solution)/shard_map/finish/pallas_call | solution.py:235
  (99 shorter events, 16.0 us)
Async XLA Ops:
  6.2 34.9 %collective-permute-start.8 = (bf16[192,1024]{1,0:T(8,128)(2,1)S(1)}, bf16[192,1024]{1,0:T(8,128)(2,1)S(1)}, u32[]{:S(2)}, u32[]{:S(2)}) collective-permute-start(bf16[192,1024]{1,0:T(8,128)(2,1)S(1)} %get-tuple-element.47), channel_id=1, source_target_pairs={{16,0},{24,8},{0,16},{8,24},{17,1},{25,9},{1,17},{9,25},{18,2},{26... | collective-permute-start | bytes 1179656 | tf_op jit(solution)/shard_map/ppermute | solution.py:248
  10.1 15.6 %collective-permute-start.2 = (bf16[1024,128]{1,0:T(8,128)(2,1)}, bf16[1024,128]{1,0:T(8,128)(2,1)S(1)}, u32[]{:S(2)}, u32[]{:S(2)}) collective-permute-start(bf16[1024,128]{1,0:T(8,128)(2,1)} %get-tuple-element.39), channel_id=1, source_target_pairs={{16,0},{24,8},{0,16},{8,24},{17,1},{25,9},{1,17},{9,25},{18,2},{26... | collective-permute-start | bytes 786440 | tf_op jit(solution)/shard_map/ppermute | solution.py:248
  10.1 20.8 %collective-permute-start.1 = (bf16[1024,128]{1,0:T(8,128)(2,1)}, bf16[1024,128]{1,0:T(8,128)(2,1)S(1)}, u32[]{:S(2)}, u32[]{:S(2)}) collective-permute-start(bf16[1024,128]{1,0:T(8,128)(2,1)} %get-tuple-element.39), channel_id=1, source_target_pairs={{24,0},{0,8},{8,16},{16,24},{25,1},{1,9},{9,17},{17,25},{26,2},{2,... | collective-permute-start | bytes 786440 | tf_op jit(solution)/shard_map/ppermute | solution.py:248
  11.6 28.8 %collective-permute-start = (bf16[1024,128]{1,0:T(8,128)(2,1)}, bf16[1024,128]{1,0:T(8,128)(2,1)S(1)}, u32[]{:S(2)}, u32[]{:S(2)}) collective-permute-start(bf16[1024,128]{1,0:T(8,128)(2,1)} %get-tuple-element.39), channel_id=1, source_target_pairs={{8,0},{16,8},{24,16},{0,24},{9,1},{17,9},{25,17},{1,25},{10,2},{18... | collective-permute-start | bytes 786440 | tf_op jit(solution)/shard_map/ppermute | solution.py:248
  13.8 36.6 %collective-permute-start.7 = (bf16[192,1024]{1,0:T(8,128)(2,1)S(1)}, bf16[192,1024]{1,0:T(8,128)(2,1)}, u32[]{:S(2)}, u32[]{:S(2)}) collective-permute-start(bf16[192,1024]{1,0:T(8,128)(2,1)S(1)} %get-tuple-element.47), channel_id=1, source_target_pairs={{24,0},{0,8},{8,16},{16,24},{25,1},{1,9},{9,17},{17,25},{26,2},{2,... | collective-permute-start | bytes 1179656 | tf_op jit(solution)/shard_map/ppermute | solution.py:248
  25.7 18.1 %copy-start.20 = (bf16[1024,128]{1,0:T(8,128)(2,1)}, bf16[1024,128]{1,0:T(8,128)(2,1)S(1)}, u32[]{:S(2)}) copy-start(bf16[1024,128]{1,0:T(8,128)(2,1)S(1)} %collective-permute-done.2.z3) | copy-start | bytes 786436
  25.7 26.7 %collective-permute-start.6 = (bf16[192,1024]{1,0:T(8,128)(2,1)S(1)}, bf16[192,1024]{1,0:T(8,128)(2,1)}, u32[]{:S(2)}, u32[]{:S(2)}) collective-permute-start(bf16[192,1024]{1,0:T(8,128)(2,1)S(1)} %get-tuple-element.47), channel_id=1, source_target_pairs={{8,0},{16,8},{24,16},{0,24},{9,1},{17,9},{25,17},{1,25},{10,2},{18... | collective-permute-start | bytes 1179656 | tf_op jit(solution)/shard_map/ppermute | solution.py:248
  31.0 12.8 %copy-start.21 = (bf16[1024,128]{1,0:T(8,128)(2,1)}, bf16[1024,128]{1,0:T(8,128)(2,1)S(1)}, u32[]{:S(2)}) copy-start(bf16[1024,128]{1,0:T(8,128)(2,1)S(1)} %collective-permute-done.1.z2) | copy-start | bytes 786436
  31.0 25.4 %collective-permute-start.11 = (bf16[192,1024]{1,0:T(8,128)(2,1)S(1)}, bf16[192,1024]{1,0:T(8,128)(2,1)S(1)}, u32[]{:S(2)}, u32[]{:S(2)}) collective-permute-start(bf16[192,1024]{1,0:T(8,128)(2,1)S(1)} %get-tuple-element.48), channel_id=1, source_target_pairs={{64,0},{96,32},{0,64},{32,96},{65,1},{97,33},{1,65},{33,97},{66,2}... | collective-permute-start | bytes 1179656 | tf_op jit(solution)/shard_map/ppermute | solution.py:248
  34.6 9.1 %copy-start.25 = (bf16[1024,128]{1,0:T(8,128)(2,1)S(1)}, bf16[1024,128]{1,0:T(8,128)(2,1)}, u32[]{:S(2)}) copy-start(bf16[1024,128]{1,0:T(8,128)(2,1)} %get-tuple-element.39) | copy-start | bytes 786436
  40.4 9.9 %copy-start.22 = (bf16[1024,128]{1,0:T(8,128)(2,1)}, bf16[1024,128]{1,0:T(8,128)(2,1)S(1)}, u32[]{:S(2)}) copy-start(bf16[1024,128]{1,0:T(8,128)(2,1)S(1)} %collective-permute-done.z1) | copy-start | bytes 786436
  40.4 20.0 %collective-permute-start.10 = (bf16[192,1024]{1,0:T(8,128)(2,1)S(1)}, bf16[192,1024]{1,0:T(8,128)(2,1)}, u32[]{:S(2)}, u32[]{:S(2)}) collective-permute-start(bf16[192,1024]{1,0:T(8,128)(2,1)S(1)} %get-tuple-element.48), channel_id=1, source_target_pairs={{96,0},{0,32},{32,64},{64,96},{97,1},{1,33},{33,65},{65,97},{98,2}... | collective-permute-start | bytes 1179656 | tf_op jit(solution)/shard_map/ppermute | solution.py:248
  41.1 19.3 %collective-permute-start.9 = (bf16[192,1024]{1,0:T(8,128)(2,1)S(1)}, bf16[192,1024]{1,0:T(8,128)(2,1)}, u32[]{:S(2)}, u32[]{:S(2)}) collective-permute-start(bf16[192,1024]{1,0:T(8,128)(2,1)S(1)} %get-tuple-element.48), channel_id=1, source_target_pairs={{32,0},{64,32},{96,64},{0,96},{33,1},{65,33},{97,65},{1,97},{34,2}... | collective-permute-start | bytes 1179656 | tf_op jit(solution)/shard_map/ppermute | solution.py:248
  50.3 11.4 %collective-permute-start.3 = (bf16[1024,128]{1,0:T(8,128)(2,1)}, bf16[1024,128]{1,0:T(8,128)(2,1)}, u32[]{:S(2)}, u32[]{:S(2)}) collective-permute-start(bf16[1024,128]{1,0:T(8,128)(2,1)} %add_convert_fusion.2), channel_id=1, source_target_pairs={{0,32},{32,64},{64,96},{1,33},{33,65},{65,97},{2,34},{34,66},{66,9... | collective-permute-start | bytes 786440 | tf_op jit(solution)/shard_map/ppermute | solution.py:252
  52.3 9.8 %collective-permute-start.4 = (bf16[1024,128]{1,0:T(8,128)(2,1)}, bf16[1024,128]{1,0:T(8,128)(2,1)}, u32[]{:S(2)}, u32[]{:S(2)}) collective-permute-start(bf16[1024,128]{1,0:T(8,128)(2,1)} %add_convert_fusion.2), channel_id=1, source_target_pairs={{0,64},{32,96},{1,65},{33,97},{2,66},{34,98},{3,67},{35,99},{4,68}... | collective-permute-start | bytes 786440 | tf_op jit(solution)/shard_map/ppermute | solution.py:252
  57.1 7.3 %collective-permute-start.5 = (bf16[1024,128]{1,0:T(8,128)(2,1)}, bf16[1024,128]{1,0:T(8,128)(2,1)}, u32[]{:S(2)}, u32[]{:S(2)}) collective-permute-start(bf16[1024,128]{1,0:T(8,128)(2,1)} %add_convert_fusion.2), channel_id=1, source_target_pairs={{0,96},{1,97},{2,98},{3,99},{4,100},{5,101},{6,102},{7,103},{8,104... | collective-permute-start | bytes 786440 | tf_op jit(solution)/shard_map/ppermute | solution.py:252
  59.1 1.3 copy-start.24
  74.1 8.1 %copy-start.9 = (bf16[512,1024]{1,0:T(8,128)(2,1)S(1)}, bf16[512,1024]{1,0:T(8,128)(2,1)}, u32[]{:S(2)}) copy-start(bf16[512,1024]{1,0:T(8,128)(2,1)} %get-tuple-element.46.n_ref) | copy-start | bytes 3145732
  76.3 5.9 %collective-permute-start.12 = (bf16[512,1536]{1,0:T(8,128)(2,1)S(1)}, bf16[512,1536]{1,0:T(8,128)(2,1)S(1)}, u32[]{:S(2)}, u32[]{:S(2)}) collective-permute-start(bf16[512,1536]{1,0:T(8,128)(2,1)S(1)} %project.6), channel_id=1, source_target_pairs={{0,1},{1,0},{2,3},{3,2},{4,5},{5,4},{6,7},{7,6},{8,9},{9,8},{10,11... | collective-permute-start | bytes 4718600 | tf_op jit(solution)/shard_map/ppermute | solution.py:256
  76.4 36.8 %collective-permute-start.18 = (bf16[768,1024]{1,0:T(8,128)(2,1)S(1)}, bf16[768,1024]{1,0:T(8,128)(2,1)S(1)}, u32[]{:S(2)}, u32[]{:S(2)}) collective-permute-start(bf16[768,1024]{1,0:T(8,128)(2,1)S(1)} %pad_maximum_fusion.1.refs_1_), channel_id=1, source_target_pairs={{8,0},{16,8},{24,16},{0,24},{9,1},{17,9},{25,17},{1,25},{10,2},{18... | collective-permute-start | bytes 4718600 | tf_op jit(solution)/shard_map/ppermute | solution.py:248
  76.6 38.5 %collective-permute-start.19 = (bf16[768,1024]{1,0:T(8,128)(2,1)S(1)}, bf16[768,1024]{1,0:T(8,128)(2,1)S(1)}, u32[]{:S(2)}, u32[]{:S(2)}) collective-permute-start(bf16[768,1024]{1,0:T(8,128)(2,1)S(1)} %pad_maximum_fusion.1.refs_1_), channel_id=1, source_target_pairs={{24,0},{0,8},{8,16},{16,24},{25,1},{1,9},{9,17},{17,25},{26,2},{2,... | collective-permute-start | bytes 4718600 | tf_op jit(solution)/shard_map/ppermute | solution.py:248
  78.5 37.4 %collective-permute-start.16 = (bf16[768,1024]{1,0:T(8,128)(2,1)S(1)}, bf16[768,1024]{1,0:T(8,128)(2,1)S(1)}, u32[]{:S(2)}, u32[]{:S(2)}) collective-permute-start(bf16[768,1024]{1,0:T(8,128)(2,1)S(1)} %pad_maximum_fusion.refs_0_), channel_id=1, source_target_pairs={{32,0},{64,32},{96,64},{0,96},{33,1},{65,33},{97,65},{1,97},{34,2}... | collective-permute-start | bytes 4718600 | tf_op jit(solution)/shard_map/ppermute | solution.py:248
  82.2 37.1 %collective-permute-start.17 = (bf16[768,1024]{1,0:T(8,128)(2,1)S(1)}, bf16[768,1024]{1,0:T(8,128)(2,1)S(1)}, u32[]{:S(2)}, u32[]{:S(2)}) collective-permute-start(bf16[768,1024]{1,0:T(8,128)(2,1)S(1)} %pad_maximum_fusion.refs_0_), channel_id=1, source_target_pairs={{96,0},{0,32},{32,64},{64,96},{97,1},{1,33},{33,65},{65,97},{98,2}... | collective-permute-start | bytes 4718600 | tf_op jit(solution)/shard_map/ppermute | solution.py:248
  123.7 7.3 %collective-permute-start.20 = (bf16[512,3072]{1,0:T(8,128)(2,1)S(1)}, bf16[512,3072]{1,0:T(8,128)(2,1)S(1)}, u32[]{:S(2)}, u32[]{:S(2)}) collective-permute-start(bf16[512,3072]{1,0:T(8,128)(2,1)S(1)} %project.8), channel_id=1, source_target_pairs={{0,1},{1,0},{2,3},{3,2},{4,5},{5,4},{6,7},{7,6},{8,9},{9,8},{10,11... | collective-permute-start | bytes 9437192 | tf_op jit(solution)/shard_map/ppermute | solution.py:256
  124.7 20.2 %collective-permute-start.27 = (bf16[384,1024]{1,0:T(8,128)(2,1)}, bf16[384,1024]{1,0:T(8,128)(2,1)S(1)}, u32[]{:S(2)}, u32[]{:S(2)}) collective-permute-start(bf16[384,1024]{1,0:T(8,128)(2,1)} %slice.52), channel_id=1, source_target_pairs={{8,0},{16,8},{24,16},{0,24},{9,1},{17,9},{25,17},{1,25},{10,2},{18... | collective-permute-start | bytes 2359304 | tf_op jit(solution)/shard_map/ppermute | solution.py:248
  127.8 21.1 %collective-permute-start.28 = (bf16[384,1024]{1,0:T(8,128)(2,1)}, bf16[384,1024]{1,0:T(8,128)(2,1)S(1)}, u32[]{:S(2)}, u32[]{:S(2)}) collective-permute-start(bf16[384,1024]{1,0:T(8,128)(2,1)} %slice.53), channel_id=1, source_target_pairs={{24,0},{0,8},{8,16},{16,24},{25,1},{1,9},{9,17},{17,25},{26,2},{2,... | collective-permute-start | bytes 2359304 | tf_op jit(solution)/shard_map/ppermute | solution.py:248
  128.8 20.9 %collective-permute-start.25 = (bf16[384,1024]{1,0:T(8,128)(2,1)}, bf16[384,1024]{1,0:T(8,128)(2,1)S(1)}, u32[]{:S(2)}, u32[]{:S(2)}) collective-permute-start(bf16[384,1024]{1,0:T(8,128)(2,1)} %slice.50), channel_id=1, source_target_pairs={{32,0},{64,32},{96,64},{0,96},{33,1},{65,33},{97,65},{1,97},{34,2}... | collective-permute-start | bytes 2359304 | tf_op jit(solution)/shard_map/ppermute | solution.py:248
  129.1 21.0 %collective-permute-start.26 = (bf16[384,1024]{1,0:T(8,128)(2,1)S(1)}, bf16[384,1024]{1,0:T(8,128)(2,1)S(1)}, u32[]{:S(2)}, u32[]{:S(2)}) collective-permute-start(bf16[384,1024]{1,0:T(8,128)(2,1)S(1)} %slice.51), channel_id=1, source_target_pairs={{96,0},{0,32},{32,64},{64,96},{97,1},{1,33},{33,65},{65,97},{98,2}... | collective-permute-start | bytes 2359304 | tf_op jit(solution)/shard_map/ppermute | solution.py:248
  135.7 18.5 %collective-permute-start.21 = (bf16[128,1536]{1,0:T(8,128)(2,1)S(1)}, bf16[128,1536]{1,0:T(8,128)(2,1)S(1)}, u32[]{:S(2)}, u32[]{:S(2)}) collective-permute-start(bf16[128,1536]{1,0:T(8,128)(2,1)S(1)} %get-tuple-element.66), channel_id=1, source_target_pairs={{6,0},{0,2},{2,4},{4,6},{7,1},{1,3},{3,5},{5,7},{14,8},{8,10},{10,... | collective-permute-start | bytes 1179656 | tf_op jit(solution)/shard_map/ppermute | solution.py:248
  144.9 8.4 %copy-start.12 = (bf16[384,1024]{1,0:T(8,128)(2,1)}, bf16[384,1024]{1,0:T(8,128)(2,1)S(1)}, u32[]{:S(2)}) copy-start(bf16[384,1024]{1,0:T(8,128)(2,1)S(1)} %collective-permute-done.27.refs_2_) | copy-start | bytes 2359300
  144.9 31.4 %collective-permute-start.13 = (bf16[128,1536]{1,0:T(8,128)(2,1)}, bf16[128,1536]{1,0:T(8,128)(2,1)S(1)}, u32[]{:S(2)}, u32[]{:S(2)}) collective-permute-start(bf16[128,1536]{1,0:T(8,128)(2,1)} %get-tuple-element.51), channel_id=1, source_target_pairs={{6,0},{0,2},{2,4},{4,6},{7,1},{1,3},{3,5},{5,7},{14,8},{8,10},{10,... | collective-permute-start | bytes 1179656 | tf_op jit(solution)/shard_map/ppermute | solution.py:248
  148.9 4.4 %copy-start.14 = (bf16[384,1024]{1,0:T(8,128)(2,1)}, bf16[384,1024]{1,0:T(8,128)(2,1)S(1)}, u32[]{:S(2)}) copy-start(bf16[384,1024]{1,0:T(8,128)(2,1)S(1)} %collective-permute-done.28.refs_3_) | copy-start | bytes 2359300
  148.9 29.6 %collective-permute-start.14 = (bf16[128,1536]{1,0:T(8,128)(2,1)}, bf16[128,1536]{1,0:T(8,128)(2,1)S(1)}, u32[]{:S(2)}, u32[]{:S(2)}) collective-permute-start(bf16[128,1536]{1,0:T(8,128)(2,1)} %get-tuple-element.52), channel_id=1, source_target_pairs={{2,0},{4,2},{6,4},{0,6},{3,1},{5,3},{7,5},{1,7},{10,8},{12,10},{14... | collective-permute-start | bytes 1179656 | tf_op jit(solution)/shard_map/ppermute | solution.py:248
  149.7 3.7 %copy-start.16 = (bf16[384,1024]{1,0:T(8,128)(2,1)}, bf16[384,1024]{1,0:T(8,128)(2,1)S(1)}, u32[]{:S(2)}) copy-start(bf16[384,1024]{1,0:T(8,128)(2,1)S(1)} %collective-permute-done.25.refs_0_) | copy-start | bytes 2359300
  149.7 19.5 %collective-permute-start.23 = (bf16[128,1536]{1,0:T(8,128)(2,1)S(1)}, bf16[128,1536]{1,0:T(8,128)(2,1)S(1)}, u32[]{:S(2)}, u32[]{:S(2)}) collective-permute-start(bf16[128,1536]{1,0:T(8,128)(2,1)S(1)} %get-tuple-element.65), channel_id=1, source_target_pairs={{2,0},{4,2},{6,4},{0,6},{3,1},{5,3},{7,5},{1,7},{10,8},{12,10},{14... | collective-permute-start | bytes 1179656 | tf_op jit(solution)/shard_map/ppermute | solution.py:248
  154.3 16.0 %collective-permute-start.29 = (bf16[512,1536]{1,0:T(8,128)(2,1)S(1)}, bf16[512,1536]{1,0:T(8,128)(2,1)S(1)}, u32[]{:S(2)}, u32[]{:S(2)}) collective-permute-start(bf16[512,1536]{1,0:T(8,128)(2,1)S(1)} %project.10), channel_id=1, source_target_pairs={{0,1},{1,0},{2,3},{3,2},{4,5},{5,4},{6,7},{7,6},{8,9},{9,8},{10,11... | collective-permute-start | bytes 4718600 | tf_op jit(solution)/shard_map/ppermute | solution.py:256
  154.4 16.9 %copy-start.17 = (bf16[384,1024]{1,0:T(8,128)(2,1)S(1)}, bf16[384,1024]{1,0:T(8,128)(2,1)}, u32[]{:S(2)}) copy-start(bf16[384,1024]{1,0:T(8,128)(2,1)} %copy-done.16) | copy-start | bytes 2359300
  154.4 16.9 %copy-start.19 = (bf16[384,1024]{1,0:T(8,128)(2,1)S(1)}, bf16[384,1024]{1,0:T(8,128)(2,1)}, u32[]{:S(2)}) copy-start(bf16[384,1024]{1,0:T(8,128)(2,1)} %copy-done.18) | copy-start | bytes 2359300
  155.3 15.9 %copy-start.10 = (bf16[512,1024]{1,0:T(8,128)(2,1)S(1)}, bf16[512,1024]{1,0:T(8,128)(2,1)}, u32[]{:S(2)}) copy-start(bf16[512,1024]{1,0:T(8,128)(2,1)} %get-tuple-element.46.n_ref) | copy-start | bytes 3145732
  155.3 15.9 %copy-start.13 = (bf16[384,1024]{1,0:T(8,128)(2,1)S(1)}, bf16[384,1024]{1,0:T(8,128)(2,1)}, u32[]{:S(2)}) copy-start(bf16[384,1024]{1,0:T(8,128)(2,1)} %copy-done.12) | copy-start | bytes 2359300
  155.3 15.9 %copy-start.15 = (bf16[384,1024]{1,0:T(8,128)(2,1)S(1)}, bf16[384,1024]{1,0:T(8,128)(2,1)}, u32[]{:S(2)}) copy-start(bf16[384,1024]{1,0:T(8,128)(2,1)} %copy-done.14) | copy-start | bytes 2359300
  155.3 46.4 %collective-permute-start.22 = (bf16[128,3072]{1,0:T(8,128)(2,1)}, bf16[128,3072]{1,0:T(8,128)(2,1)}, u32[]{:S(2)}, u32[]{:S(2)}) collective-permute-start(bf16[128,3072]{1,0:T(8,128)(2,1)} %pad_maximum_fusion.2), channel_id=1, source_target_pairs={{6,0},{0,2},{2,4},{4,6},{7,1},{1,3},{3,5},{5,7},{14,8},{8,10},{10,... | collective-permute-start | bytes 2359304 | tf_op jit(solution)/shard_map/ppermute | solution.py:248
  170.3 31.5 %collective-permute-start.24 = (bf16[128,3072]{1,0:T(8,128)(2,1)}, bf16[128,3072]{1,0:T(8,128)(2,1)}, u32[]{:S(2)}, u32[]{:S(2)}) collective-permute-start(bf16[128,3072]{1,0:T(8,128)(2,1)} %pad_maximum_fusion.3), channel_id=1, source_target_pairs={{2,0},{4,2},{6,4},{0,6},{3,1},{5,3},{7,5},{1,7},{10,8},{12,10},{14... | collective-permute-start | bytes 2359304 | tf_op jit(solution)/shard_map/ppermute | solution.py:248
  170.3 44.7 %copy-start = (bf16[128,6144]{1,0:T(8,128)(2,1)S(1)}, bf16[128,6144]{1,0:T(8,128)(2,1)}, u32[]{:S(2)}) copy-start(bf16[128,6144]{1,0:T(8,128)(2,1)} %res_ref.1) | copy-start | bytes 4718596
  170.3 28.1 %collective-permute-start.15 = (bf16[128,1536]{1,0:T(8,128)(2,1)S(1)}, bf16[128,1536]{1,0:T(8,128)(2,1)S(1)}, u32[]{:S(2)}, u32[]{:S(2)}) collective-permute-start(bf16[128,1536]{1,0:T(8,128)(2,1)S(1)} %get-tuple-element.53), channel_id=1, source_target_pairs={{4,0},{6,2},{0,4},{2,6},{5,1},{7,3},{1,5},{3,7},{12,8},{14,10},{8,... | collective-permute-start | bytes 1179656 | tf_op jit(solution)/shard_map/ppermute | solution.py:248
  176.3 25.5 %collective-permute-start.30 = (bf16[128,1536]{1,0:T(8,128)(2,1)}, bf16[128,1536]{1,0:T(8,128)(2,1)}, u32[]{:S(2)}, u32[]{:S(2)}) collective-permute-start(bf16[128,1536]{1,0:T(8,128)(2,1)} %get-tuple-element.62), channel_id=1, source_target_pairs={{6,0},{0,2},{2,4},{4,6},{7,1},{1,3},{3,5},{5,7},{14,8},{8,10},{10,... | collective-permute-start | bytes 1179656 | tf_op jit(solution)/shard_map/ppermute | solution.py:248
  179.3 35.7 %collective-permute-start.31 = (bf16[128,1536]{1,0:T(8,128)(2,1)}, bf16[128,1536]{1,0:T(8,128)(2,1)}, u32[]{:S(2)}, u32[]{:S(2)}) collective-permute-start(bf16[128,1536]{1,0:T(8,128)(2,1)} %get-tuple-element.63), channel_id=1, source_target_pairs={{2,0},{4,2},{6,4},{0,6},{3,1},{5,3},{7,5},{1,7},{10,8},{12,10},{14... | collective-permute-start | bytes 1179656 | tf_op jit(solution)/shard_map/ppermute | solution.py:248
  199.2 15.8 %collective-permute-start.32 = (bf16[128,1536]{1,0:T(8,128)(2,1)}, bf16[128,1536]{1,0:T(8,128)(2,1)}, u32[]{:S(2)}, u32[]{:S(2)}) collective-permute-start(bf16[128,1536]{1,0:T(8,128)(2,1)} %get-tuple-element.64), channel_id=1, source_target_pairs={{4,0},{6,2},{0,4},{2,6},{5,1},{7,3},{1,5},{3,7},{12,8},{14,10},{8,... | collective-permute-start | bytes 1179656 | tf_op jit(solution)/shard_map/ppermute | solution.py:248
  (11 other events, 10.4 us)

commit v2 on v1

v2 whole, which is shorter than its diff:
```python
import functools

import jax
import jax.numpy as jnp
from jax import lax
from jax.experimental import pallas as pl
from jax.experimental.pallas import tpu as pltpu
from jax.sharding import Mesh, PartitionSpec as P

DH = 128
F32 = jnp.float32
BF16 = jnp.bfloat16
REL = (0, 1, 3, 2)
YREL = (2, 1, 3, 0)
CHUNK = 256


def silu(block):
    wide = block.astype(F32)
    return (0.5 * wide * (1.0 + jnp.tanh(0.5 * wide))).astype(BF16)


def after(value, *others):
    return lax.optimization_barrier((value, *others))[0]


def contract(left, right, dims):
    return lax.dot_general(left, right, (dims, ((), ())), preferred_element_type=F32)


def state_body(k_ref, v_ref, kact_ref, state_ref):
    k_act = silu(k_ref[...])
    kact_ref[...] = k_act
    both = contract(k_act, v_ref[...], ((0,), (0,))).astype(BF16)
    state_ref[:DH, :] = both[:DH, :DH]
    state_ref[DH:, :] = both[DH:, DH:]


def span_state(key_in, value):
    tokens, width = key_in.shape
    column = pl.BlockSpec((tokens, 2 * DH), lambda h: (0, h))
    return pl.pallas_call(
        state_body,
        grid=(width // (2 * DH),),
        in_specs=[column, column],
        out_specs=[column, pl.BlockSpec((2 * DH, DH), lambda h: (h, 0))],
        out_shape=[
            jax.ShapeDtypeStruct((tokens, width), BF16),
            jax.ShapeDtypeStruct((width, DH), BF16),
        ],
        name="span_state",
    )(key_in, value)


def local_body(q_ref, kact_ref, v_ref, qact_ref, local_ref):
    q_act = silu(q_ref[...])
    qact_ref[...] = q_act
    tokens = q_act.shape[0]
    rows = lax.broadcasted_iota(jnp.int32, (CHUNK, CHUNK), 0)
    cols = lax.broadcasted_iota(jnp.int32, (CHUNK, CHUNK), 1)
    running = None
    for start in range(0, tokens, CHUNK):
        q_part = q_act[start : start + CHUNK]
        k_part = kact_ref[start : start + CHUNK, :]
        v_part = v_ref[start : start + CHUNK, :]
        scores = contract(q_part, k_part, ((1,), (1,)))
        scores = jnp.where(rows >= cols, scores, 0.0).astype(BF16)
        inner = contract(scores, v_part, ((1,), (0,)))
        if running is not None:
            inner = inner + contract(q_part, running.astype(BF16), ((1,), (0,)))
        local_ref[start : start + CHUNK, :] = inner
        if start + CHUNK < tokens:
            update = contract(k_part, v_part, ((0,), (0,)))
            running = update if running is None else running + update


def local_attention(query, k_act, value, first, heads):
    tokens, width = query.shape[0], heads * DH
    source = pl.BlockSpec((tokens, DH), lambda h: (0, h + first))
    column = pl.BlockSpec((tokens, DH), lambda h: (0, h))
    return pl.pallas_call(
        local_body,
        grid=(heads,),
        in_specs=[source, source, source],
        out_specs=[column, column],
        out_shape=[
            jax.ShapeDtypeStruct((tokens, width), BF16),
            jax.ShapeDtypeStruct((tokens, width), F32),
        ],
        name="local_attention",
    )(query, k_act, value)


def message_body(tab_ref, state_ref, z1, z2, z3, *outs):
    pieces = [piece[...].astype(F32) for piece in (z1, z2, z3)]
    zero = jnp.zeros_like(pieces[0])
    lower = zero
    for index, piece in enumerate(pieces):
        lower = lower + jnp.where(tab_ref[8 + index] > 0, piece, zero)
    first_core = tab_ref[14] == 0
    through = jnp.where(first_core, zero, lower)
    total = state_ref[...].astype(F32)
    total = total + jnp.where(first_core, pieces[0] + pieces[1] + pieces[2], zero)
    for index, out in enumerate(outs):
        out[...] = (through + jnp.where(tab_ref[11 + index] > 0, total, zero)).astype(BF16)


def messages(table, state, pieces):
    whole = pl.BlockSpec(state.shape, lambda g, t: (0, 0))
    return pl.pallas_call(
        message_body,
        grid_spec=pltpu.PrefetchScalarGridSpec(
            num_scalar_prefetch=1, grid=(1,), in_specs=[whole] * 4, out_specs=[whole] * 3
        ),
        out_shape=[jax.ShapeDtypeStruct(state.shape, BF16)] * 3,
        name="messages",
    )(table, state, *pieces)


def norm_body(
    tab_ref, qa_ref, la_ref, qb_ref, lb_ref, gain_ref, z1, z2, z3, x1, x2, x3, out_ref
):
    def part(q_ref, local_ref):
        prefix = x1[...].astype(F32) + x2[...].astype(F32) + x3[...].astype(F32)
        for index, piece in enumerate((z1, z2, z3)):
            prefix = prefix + jnp.where(tab_ref[8 + index] > 0, piece[...].astype(F32), 0.0)
        prefix = prefix.astype(BF16)
        zero = jnp.zeros((DH, DH), BF16)
        prefix = jnp.concatenate(
            [
                jnp.concatenate([prefix[:DH], zero], axis=1),
                jnp.concatenate([zero, prefix[DH:]], axis=1),
            ],
            axis=0,
        )
        head = lax.broadcasted_iota(jnp.int32, (2 * DH, 2 * DH), 0) // DH
        other = lax.broadcasted_iota(jnp.int32, (2 * DH, 2 * DH), 1) // DH
        average = jnp.where(head == other, 1.0 / DH, 0.0).astype(BF16)
        gain = gain_ref[...]
        for place in range(8):
            source = pl.ds(pl.multiple_of(tab_ref[place] * 128, 128), 128)
            attended = local_ref[source, :] + contract(q_ref[source, :], prefix, ((1,), (0,)))
            meansq = contract((attended * attended).astype(BF16), average, ((1,), (0,)))
            normed = (attended * lax.rsqrt(meansq + 1e-06) * gain).astype(BF16)
            out_ref[place * 128 : (place + 1) * 128, :] = normed

    early = pl.program_id(0) < pl.num_programs(0) // 2
    pl.when(early)(lambda: part(qa_ref, la_ref))
    pl.when(jnp.logical_not(early))(lambda: part(qb_ref, lb_ref))


def norm(table, halves, gain, z_pieces, x_pieces):
    (qa, la), (qb, lb) = halves
    tokens, width = qa.shape[0], qa.shape[1] * 2
    steps = width // (2 * DH)
    first = pl.BlockSpec((tokens, 2 * DH), lambda h, t: (0, jnp.minimum(h, steps // 2 - 1)))
    second = pl.BlockSpec((tokens, 2 * DH), lambda h, t: (0, jnp.maximum(h - steps // 2, 0)))
    pair = pl.BlockSpec((tokens, 2 * DH), lambda h, t: (0, h))
    square = pl.BlockSpec((2 * DH, DH), lambda h, t: (h, 0))
    return pl.pallas_call(
        norm_body,
        grid_spec=pltpu.PrefetchScalarGridSpec(
            num_scalar_prefetch=1,
            grid=(steps,),
            in_specs=[first, first, second, second, pl.BlockSpec((1, 2 * DH), lambda h, t: (0, h))]
            + [square] * 6,
            out_specs=pair,
        ),
        out_shape=jax.ShapeDtypeStruct((tokens, width), BF16),
        name="norm",
    )(table, qa, la, qb, lb, gain, *z_pieces, *x_pieces)


def project_body(counts, core_ref, own_ref, other_ref, *refs):
    weights, outs = refs[: len(counts)], refs[len(counts) :]
    step = pl.program_id(0)
    depth, rows = own_ref.shape[1], outs[0].shape[0]
    first_core = core_ref[0] == 0
    first = 0
    for w_ref, count in zip(weights, counts):

        @pl.when((step >= first) & (step < first + count))
        def _(w_ref=w_ref):
            total = contract(own_ref[...], w_ref[:, :depth], ((1,), (1,)))
            total = total + contract(other_ref[...], w_ref[:, depth:], ((1,), (1,)))
            far, right, left, own = (
                total[index * rows : (index + 1) * rows].astype(BF16) for index in range(4)
            )
            for out, block in zip(
                outs,
                (jnp.where(first_core, left, right), far, jnp.where(first_core, right, left), own),
            ):
                out[...] = block

        first += count


def project(core, own, other, weights, tile):
    rows, depth = own.shape
    counts = tuple(w.shape[0] // tile for w in weights)
    columns = tile * sum(counts)
    specs, first = [], 0
    for count in counts:
        specs.append(
            pl.BlockSpec(
                (tile, 2 * depth),
                lambda g, t, first=first, count=count: (jnp.clip(g - first, 0, count - 1), 0),
            )
        )
        first += count
    whole = pl.BlockSpec((rows, depth), lambda g, t: (0, 0))
    return pl.pallas_call(
        functools.partial(project_body, counts),
        grid_spec=pltpu.PrefetchScalarGridSpec(
            num_scalar_prefetch=1,
            grid=(sum(counts),),
            in_specs=[whole, whole] + specs,
            out_specs=[pl.BlockSpec((rows // 4, tile), lambda g, t: (0, g))] * 4,
        ),
        out_shape=[jax.ShapeDtypeStruct((rows // 4, columns), BF16)] * 4,
        compiler_params=pltpu.CompilerParams(vmem_limit_bytes=40 * 1024 * 1024),
        name="project",
    )(core, own, other, *weights)


def finish_body(layout, tab_ref, res_ref, *refs):
    out_ref = refs[-1]
    kept, got = refs[: len(refs) // 2], refs[len(refs) // 2 : -1]
    first_core = tab_ref[16] == 0
    groups = []
    for keep, receive in zip(kept, got):
        mine, theirs = keep[...], receive[...].astype(F32)
        groups.append((jnp.where(first_core, mine, theirs), jnp.where(first_core, theirs, mine)))
    for place, ((c0, o0), (c1, o1)) in enumerate(layout):
        both = jnp.concatenate(
            [groups[c0][0][:, o0 : o0 + 192], groups[c1][1][:, o1 : o1 + 192]], axis=1
        )
        target = pl.ds(pl.multiple_of(tab_ref[place] * 384, 128), 384)
        out_ref[:, target] = (both + res_ref[:, target].astype(F32)).astype(BF16)


def finish(layout, table, residual, kept, got):
    return pl.pallas_call(
        functools.partial(finish_body, layout),
        in_specs=[pl.BlockSpec(memory_space=pltpu.SMEM)]
        + [pl.BlockSpec(memory_space=pltpu.VMEM)] * (1 + len(kept) + len(got)),
        out_specs=pl.BlockSpec(memory_space=pltpu.VMEM),
        out_shape=jax.ShapeDtypeStruct(residual.shape, BF16),
        compiler_params=pltpu.CompilerParams(vmem_limit_bytes=40 * 1024 * 1024),
        name="finish",
    )(table, residual, *kept, *got)


def fetch(array, axis, offset):
    return lax.ppermute(array, axis, [((i + offset) % 4, i) for i in range(4)])


def fetch_mixed(array, level, offset):
    pairs = []
    for x in range(4):
        for z in range(4):
            for c in range(2):
                if (level == 1) == (c == 0):
                    source = (x, (z + offset) % 4, c)
                else:
                    source = ((x + offset) % 4, z, c)
                pairs.append(((source[0] * 4 + source[1]) * 2 + c, (x * 4 + z) * 2 + c))
    return lax.ppermute(array, ("x", "z", "c"), pairs)


def swap(array):
    return lax.ppermute(array, "c", [(0, 1), (1, 0)])


def push(array, hops):
    pairs = []
    for y in range(4):
        pairs.append((y * 2, (y + hops) % 4 * 2))
        pairs.append((y * 2 + 1, (y - hops) % 4 * 2 + 1))
    return lax.ppermute(array, ("y", "c"), pairs)


def add(left, right):
    return (left.astype(F32) + right.astype(F32)).astype(BF16)


def reduce_ring(parts):
    behind, far, ahead, own = parts
    return own, push(add(push(add(push(behind, 1), far), 1), ahead), 1)


def reduce_direct(parts):
    behind, far, ahead, own = parts
    return own, push(far, 2), push(ahead, 1), push(behind, 3)


def settle_chunk(parts, c):
    def rows(which):
        total = 0.0
        for part in parts:
            total = total + lax.dynamic_slice_in_dim(part, which * 128, 128).astype(F32)
        return total

    return rows(c), swap(rows(1 - c).astype(BF16))


def per_device(query, key_in, value, head_gain, out_weight, residual):
    x, z, y, c = (lax.axis_index(name) for name in ("x", "z", "y", "c"))
    near, away = jnp.where(c == 0, z, x), jnp.where(c == 0, x, z)
    blocks = [(y + offset) % 4 * 2 + core for offset in YREL for core in (0, 1)]
    flags = [(near + offset) % 4 < near for offset in REL[1:]]
    flags += [away < (away - offset) % 4 for offset in REL[1:]]
    table = jnp.stack([jnp.asarray(entry, jnp.int32) for entry in blocks + flags + [c]])

    turned = out_weight.T
    half = turned.shape[0] // 2
    keep = lax.dynamic_slice_in_dim(turned, c * half, half)
    give = lax.dynamic_slice_in_dim(turned, (1 - c) * half, half)
    k_act, state = span_state(after(key_in, keep, give), value)
    level1 = [fetch_mixed(state, 1, offset) for offset in REL[1:]]
    base = jnp.concatenate([keep, after(swap(give), state)], axis=1)
    near_plus, near_minus = fetch_mixed(base, 1, 1), fetch_mixed(base, 1, 3)

    heads = query.shape[1] // DH // 2
    early = local_attention(query, k_act, value, 0, heads)
    level1 = [after(piece, early[0]) for piece in level1]
    sent = messages(table, state, level1)
    level2 = [fetch_mixed(piece, 2, offset) for piece, offset in zip(sent, REL[1:])]
    far_weights = fetch_mixed(after(base, sent[0]), 1, 2)
    late = local_attention(after(query, sent[0]), k_act, value, heads, heads)
    level2 = [after(piece, late[0]) for piece in level2]

    g0a = jnp.concatenate([base, near_plus], axis=0)
    ready = after(g0a, *level2)
    g1a, g3a = fetch_mixed(ready, 2, 1), fetch_mixed(ready, 2, 3)
    table = after(table, far_weights, near_plus, near_minus)
    normed = norm(table, (early, late), head_gain.reshape(1, -1), level1, level2)
    other = swap(normed)
    g0b = jnp.concatenate([near_minus, far_weights], axis=0)
    core = c.astype(jnp.int32).reshape(1)
    first = project(core, normed, other, [g0a, g0b], 384)
    ready = after(g0b, g1a, g3a, first[0])
    g1b, g3b = fetch_mixed(ready, 2, 1), fetch_mixed(ready, 2, 3)
    first = reduce_ring(first)
    second = project(core, after(normed, first[0]), other, [g1a, g3a], 384)
    g2 = [
        fetch_mixed(after(g1a, g1b, g3b, second[0]), 2, 1),
        fetch_mixed(after(g3b, g1b, second[0]), 2, 3),
    ]
    second = reduce_ring(second)
    third = project(core, after(normed, second[0], *first), other, [g1b, g3b], 384)
    third = reduce_ring(third)
    fourth = project(core, after(normed, third[0], *second), other, g2, 384)
    fourth = reduce_direct(fourth)
    settled = [settle_chunk(parts, c) for parts in (first, second, third, fourth)]
    spot = (
        ((0, 0), (0, 1), (0, 2), (0, 3)),
        ((1, 0), (1, 1), (2, 0), (2, 1)),
        ((1, 2), (1, 3), (2, 2), (2, 3)),
        ((3, 0), (3, 1), (3, 2), (3, 3)),
    )
    layout, shards = [], []
    for i, x_off in enumerate(REL):
        for j, z_off in enumerate(REL):
            layout.append(
                tuple((chunk, part * half) for chunk, part in (spot[i][j], spot[j][i]))
            )
            shards.append((x + x_off) % 4 * 4 + (z + z_off) % 4)
    shard_table = jnp.stack([jnp.asarray(entry, jnp.int32) for entry in shards + [c]])
    kept, got = zip(*settled)
    return finish(tuple(layout), shard_table, residual, kept, got)


def solution(mesh):
    torus = Mesh(mesh.devices.reshape(4, 4, 4, 2), ("x", "z", "y", "c"))
    seq, hx = ("x", "z"), ("y", "c")
    return jax.shard_map(
        per_device,
        mesh=torus,
        in_specs=(P(seq, hx), P(seq, hx), P(seq, hx), P(hx), P(hx, seq), P(seq + hx, None)),
        out_specs=P(seq + hx, None),
        check_vma=False,
    )
```

time: 224 us -> 176 us (0.79)
  the two profiles are of different devices: /device:TPU:24 before, /device:TPU:1 now
where the time goes in v2:
time: 176 us; the launch traced here: 175 us
  starting transfers between devices  57.9 us (33%)
  waiting for transfers between devices  52.8 us (30%)
  Pallas kernels  49.6 us (28%)
  other arithmetic  9.12 us (5%)
  local copies, waits for them, and re-layouts  5.85 us (3%)
    ppermute x15, waiting for transfers between devices, fetch_mixed(): return lax.ppermute(array, ('x', 'z', 'c'), pairs)  30.5 us
    ppermute x12, starting transfers between devices, push(): return lax.ppermute(array, ('y', 'c'), pairs)  22.3 us
    pallas_call x4, Pallas kernels, project(): pl.pallas_call(functools.partial(project_body, counts), grid_spec=pltpu.P...  20.3 us
    ppermute x12, waiting for transfers between devices, push(): return lax.ppermute(array, ('y', 'c'), pairs)  20.1 us
    ppermute x6, starting transfers between devices, swap(): return lax.ppermute(array, 'c', [(0, 1), (1, 0)])  19.1 us
    ppermute x15, starting transfers between devices, fetch_mixed(): return lax.ppermute(array, ('x', 'z', 'c'), pairs)  16.4 us
    pallas_call x2, Pallas kernels, local_attention(): pl.pallas_call(local_body, grid=(heads,), in_specs=[source, source, sourc...  11.5 us
    pallas_call x1, Pallas kernels, norm(): pl.pallas_call(norm_body, grid_spec=pltpu.PrefetchScalarGridSpec(num_scal...  6.96 us
  transfers between devices with their start and end apart: 33, of which 14 were waited for; matrix products, arithmetic and copies ran while one was open for 5% of the time, Pallas kernels for 23%

profile of v2, /device:TPU:1, one launch (start us, length us, event | category | flops | bytes accessed | tf_op | source)
XLA Modules:
  0.0 175.5 jit_solution(12277249935808717044)
XLA Ops:
  0.0 1.8 %constant_dynamic-slice_fusion.1 = (bf16[1024,192]{1,0:T(8,128)(2,1)S(1)}, bf16[1024,192]{1,0:T(8,128)(2,1)S(1)}) fusion(bf16[1024,384]{1,0:T(8,128)(2,1)} %param.10, s32[]{:T(128)S(6)} %select_n.187, s32[]{:T(128)S(6)} %select_n.188), kind=kLoop, calls=%fused_computation.19 | loop fusion | bytes 1572872 | tf_op jit(solution)/shard_map/dynamic-slice
  2.0 1.5 collective-permute-start
  3.7 4.7 %span_state.1 = (bf16[1024,1024]{1,0:T(8,128)(2,1)}, bf16[1024,128]{1,0:T(8,128)(2,1)}) custom-call(bf16[1024,1024]{1,0:T(8,128)(2,1)} %k_ref, bf16[1024,1024]{1,0:T(8,128)(2,1)} %v_ref.5), custom_call_target="tpu_custom_call" | custom-call | tf_op jit(solution)/shard_map/span_state/pallas_call | solution.py:42
  8.4 2.6 %collective-permute-start.1 = (bf16[1024,128]{1,0:T(8,128)(2,1)}, bf16[1024,128]{1,0:T(8,128)(2,1)S(1)}, u32[]{:S(2)}, u32[]{:S(2)}) collective-permute-start(bf16[1024,128]{1,0:T(8,128)(2,1)} %get-tuple-element.49.state_ref), channel_id=1, source_target_pairs={{8,0},{33,1},{16,8},{41,9},{24,16},{49,17},{0,24},{57,25},{40,32},... | collective-permute-start | bytes 786440 | tf_op jit(solution)/shard_map/ppermute | solution.py:268
  11.0 1.7 collective-permute-start.3
  12.7 5.7 %local_attention.2 = (bf16[1024,512]{1,0:T(8,128)(2,1)}, f32[1024,512]{1,0:T(8,128)}) custom-call(bf16[1024,1024]{1,0:T(8,128)(2,1)} %q_ref.2, bf16[1024,1024]{1,0:T(8,128)(2,1)} %get-tuple-element.51.kact_ref, bf16[1024,1024]{1,0:T(8,128)(2,1)} %v_ref.5), custom_call_target="tpu_custom_call" | custom-call | tf_op jit(solution)/shard_map/local_attention/pallas_call | solution.py:81
  19.1 1.6 collective-permute-done.2.z2
  22.1 3.1 %messages.1 = (bf16[1024,128]{1,0:T(8,128)(2,1)}, bf16[1024,128]{1,0:T(8,128)(2,1)}, bf16[1024,128]{1,0:T(8,128)(2,1)}) custom-call(s32[15]{0:T(128)} %stack.156.tab_ref, bf16[1024,128]{1,0:T(8,128)(2,1)} %get-tuple-element.49.state_ref, bf16[1024,128]{1,0:T(8,128)(2,1)} %copy-done.2, bf16[1024,128]{1,0:T(8,128)(2,1)} %copy-done.3, bf16[1024,128]{1,0:T(8,128)(2,1)} %copy-done.4), custom_call_target="tpu_custom_call" | custom-call | tf_op jit(solution)/shard_map/messages/pallas_call | solution.py:110
  26.2 2.4 %collective-permute-start.5 = (bf16[192,2048]{1,0:T(8,128)(2,1)}, bf16[192,2048]{1,0:T(8,128)(2,1)}, u32[]{:S(2)}, u32[]{:S(2)}) collective-permute-start(bf16[192,2048]{1,0:T(8,128)(2,1)} %pad_maximum_fusion.1), channel_id=1, source_target_pairs={{8,0},{33,1},{16,8},{41,9},{24,16},{49,17},{0,24},{57,25},{40,32},... | collective-permute-start | bytes 2359304 | tf_op jit(solution)/shard_map/ppermute | solution.py:268
  28.6 3.8 %collective-permute-start.7 = (bf16[1024,128]{1,0:T(8,128)(2,1)S(1)}, bf16[1024,128]{1,0:T(8,128)(2,1)S(1)}, u32[]{:S(2)}, u32[]{:S(2)}) collective-permute-start(bf16[1024,128]{1,0:T(8,128)(2,1)S(1)} %copy-done.11), channel_id=1, source_target_pairs={{32,0},{9,1},{40,8},{17,9},{48,16},{25,17},{56,24},{1,25},{64,32},... | collective-permute-start | bytes 786440 | tf_op jit(solution)/shard_map/ppermute | solution.py:268
  32.4 12.8 %collective-permute-done.7.x1 = bf16[1024,128]{1,0:T(8,128)(2,1)S(1)} collective-permute-done((bf16[1024,128]{1,0:T(8,128)(2,1)S(1)}, bf16[1024,128]{1,0:T(8,128)(2,1)S(1)}, u32[]{:S(2)}, u32[]{:S(2)}) %collective-permute-start.7) | collective-permute-done | bytes 262176 | tf_op jit(solution)/shard_map/ppermute | solution.py:268
  45.2 1.5 collective-permute-start.9
  46.6 5.7 %local_attention.3 = (bf16[1024,512]{1,0:T(8,128)(2,1)}, f32[1024,512]{1,0:T(8,128)}) custom-call(bf16[1024,1024]{1,0:T(8,128)(2,1)} %q_ref.2, bf16[1024,1024]{1,0:T(8,128)(2,1)} %get-tuple-element.51.kact_ref, bf16[1024,1024]{1,0:T(8,128)(2,1)} %v_ref.5), custom_call_target="tpu_custom_call" | custom-call | tf_op jit(solution)/shard_map/local_attention/pallas_call | solution.py:81
  52.4 2.4 %collective-permute-done.9.x3 = bf16[1024,128]{1,0:T(8,128)(2,1)S(1)} collective-permute-done((bf16[1024,128]{1,0:T(8,128)(2,1)S(1)}, bf16[1024,128]{1,0:T(8,128)(2,1)S(1)}, u32[]{:S(2)}, u32[]{:S(2)}) %collective-permute-start.9) | collective-permute-done | bytes 262176 | tf_op jit(solution)/shard_map/ppermute | solution.py:268
  55.5 7.0 %norm.1.own_ref = bf16[1024,1024]{1,0:T(8,128)(2,1)} custom-call(s32[15]{0:T(128)} %stack.156.tab_ref, bf16[1024,512]{1,0:T(8,128)(2,1)} %get-tuple-element.52.qa_ref, f32[1024,512]{1,0:T(8,128)} %get-tuple-element.59.la_ref, bf16[1024,512]{1,0:T(8,128)(2,1)} %get-tuple-element.61.qb_ref, f32[1024,512]{1,0:T(8,128)} %get-tuple-element.62.lb_ref, ...), custom_call_target="tpu_custom_call" | custom-call | tf_op jit(solution)/shard_map/norm/pallas_call | solution.py:160
  62.4 1.3 collective-permute-start.10
  63.7 1.3 pad_maximum_fusion.refs_0_
  65.5 1.1 collective-permute-start.15
  67.7 4.9 %project.4 = (bf16[256,768]{1,0:T(8,128)(2,1)S(1)}, bf16[256,768]{1,0:T(8,128)(2,1)S(1)}, bf16[256,768]{1,0:T(8,128)(2,1)S(1)}, bf16[256,768]{1,0:T(8,128)(2,1)S(1)}) custom-call(s32[1]{0:T(128)} %bitcast.16.core_ref, bf16[1024,1024]{1,0:T(8,128)(2,1)S(1)} %copy-done, bf16[1024,1024]{1,0:T(8,128)(2,1)S(1)} %collective-permute-done.10.other_ref, ...), custom_call_target="tpu_custom_call" | custom-call | tf_op jit(solution)/shard_map/project/pallas_call | solution.py:212
  72.6 12.0 %collective-permute-done.14.refs_0_ = bf16[384,2048]{1,0:T(8,128)(2,1)S(1)} collective-permute-done((bf16[384,2048]{1,0:T(8,128)(2,1)S(1)}, bf16[384,2048]{1,0:T(8,128)(2,1)S(1)}, u32[]{:S(2)}, u32[]{:S(2)}) %collective-permute-start.14) | collective-permute-done | bytes 1572896 | tf_op jit(solution)/shard_map/ppermute | solution.py:268
  84.7 1.6 collective-permute-done.15.refs_1_
  86.3 1.5 collective-permute-start.20
  87.8 2.7 %collective-permute-start.11 = (bf16[256,768]{1,0:T(8,128)(2,1)S(1)}, bf16[256,768]{1,0:T(8,128)(2,1)S(1)}, u32[]{:S(2)}, u32[]{:S(2)}) collective-permute-start(bf16[256,768]{1,0:T(8,128)(2,1)S(1)} %get-tuple-element.69), channel_id=1, source_target_pairs={{0,2},{1,7},{2,4},{3,1},{4,6},{5,3},{6,0},{7,5},{8,10},{9,15},{10,... | collective-permute-start | bytes 1179656 | tf_op jit(solution)/shard_map/ppermute | solution.py:280
  90.5 4.7 %collective-permute-done.11 = bf16[256,768]{1,0:T(8,128)(2,1)S(1)} collective-permute-done((bf16[256,768]{1,0:T(8,128)(2,1)S(1)}, bf16[256,768]{1,0:T(8,128)(2,1)S(1)}, u32[]{:S(2)}, u32[]{:S(2)}) %collective-permute-start.11) | collective-permute-done | bytes 393248 | tf_op jit(solution)/shard_map/ppermute | solution.py:280
  95.3 3.5 %collective-permute-start.12 = (bf16[256,768]{1,0:T(8,128)(2,1)S(1)}, bf16[256,768]{1,0:T(8,128)(2,1)S(1)}, u32[]{:S(2)}, u32[]{:S(2)}) collective-permute-start(bf16[256,768]{1,0:T(8,128)(2,1)S(1)} %add_convert_fusion.5), channel_id=1, source_target_pairs={{0,2},{1,7},{2,4},{3,1},{4,6},{5,3},{6,0},{7,5},{8,10},{9,15},{10,... | collective-permute-start | bytes 1179656 | tf_op jit(solution)/shard_map/ppermute | solution.py:280
  98.8 4.7 %collective-permute-done.12 = bf16[256,768]{1,0:T(8,128)(2,1)S(1)} collective-permute-done((bf16[256,768]{1,0:T(8,128)(2,1)S(1)}, bf16[256,768]{1,0:T(8,128)(2,1)S(1)}, u32[]{:S(2)}, u32[]{:S(2)}) %collective-permute-start.12) | collective-permute-done | bytes 393248 | tf_op jit(solution)/shard_map/ppermute | solution.py:280
  103.6 3.5 %collective-permute-start.13 = (bf16[256,768]{1,0:T(8,128)(2,1)S(1)}, bf16[256,768]{1,0:T(8,128)(2,1)S(1)}, u32[]{:S(2)}, u32[]{:S(2)}) collective-permute-start(bf16[256,768]{1,0:T(8,128)(2,1)S(1)} %add_convert_fusion.4), channel_id=1, source_target_pairs={{0,2},{1,7},{2,4},{3,1},{4,6},{5,3},{6,0},{7,5},{8,10},{9,15},{10,... | collective-permute-start | bytes 1179656 | tf_op jit(solution)/shard_map/ppermute | solution.py:280
  107.1 4.9 %project.5 = (bf16[256,768]{1,0:T(8,128)(2,1)S(1)}, bf16[256,768]{1,0:T(8,128)(2,1)S(1)}, bf16[256,768]{1,0:T(8,128)(2,1)S(1)}, bf16[256,768]{1,0:T(8,128)(2,1)S(1)}) custom-call(s32[1]{0:T(128)} %bitcast.16.core_ref, bf16[1024,1024]{1,0:T(8,128)(2,1)S(1)} %copy-done, bf16[1024,1024]{1,0:T(8,128)(2,1)S(1)} %collective-permute-done.10.other_ref, ...), custom_call_target="tpu_custom_call" | custom-call | tf_op jit(solution)/shard_map/project/pallas_call | solution.py:212
  112.1 1.3 collective-permute-start.24
  113.6 4.9 %project.6 = (bf16[256,768]{1,0:T(8,128)(2,1)S(1)}, bf16[256,768]{1,0:T(8,128)(2,1)S(1)}, bf16[256,768]{1,0:T(8,128)(2,1)S(1)}, bf16[256,768]{1,0:T(8,128)(2,1)S(1)}) custom-call(s32[1]{0:T(128)} %bitcast.16.core_ref, bf16[1024,1024]{1,0:T(8,128)(2,1)S(1)} %copy-done, bf16[1024,1024]{1,0:T(8,128)(2,1)S(1)} %collective-permute-done.10.other_ref, ...), custom_call_target="tpu_custom_call" | custom-call | tf_op jit(solution)/shard_map/project/pallas_call | solution.py:212
  118.5 1.4 collective-permute-start.21
  120.1 5.4 %collective-permute-done.21 = bf16[256,768]{1,0:T(8,128)(2,1)S(1)} collective-permute-done((bf16[256,768]{1,0:T(8,128)(2,1)S(1)}, bf16[256,768]{1,0:T(8,128)(2,1)S(1)}, u32[]{:S(2)}, u32[]{:S(2)}) %collective-permute-start.21) | collective-permute-done | bytes 393248 | tf_op jit(solution)/shard_map/ppermute | solution.py:280
  125.6 2.6 %collective-permute-start.22 = (bf16[256,768]{1,0:T(8,128)(2,1)S(1)}, bf16[256,768]{1,0:T(8,128)(2,1)S(1)}, u32[]{:S(2)}, u32[]{:S(2)}) collective-permute-start(bf16[256,768]{1,0:T(8,128)(2,1)S(1)} %add_convert_fusion.1), channel_id=1, source_target_pairs={{0,2},{1,7},{2,4},{3,1},{4,6},{5,3},{6,0},{7,5},{8,10},{9,15},{10,... | collective-permute-start | bytes 1179656 | tf_op jit(solution)/shard_map/ppermute | solution.py:280
  128.2 1.5 collective-permute-done.17
  129.8 2.6 %collective-permute-start.18 = (bf16[256,768]{1,0:T(8,128)(2,1)S(1)}, bf16[256,768]{1,0:T(8,128)(2,1)S(1)}, u32[]{:S(2)}, u32[]{:S(2)}) collective-permute-start(bf16[256,768]{1,0:T(8,128)(2,1)S(1)} %add_convert_fusion.2), channel_id=1, source_target_pairs={{0,2},{1,7},{2,4},{3,1},{4,6},{5,3},{6,0},{7,5},{8,10},{9,15},{10,... | collective-permute-start | bytes 1179656 | tf_op jit(solution)/shard_map/ppermute | solution.py:280
  132.4 1.5 collective-permute-done.22
  134.8 2.5 %collective-permute-start.23 = (bf16[256,768]{1,0:T(8,128)(2,1)}, bf16[256,768]{1,0:T(8,128)(2,1)}, u32[]{:S(2)}, u32[]{:S(2)}) collective-permute-start(bf16[256,768]{1,0:T(8,128)(2,1)} %add_convert_fusion), channel_id=1, source_target_pairs={{0,2},{1,7},{2,4},{3,1},{4,6},{5,3},{6,0},{7,5},{8,10},{9,15},{10,... | collective-permute-start | bytes 1179656 | tf_op jit(solution)/shard_map/ppermute | solution.py:280
  138.9 5.6 %project.7 = (bf16[256,768]{1,0:T(8,128)(2,1)}, bf16[256,768]{1,0:T(8,128)(2,1)}, bf16[256,768]{1,0:T(8,128)(2,1)}, bf16[256,768]{1,0:T(8,128)(2,1)S(1)}) custom-call(s32[1]{0:T(128)} %bitcast.16.core_ref, bf16[1024,1024]{1,0:T(8,128)(2,1)S(1)} %copy-done, bf16[1024,1024]{1,0:T(8,128)(2,1)S(1)} %collective-permute-done.10.other_ref, ...), custom_call_target="tpu_custom_call" | custom-call | tf_op jit(solution)/shard_map/project/pallas_call | solution.py:212
  144.5 1.4 collective-permute-start.28
  145.9 1.3 collective-permute-start.27
  148.7 7.3 %collective-permute-start.29 = (bf16[128,768]{1,0:T(8,128)(2,1)}, bf16[128,768]{1,0:T(8,128)(2,1)}, u32[]{:S(2)}, u32[]{:S(2)}) collective-permute-start(bf16[128,768]{1,0:T(8,128)(2,1)} %get-tuple-element.97), channel_id=1, source_target_pairs={{0,1},{1,0},{2,3},{3,2},{4,5},{5,4},{6,7},{7,6},{8,9},{9,8},{10,11... | collective-permute-start | bytes 589832 | tf_op jit(solution)/shard_map/ppermute | solution.py:272
  156.7 1.7 collective-permute-start.30
  158.4 1.8 %add_convert_fusion.7 = (bf16[128,768]{1,0:T(8,128)(2,1)}, f32[128,768]{1,0:T(8,128)S(1)}) fusion(bf16[256,768]{1,0:T(8,128)(2,1)} %collective-permute-done.23, s32[]{:T(128)S(6)} %select_n.190, bf16[256,768]{1,0:T(8,128)(2,1)S(1)} %get-tuple-element.80, s32[]{:T(128)S(6)} %select_n.189), kind=kLoop, calls=%fused_computation.9 | loop fusion | flops 688128 | bytes 1376264 | tf_op jit(solution)/shard_map/convert_element_type | solution.py:304
  160.2 1.3 collective-permute-done.28
  162.0 2.2 %add_convert_fusion.6 = (bf16[128,768]{1,0:T(8,128)(2,1)}, f32[128,768]{1,0:T(8,128)S(1)}) fusion(bf16[256,768]{1,0:T(8,128)(2,1)} %collective-permute-done.28, s32[]{:T(128)S(6)} %select_n.190, bf16[256,768]{1,0:T(8,128)(2,1)} %collective-permute-done.27, bf16[256,768]{1,0:T(8,128)(2,1)} %collective-permute-done.26, ...), kind=kLoop, calls=%fused_computation.8 | loop fusion | flops 1474560 | bytes 2162696 | tf_op jit(solution)/shard_map/convert_element_type | solution.py:304
  164.2 6.8 %collective-permute-start.32 = (bf16[128,768]{1,0:T(8,128)(2,1)}, bf16[128,768]{1,0:T(8,128)(2,1)S(1)}, u32[]{:S(2)}, u32[]{:S(2)}) collective-permute-start(bf16[128,768]{1,0:T(8,128)(2,1)} %get-tuple-element.91), channel_id=1, source_target_pairs={{0,1},{1,0},{2,3},{3,2},{4,5},{5,4},{6,7},{7,6},{8,9},{9,8},{10,11... | collective-permute-start | bytes 589832 | tf_op jit(solution)/shard_map/ppermute | solution.py:272
  171.2 1.2 collective-permute-done.32.refs_7_
  172.3 3.1 %finish.1 = bf16[128,6144]{1,0:T(8,128)(2,1)} custom-call(s32[17]{0:T(128)S(1)} %stack.135.tab_ref, bf16[128,6144]{1,0:T(8,128)(2,1)S(1)} %copy-done.1, f32[128,768]{1,0:T(8,128)S(1)} %get-tuple-element.98.refs_0_, f32[128,768]{1,0:T(8,128)S(1)} %get-tuple-element.96.refs_1_, f32[128,768]{1,0:T(8,128)S(1)} %get-tuple-element.94.refs_2_, ...), custom_call_target="tpu_custom_call" | custom-call | tf_op jit(solution)/shard_map/finish/pallas_call | solution.py:243
  (71 shorter events, 12.1 us)
Async XLA Ops:
  2.0 23.2 %collective-permute-start = (bf16[192,1024]{1,0:T(8,128)(2,1)S(1)}, bf16[192,1024]{1,0:T(8,128)(2,1)S(1)}, u32[]{:S(2)}, u32[]{:S(2)}) collective-permute-start(bf16[192,1024]{1,0:T(8,128)(2,1)S(1)} %bitcast.36), channel_id=1, source_target_pairs={{0,1},{1,0},{2,3},{3,2},{4,5},{5,4},{6,7},{7,6},{8,9},{9,8},{10,11... | collective-permute-start | bytes 1179656 | tf_op jit(solution)/shard_map/ppermute | solution.py:272
  8.4 10.7 %collective-permute-start.1 = (bf16[1024,128]{1,0:T(8,128)(2,1)}, bf16[1024,128]{1,0:T(8,128)(2,1)S(1)}, u32[]{:S(2)}, u32[]{:S(2)}) collective-permute-start(bf16[1024,128]{1,0:T(8,128)(2,1)} %get-tuple-element.49.state_ref), channel_id=1, source_target_pairs={{8,0},{33,1},{16,8},{41,9},{24,16},{49,17},{0,24},{57,25},{40,32},... | collective-permute-start | bytes 786440 | tf_op jit(solution)/shard_map/ppermute | solution.py:268
  11.0 9.7 %collective-permute-start.2 = (bf16[1024,128]{1,0:T(8,128)(2,1)}, bf16[1024,128]{1,0:T(8,128)(2,1)S(1)}, u32[]{:S(2)}, u32[]{:S(2)}) collective-permute-start(bf16[1024,128]{1,0:T(8,128)(2,1)} %get-tuple-element.49.state_ref), channel_id=1, source_target_pairs={{24,0},{97,1},{0,8},{105,9},{8,16},{113,17},{16,24},{121,25},{56,3... | collective-permute-start | bytes 786440 | tf_op jit(solution)/shard_map/ppermute | solution.py:268
  11.0 9.7 %collective-permute-start.3 = (bf16[1024,128]{1,0:T(8,128)(2,1)}, bf16[1024,128]{1,0:T(8,128)(2,1)S(1)}, u32[]{:S(2)}, u32[]{:S(2)}) collective-permute-start(bf16[1024,128]{1,0:T(8,128)(2,1)} %get-tuple-element.49.state_ref), channel_id=1, source_target_pairs={{16,0},{65,1},{24,8},{73,9},{0,16},{81,17},{8,24},{89,25},{48,32},... | collective-permute-start | bytes 786440 | tf_op jit(solution)/shard_map/ppermute | solution.py:268
  19.1 1.7 copy-start.2
  20.7 0.7 copy-start.3
  21.4 0.7 copy-start.4
  25.2 3.4 %copy-start.11 = (bf16[1024,128]{1,0:T(8,128)(2,1)S(1)}, bf16[1024,128]{1,0:T(8,128)(2,1)}, u32[]{:S(2)}) copy-start(bf16[1024,128]{1,0:T(8,128)(2,1)} %get-tuple-element.56) | copy-start | bytes 786436
  25.2 19.9 %copy-start.10 = (bf16[1024,128]{1,0:T(8,128)(2,1)S(1)}, bf16[1024,128]{1,0:T(8,128)(2,1)}, u32[]{:S(2)}) copy-start(bf16[1024,128]{1,0:T(8,128)(2,1)} %get-tuple-element.66) | copy-start | bytes 786436
  26.2 28.5 %collective-permute-start.4 = (bf16[192,2048]{1,0:T(8,128)(2,1)}, bf16[192,2048]{1,0:T(8,128)(2,1)S(1)}, u32[]{:S(2)}, u32[]{:S(2)}) collective-permute-start(bf16[192,2048]{1,0:T(8,128)(2,1)} %pad_maximum_fusion.1), channel_id=1, source_target_pairs={{16,0},{65,1},{24,8},{73,9},{0,16},{81,17},{8,24},{89,25},{48,32},... | collective-permute-start | bytes 2359304 | tf_op jit(solution)/shard_map/ppermute | solution.py:268
  26.2 28.5 %collective-permute-start.5 = (bf16[192,2048]{1,0:T(8,128)(2,1)}, bf16[192,2048]{1,0:T(8,128)(2,1)}, u32[]{:S(2)}, u32[]{:S(2)}) collective-permute-start(bf16[192,2048]{1,0:T(8,128)(2,1)} %pad_maximum_fusion.1), channel_id=1, source_target_pairs={{8,0},{33,1},{16,8},{41,9},{24,16},{49,17},{0,24},{57,25},{40,32},... | collective-permute-start | bytes 2359304 | tf_op jit(solution)/shard_map/ppermute | solution.py:268
  28.6 26.2 %collective-permute-start.6 = (bf16[192,2048]{1,0:T(8,128)(2,1)}, bf16[192,2048]{1,0:T(8,128)(2,1)S(1)}, u32[]{:S(2)}, u32[]{:S(2)}) collective-permute-start(bf16[192,2048]{1,0:T(8,128)(2,1)} %pad_maximum_fusion.1), channel_id=1, source_target_pairs={{24,0},{97,1},{0,8},{105,9},{8,16},{113,17},{16,24},{121,25},{56,3... | collective-permute-start | bytes 2359304 | tf_op jit(solution)/shard_map/ppermute | solution.py:268
  28.6 16.6 %collective-permute-start.7 = (bf16[1024,128]{1,0:T(8,128)(2,1)S(1)}, bf16[1024,128]{1,0:T(8,128)(2,1)S(1)}, u32[]{:S(2)}, u32[]{:S(2)}) collective-permute-start(bf16[1024,128]{1,0:T(8,128)(2,1)S(1)} %copy-done.11), channel_id=1, source_target_pairs={{32,0},{9,1},{40,8},{17,9},{48,16},{25,17},{56,24},{1,25},{64,32},... | collective-permute-start | bytes 786440 | tf_op jit(solution)/shard_map/ppermute | solution.py:268
  32.4 20.0 %collective-permute-start.8 = (bf16[1024,128]{1,0:T(8,128)(2,1)}, bf16[1024,128]{1,0:T(8,128)(2,1)S(1)}, u32[]{:S(2)}, u32[]{:S(2)}) collective-permute-start(bf16[1024,128]{1,0:T(8,128)(2,1)} %get-tuple-element.64), channel_id=1, source_target_pairs={{96,0},{25,1},{104,8},{1,9},{112,16},{9,17},{120,24},{17,25},{0,32... | collective-permute-start | bytes 786440 | tf_op jit(solution)/shard_map/ppermute | solution.py:268
  45.2 7.2 %copy-start.7 = (bf16[1024,128]{1,0:T(8,128)(2,1)}, bf16[1024,128]{1,0:T(8,128)(2,1)S(1)}, u32[]{:S(2)}) copy-start(bf16[1024,128]{1,0:T(8,128)(2,1)S(1)} %collective-permute-done.7.x1) | copy-start | bytes 786436
  45.2 9.6 %collective-permute-start.9 = (bf16[1024,128]{1,0:T(8,128)(2,1)S(1)}, bf16[1024,128]{1,0:T(8,128)(2,1)S(1)}, u32[]{:S(2)}, u32[]{:S(2)}) collective-permute-start(bf16[1024,128]{1,0:T(8,128)(2,1)S(1)} %copy-done.10), channel_id=1, source_target_pairs={{64,0},{17,1},{72,8},{25,9},{80,16},{1,17},{88,24},{9,25},{96,32},... | collective-permute-start | bytes 786440 | tf_op jit(solution)/shard_map/ppermute | solution.py:268
  52.4 2.4 %copy-start.8 = (bf16[1024,128]{1,0:T(8,128)(2,1)}, bf16[1024,128]{1,0:T(8,128)(2,1)S(1)}, u32[]{:S(2)}) copy-start(bf16[1024,128]{1,0:T(8,128)(2,1)S(1)} %collective-permute-done.8.x2) | copy-start | bytes 786436
  54.8 0.7 copy-start.9
  62.4 5.3 %collective-permute-start.10 = (bf16[1024,1024]{1,0:T(8,128)(2,1)}, bf16[1024,1024]{1,0:T(8,128)(2,1)S(1)}, u32[]{:S(2)}, u32[]{:S(2)}) collective-permute-start(bf16[1024,1024]{1,0:T(8,128)(2,1)} %norm.1.own_ref), channel_id=1, source_target_pairs={{0,1},{1,0},{2,3},{3,2},{4,5},{5,4},{6,7},{7,6},{8,9},{9,8},{10,11... | collective-permute-start | bytes 6291464 | tf_op jit(solution)/shard_map/ppermute | solution.py:272
  65.0 2.7 %copy-start = (bf16[1024,1024]{1,0:T(8,128)(2,1)S(1)}, bf16[1024,1024]{1,0:T(8,128)(2,1)}, u32[]{:S(2)}) copy-start(bf16[1024,1024]{1,0:T(8,128)(2,1)} %norm.1.own_ref) | copy-start | bytes 6291460
  65.0 19.6 %collective-permute-start.14 = (bf16[384,2048]{1,0:T(8,128)(2,1)S(1)}, bf16[384,2048]{1,0:T(8,128)(2,1)S(1)}, u32[]{:S(2)}, u32[]{:S(2)}) collective-permute-start(bf16[384,2048]{1,0:T(8,128)(2,1)S(1)} %pad_maximum_fusion.refs_0_), channel_id=1, source_target_pairs={{32,0},{9,1},{40,8},{17,9},{48,16},{25,17},{56,24},{1,25},{64,32},... | collective-permute-start | bytes 4718600 | tf_op jit(solution)/shard_map/ppermute | solution.py:268
  65.5 20.8 %collective-permute-start.15 = (bf16[384,2048]{1,0:T(8,128)(2,1)S(1)}, bf16[384,2048]{1,0:T(8,128)(2,1)S(1)}, u32[]{:S(2)}, u32[]{:S(2)}) collective-permute-start(bf16[384,2048]{1,0:T(8,128)(2,1)S(1)} %pad_maximum_fusion.refs_0_), channel_id=1, source_target_pairs={{96,0},{25,1},{104,8},{1,9},{112,16},{9,17},{120,24},{17,25},{0,32... | collective-permute-start | bytes 4718600 | tf_op jit(solution)/shard_map/ppermute | solution.py:268
  86.3 25.8 %collective-permute-start.19 = (bf16[384,2048]{1,0:T(8,128)(2,1)S(1)}, bf16[384,2048]{1,0:T(8,128)(2,1)S(1)}, u32[]{:S(2)}, u32[]{:S(2)}) collective-permute-start(bf16[384,2048]{1,0:T(8,128)(2,1)S(1)} %constant_dynamic-update-slice_fusion.refs_1_), channel_id=1, source_target_pairs={{32,0},{9,1},{40,8},{17,9},{48,16},{25,17},{56,24},{1,25},{64,32},... | collective-permute-start | bytes 4718600 | tf_op jit(solution)/shard_map/ppermute | solution.py:268
  86.3 25.8 %collective-permute-start.20 = (bf16[384,2048]{1,0:T(8,128)(2,1)S(1)}, bf16[384,2048]{1,0:T(8,128)(2,1)S(1)}, u32[]{:S(2)}, u32[]{:S(2)}) collective-permute-start(bf16[384,2048]{1,0:T(8,128)(2,1)S(1)} %constant_dynamic-update-slice_fusion.refs_1_), channel_id=1, source_target_pairs={{96,0},{25,1},{104,8},{1,9},{112,16},{9,17},{120,24},{17,25},{0,32... | collective-permute-start | bytes 4718600 | tf_op jit(solution)/shard_map/ppermute | solution.py:268
  87.8 7.5 %collective-permute-start.11 = (bf16[256,768]{1,0:T(8,128)(2,1)S(1)}, bf16[256,768]{1,0:T(8,128)(2,1)S(1)}, u32[]{:S(2)}, u32[]{:S(2)}) collective-permute-start(bf16[256,768]{1,0:T(8,128)(2,1)S(1)} %get-tuple-element.69), channel_id=1, source_target_pairs={{0,2},{1,7},{2,4},{3,1},{4,6},{5,3},{6,0},{7,5},{8,10},{9,15},{10,... | collective-permute-start | bytes 1179656 | tf_op jit(solution)/shard_map/ppermute | solution.py:280
  95.3 8.2 %collective-permute-start.12 = (bf16[256,768]{1,0:T(8,128)(2,1)S(1)}, bf16[256,768]{1,0:T(8,128)(2,1)S(1)}, u32[]{:S(2)}, u32[]{:S(2)}) collective-permute-start(bf16[256,768]{1,0:T(8,128)(2,1)S(1)} %add_convert_fusion.5), channel_id=1, source_target_pairs={{0,2},{1,7},{2,4},{3,1},{4,6},{5,3},{6,0},{7,5},{8,10},{9,15},{10,... | collective-permute-start | bytes 1179656 | tf_op jit(solution)/shard_map/ppermute | solution.py:280
  103.6 10.0 %collective-permute-start.13 = (bf16[256,768]{1,0:T(8,128)(2,1)S(1)}, bf16[256,768]{1,0:T(8,128)(2,1)S(1)}, u32[]{:S(2)}, u32[]{:S(2)}) collective-permute-start(bf16[256,768]{1,0:T(8,128)(2,1)S(1)} %add_convert_fusion.4), channel_id=1, source_target_pairs={{0,2},{1,7},{2,4},{3,1},{4,6},{5,3},{6,0},{7,5},{8,10},{9,15},{10,... | collective-permute-start | bytes 1179656 | tf_op jit(solution)/shard_map/ppermute | solution.py:280
  112.0 7.9 %collective-permute-start.16 = (bf16[256,768]{1,0:T(8,128)(2,1)S(1)}, bf16[256,768]{1,0:T(8,128)(2,1)S(1)}, u32[]{:S(2)}, u32[]{:S(2)}) collective-permute-start(bf16[256,768]{1,0:T(8,128)(2,1)S(1)} %get-tuple-element.75), channel_id=1, source_target_pairs={{0,2},{1,7},{2,4},{3,1},{4,6},{5,3},{6,0},{7,5},{8,10},{9,15},{10,... | collective-permute-start | bytes 1179656 | tf_op jit(solution)/shard_map/ppermute | solution.py:280
  112.1 26.1 %collective-permute-start.24 = (bf16[384,2048]{1,0:T(8,128)(2,1)S(1)}, bf16[384,2048]{1,0:T(8,128)(2,1)S(1)}, u32[]{:S(2)}, u32[]{:S(2)}) collective-permute-start(bf16[384,2048]{1,0:T(8,128)(2,1)S(1)} %collective-permute-done.14.refs_0_), channel_id=1, source_target_pairs={{32,0},{9,1},{40,8},{17,9},{48,16},{25,17},{56,24},{1,25},{64,32},... | collective-permute-start | bytes 4718600 | tf_op jit(solution)/shard_map/ppermute | solution.py:268
  113.4 25.5 %collective-permute-start.25 = (bf16[384,2048]{1,0:T(8,128)(2,1)S(1)}, bf16[384,2048]{1,0:T(8,128)(2,1)S(1)}, u32[]{:S(2)}, u32[]{:S(2)}) collective-permute-start(bf16[384,2048]{1,0:T(8,128)(2,1)S(1)} %collective-permute-done.20.refs_1_), channel_id=1, source_target_pairs={{96,0},{25,1},{104,8},{1,9},{112,16},{9,17},{120,24},{17,25},{0,32... | collective-permute-start | bytes 4718600 | tf_op jit(solution)/shard_map/ppermute | solution.py:268
  118.5 7.0 %collective-permute-start.21 = (bf16[256,768]{1,0:T(8,128)(2,1)S(1)}, bf16[256,768]{1,0:T(8,128)(2,1)S(1)}, u32[]{:S(2)}, u32[]{:S(2)}) collective-permute-start(bf16[256,768]{1,0:T(8,128)(2,1)S(1)} %get-tuple-element.81), channel_id=1, source_target_pairs={{0,2},{1,7},{2,4},{3,1},{4,6},{5,3},{6,0},{7,5},{8,10},{9,15},{10,... | collective-permute-start | bytes 1179656 | tf_op jit(solution)/shard_map/ppermute | solution.py:280
  120.0 9.7 %collective-permute-start.17 = (bf16[256,768]{1,0:T(8,128)(2,1)S(1)}, bf16[256,768]{1,0:T(8,128)(2,1)S(1)}, u32[]{:S(2)}, u32[]{:S(2)}) collective-permute-start(bf16[256,768]{1,0:T(8,128)(2,1)S(1)} %add_convert_fusion.3), channel_id=1, source_target_pairs={{0,2},{1,7},{2,4},{3,1},{4,6},{5,3},{6,0},{7,5},{8,10},{9,15},{10,... | collective-permute-start | bytes 1179656 | tf_op jit(solution)/shard_map/ppermute | solution.py:280
  125.6 8.3 %collective-permute-start.22 = (bf16[256,768]{1,0:T(8,128)(2,1)S(1)}, bf16[256,768]{1,0:T(8,128)(2,1)S(1)}, u32[]{:S(2)}, u32[]{:S(2)}) collective-permute-start(bf16[256,768]{1,0:T(8,128)(2,1)S(1)} %add_convert_fusion.1), channel_id=1, source_target_pairs={{0,2},{1,7},{2,4},{3,1},{4,6},{5,3},{6,0},{7,5},{8,10},{9,15},{10,... | collective-permute-start | bytes 1179656 | tf_op jit(solution)/shard_map/ppermute | solution.py:280
  129.8 8.3 %collective-permute-start.18 = (bf16[256,768]{1,0:T(8,128)(2,1)S(1)}, bf16[256,768]{1,0:T(8,128)(2,1)S(1)}, u32[]{:S(2)}, u32[]{:S(2)}) collective-permute-start(bf16[256,768]{1,0:T(8,128)(2,1)S(1)} %add_convert_fusion.2), channel_id=1, source_target_pairs={{0,2},{1,7},{2,4},{3,1},{4,6},{5,3},{6,0},{7,5},{8,10},{9,15},{10,... | collective-permute-start | bytes 1179656 | tf_op jit(solution)/shard_map/ppermute | solution.py:280
  134.8 21.9 %collective-permute-start.23 = (bf16[256,768]{1,0:T(8,128)(2,1)}, bf16[256,768]{1,0:T(8,128)(2,1)}, u32[]{:S(2)}, u32[]{:S(2)}) collective-permute-start(bf16[256,768]{1,0:T(8,128)(2,1)} %add_convert_fusion), channel_id=1, source_target_pairs={{0,2},{1,7},{2,4},{3,1},{4,6},{5,3},{6,0},{7,5},{8,10},{9,15},{10,... | collective-permute-start | bytes 1179656 | tf_op jit(solution)/shard_map/ppermute | solution.py:280
  138.2 0.7 copy-start.5
  144.5 11.5 %copy-start.6 = (bf16[256,768]{1,0:T(8,128)(2,1)S(1)}, bf16[256,768]{1,0:T(8,128)(2,1)}, u32[]{:S(2)}) copy-start(bf16[256,768]{1,0:T(8,128)(2,1)} %copy-done.5) | copy-start | bytes 1179652
  144.5 16.9 %collective-permute-start.28 = (bf16[256,768]{1,0:T(8,128)(2,1)}, bf16[256,768]{1,0:T(8,128)(2,1)}, u32[]{:S(2)}, u32[]{:S(2)}) collective-permute-start(bf16[256,768]{1,0:T(8,128)(2,1)} %get-tuple-element.90), channel_id=1, source_target_pairs={{0,6},{1,3},{2,0},{3,5},{4,2},{5,7},{6,4},{7,1},{8,14},{9,11},{10,... | collective-permute-start | bytes 1179656 | tf_op jit(solution)/shard_map/ppermute | solution.py:280
  145.9 16.1 %collective-permute-start.27 = (bf16[256,768]{1,0:T(8,128)(2,1)}, bf16[256,768]{1,0:T(8,128)(2,1)}, u32[]{:S(2)}, u32[]{:S(2)}) collective-permute-start(bf16[256,768]{1,0:T(8,128)(2,1)} %get-tuple-element.89), channel_id=1, source_target_pairs={{0,2},{1,7},{2,4},{3,1},{4,6},{5,3},{6,0},{7,5},{8,10},{9,15},{10,... | collective-permute-start | bytes 1179656 | tf_op jit(solution)/shard_map/ppermute | solution.py:280
  147.2 14.8 %collective-permute-start.26 = (bf16[256,768]{1,0:T(8,128)(2,1)}, bf16[256,768]{1,0:T(8,128)(2,1)}, u32[]{:S(2)}, u32[]{:S(2)}) collective-permute-start(bf16[256,768]{1,0:T(8,128)(2,1)} %get-tuple-element.88), channel_id=1, source_target_pairs={{0,4},{1,5},{2,6},{3,7},{4,0},{5,1},{6,2},{7,3},{8,12},{9,13},{10,... | collective-permute-start | bytes 1179656 | tf_op jit(solution)/shard_map/ppermute | solution.py:280
  148.7 22.5 %collective-permute-start.29 = (bf16[128,768]{1,0:T(8,128)(2,1)}, bf16[128,768]{1,0:T(8,128)(2,1)}, u32[]{:S(2)}, u32[]{:S(2)}) collective-permute-start(bf16[128,768]{1,0:T(8,128)(2,1)} %get-tuple-element.97), channel_id=1, source_target_pairs={{0,1},{1,0},{2,3},{3,2},{4,5},{5,4},{6,7},{7,6},{8,9},{9,8},{10,11... | collective-permute-start | bytes 589832 | tf_op jit(solution)/shard_map/ppermute | solution.py:272
  156.7 15.6 %copy-start.1 = (bf16[128,6144]{1,0:T(8,128)(2,1)S(1)}, bf16[128,6144]{1,0:T(8,128)(2,1)}, u32[]{:S(2)}) copy-start(bf16[128,6144]{1,0:T(8,128)(2,1)} %res_ref.1) | copy-start | bytes 4718596
  156.7 14.4 %collective-permute-start.30 = (bf16[128,768]{1,0:T(8,128)(2,1)}, bf16[128,768]{1,0:T(8,128)(2,1)}, u32[]{:S(2)}, u32[]{:S(2)}) collective-permute-start(bf16[128,768]{1,0:T(8,128)(2,1)} %get-tuple-element.95), channel_id=1, source_target_pairs={{0,1},{1,0},{2,3},{3,2},{4,5},{5,4},{6,7},{7,6},{8,9},{9,8},{10,11... | collective-permute-start | bytes 589832 | tf_op jit(solution)/shard_map/ppermute | solution.py:272
  161.4 9.7 %collective-permute-start.31 = (bf16[128,768]{1,0:T(8,128)(2,1)}, bf16[128,768]{1,0:T(8,128)(2,1)}, u32[]{:S(2)}, u32[]{:S(2)}) collective-permute-start(bf16[128,768]{1,0:T(8,128)(2,1)} %get-tuple-element.93), channel_id=1, source_target_pairs={{0,1},{1,0},{2,3},{3,2},{4,5},{5,4},{6,7},{7,6},{8,9},{9,8},{10,11... | collective-permute-start | bytes 589832 | tf_op jit(solution)/shard_map/ppermute | solution.py:272
  164.2 8.1 %collective-permute-start.32 = (bf16[128,768]{1,0:T(8,128)(2,1)}, bf16[128,768]{1,0:T(8,128)(2,1)S(1)}, u32[]{:S(2)}, u32[]{:S(2)}) collective-permute-start(bf16[128,768]{1,0:T(8,128)(2,1)} %get-tuple-element.91), channel_id=1, source_target_pairs={{0,1},{1,0},{2,3},{3,2},{4,5},{5,4},{6,7},{7,6},{8,9},{9,8},{10,11... | collective-permute-start | bytes 589832 | tf_op jit(solution)/shard_map/ppermute | solution.py:272

commit v3 on v2

--- a/solution.py
+++ b/solution.py
@@ -32,8 +32,11 @@
     k_act = silu(k_ref[...])
     kact_ref[...] = k_act
     both = contract(k_act, v_ref[...], ((0,), (0,))).astype(BF16)
-    state_ref[:DH, :] = both[:DH, :DH]
-    state_ref[DH:, :] = both[DH:, DH:]
+    for head in range(2):
+        square = both[head * DH : (head + 1) * DH, head * DH : (head + 1) * DH]
+        for part in range(2):
+            column = (2 * head + part) * DH
+            state_ref[:, column : column + DH] = square[part * 64 : (part + 1) * 64]
 
 
 def span_state(key_in, value):
@@ -43,10 +46,10 @@
         state_body,
         grid=(width // (2 * DH),),
         in_specs=[column, column],
-        out_specs=[column, pl.BlockSpec((2 * DH, DH), lambda h: (h, 0))],
+        out_specs=[column, pl.BlockSpec((64, 4 * DH), lambda h: (0, h))],
         out_shape=[
             jax.ShapeDtypeStruct((tokens, width), BF16),
-            jax.ShapeDtypeStruct((width, DH), BF16),
+            jax.ShapeDtypeStruct((64, 2 * width), BF16),
         ],
         name="span_state",
     )(key_in, value)
@@ -106,11 +109,13 @@
 
 
 def messages(table, state, pieces):
-    whole = pl.BlockSpec(state.shape, lambda g, t: (0, 0))
+    rows, columns = state.shape
+    own = pl.BlockSpec((rows, columns // 2), lambda g, t: (0, g))
+    last = pl.BlockSpec((rows, columns // 2), lambda g, t: (0, g))
     return pl.pallas_call(
         message_body,
         grid_spec=pltpu.PrefetchScalarGridSpec(
-            num_scalar_prefetch=1, grid=(1,), in_specs=[whole] * 4, out_specs=[whole] * 3
+            num_scalar_prefetch=1, grid=(2,), in_specs=[own] + [last] * 3, out_specs=[own] * 3
         ),
         out_shape=[jax.ShapeDtypeStruct(state.shape, BF16)] * 3,
         name="messages",
@@ -118,71 +123,66 @@
 
 
 def norm_body(
-    tab_ref, qa_ref, la_ref, qb_ref, lb_ref, gain_ref, z1, z2, z3, x1, x2, x3, out_ref
+    tab_ref, q_ref, local_ref, gain_ref, z1, z2, z3, x1, x2, x3, out_ref
 ):
-    def part(q_ref, local_ref):
-        prefix = x1[...].astype(F32) + x2[...].astype(F32) + x3[...].astype(F32)
-        for index, piece in enumerate((z1, z2, z3)):
-            prefix = prefix + jnp.where(tab_ref[8 + index] > 0, piece[...].astype(F32), 0.0)
-        prefix = prefix.astype(BF16)
-        zero = jnp.zeros((DH, DH), BF16)
-        prefix = jnp.concatenate(
-            [
-                jnp.concatenate([prefix[:DH], zero], axis=1),
-                jnp.concatenate([zero, prefix[DH:]], axis=1),
-            ],
-            axis=0,
-        )
-        head = lax.broadcasted_iota(jnp.int32, (2 * DH, 2 * DH), 0) // DH
-        other = lax.broadcasted_iota(jnp.int32, (2 * DH, 2 * DH), 1) // DH
-        average = jnp.where(head == other, 1.0 / DH, 0.0).astype(BF16)
-        gain = gain_ref[...]
-        for place in range(8):
-            source = pl.ds(pl.multiple_of(tab_ref[place] * 128, 128), 128)
-            attended = local_ref[source, :] + contract(q_ref[source, :], prefix, ((1,), (0,)))
-            meansq = contract((attended * attended).astype(BF16), average, ((1,), (0,)))
-            normed = (attended * lax.rsqrt(meansq + 1e-06) * gain).astype(BF16)
-            out_ref[place * 128 : (place + 1) * 128, :] = normed
-
-    early = pl.program_id(0) < pl.num_programs(0) // 2
-    pl.when(early)(lambda: part(qa_ref, la_ref))
-    pl.when(jnp.logical_not(early))(lambda: part(qb_ref, lb_ref))
-
-
-def norm(table, halves, gain, z_pieces, x_pieces):
-    (qa, la), (qb, lb) = halves
-    tokens, width = qa.shape[0], qa.shape[1] * 2
-    steps = width // (2 * DH)
-    first = pl.BlockSpec((tokens, 2 * DH), lambda h, t: (0, jnp.minimum(h, steps // 2 - 1)))
-    second = pl.BlockSpec((tokens, 2 * DH), lambda h, t: (0, jnp.maximum(h - steps // 2, 0)))
+    prefix = x1[...].astype(F32) + x2[...].astype(F32) + x3[...].astype(F32)
+    for index, piece in enumerate((z1, z2, z3)):
+        prefix = prefix + jnp.where(tab_ref[8 + index] > 0, piece[...].astype(F32), 0.0)
+    prefix = prefix.astype(BF16)
+    zero = jnp.zeros((64, DH), BF16)
+    strips = [prefix[:, index * DH : (index + 1) * DH] for index in range(4)]
+    prefix = jnp.concatenate(
+        [jnp.concatenate([strip, zero], axis=1) for strip in strips[:2]]
+        + [jnp.concatenate([zero, strip], axis=1) for strip in strips[2:]],
+        axis=0,
+    )
+    head = lax.broadcasted_iota(jnp.int32, (2 * DH, 2 * DH), 0) // DH
+    other = lax.broadcasted_iota(jnp.int32, (2 * DH, 2 * DH), 1) // DH
+    average = jnp.where(head == other, 1.0 / DH, 0.0).astype(BF16)
+    gain = gain_ref[...]
+    for place in range(8):
+        source = pl.ds(pl.multiple_of(tab_ref[place] * 128, 128), 128)
+        attended = local_ref[source, :] + contract(q_ref[source, :], prefix, ((1,), (0,)))
+        meansq = contract((attended * attended).astype(BF16), average, ((1,), (0,)))
+        normed = (attended * lax.rsqrt(meansq + 1e-06) * gain).astype(BF16)
+        out_ref[place * 128 : (place + 1) * 128, :] = normed
+
+
+def norm(table, half, first, gain, z_pieces, x_pieces):
+    tokens, width = half[0].shape
+    skip = first * DH // (2 * DH)
     pair = pl.BlockSpec((tokens, 2 * DH), lambda h, t: (0, h))
-    square = pl.BlockSpec((2 * DH, DH), lambda h, t: (h, 0))
+    last = pl.BlockSpec((64, 4 * DH), lambda h, t: (0, h + skip))
+    square = pl.BlockSpec((64, 4 * DH), lambda h, t: (0, h + skip))
     return pl.pallas_call(
         norm_body,
         grid_spec=pltpu.PrefetchScalarGridSpec(
             num_scalar_prefetch=1,
-            grid=(steps,),
-            in_specs=[first, first, second, second, pl.BlockSpec((1, 2 * DH), lambda h, t: (0, h))]
-            + [square] * 6,
+            grid=(width // (2 * DH),),
+            in_specs=[pair, pair, pl.BlockSpec((1, 2 * DH), lambda h, t: (0, h + skip))]
+            + [last] * 3
+            + [square] * 3,
             out_specs=pair,
         ),
         out_shape=jax.ShapeDtypeStruct((tokens, width), BF16),
         name="norm",
-    )(table, qa, la, qb, lb, gain, *z_pieces, *x_pieces)
-
-
-def project_body(counts, core_ref, own_ref, other_ref, *refs):
-    weights, outs = refs[: len(counts)], refs[len(counts) :]
+    )(table, *half, gain, *z_pieces, *x_pieces)
+
+
+def project_body(counts, core_ref, *refs):
+    tokens, weights, outs = refs[:4], refs[4 : 4 + len(counts)], refs[4 + len(counts) :]
     step = pl.program_id(0)
-    depth, rows = own_ref.shape[1], outs[0].shape[0]
+    depth, rows = tokens[0].shape[1], outs[0].shape[0]
     first_core = core_ref[0] == 0
     first = 0
     for w_ref, count in zip(weights, counts):
 
         @pl.when((step >= first) & (step < first + count))
         def _(w_ref=w_ref):
-            total = contract(own_ref[...], w_ref[:, :depth], ((1,), (1,)))
-            total = total + contract(other_ref[...], w_ref[:, depth:], ((1,), (1,)))
+            total = 0.0
+            for index, t_ref in enumerate(tokens):
+                columns = slice(index * depth, (index + 1) * depth)
+                total = total + contract(t_ref[...], w_ref[:, columns], ((1,), (1,)))
             far, right, left, own = (
                 total[index * rows : (index + 1) * rows].astype(BF16) for index in range(4)
             )
@@ -195,15 +195,15 @@
         first += count
 
 
-def project(core, own, other, weights, tile):
-    rows, depth = own.shape
+def project(core, tokens, weights, tile):
+    rows, depth = tokens[0].shape
     counts = tuple(w.shape[0] // tile for w in weights)
     columns = tile * sum(counts)
     specs, first = [], 0
     for count in counts:
         specs.append(
             pl.BlockSpec(
-                (tile, 2 * depth),
+                (tile, 4 * depth),
                 lambda g, t, first=first, count=count: (jnp.clip(g - first, 0, count - 1), 0),
             )
         )
@@ -214,13 +214,13 @@
         grid_spec=pltpu.PrefetchScalarGridSpec(
             num_scalar_prefetch=1,
             grid=(sum(counts),),
-            in_specs=[whole, whole] + specs,
+            in_specs=[whole] * 4 + specs,
             out_specs=[pl.BlockSpec((rows // 4, tile), lambda g, t: (0, g))] * 4,
         ),
         out_shape=[jax.ShapeDtypeStruct((rows // 4, columns), BF16)] * 4,
         compiler_params=pltpu.CompilerParams(vmem_limit_bytes=40 * 1024 * 1024),
         name="project",
-    )(core, own, other, *weights)
+    )(core, *tokens, *weights)
 
 
 def finish_body(layout, tab_ref, res_ref, *refs):
@@ -284,16 +284,6 @@
     return (left.astype(F32) + right.astype(F32)).astype(BF16)
 
 
-def reduce_ring(parts):
-    behind, far, ahead, own = parts
-    return own, push(add(push(add(push(behind, 1), far), 1), ahead), 1)
-
-
-def reduce_direct(parts):
-    behind, far, ahead, own = parts
-    return own, push(far, 2), push(ahead, 1), push(behind, 3)
-
-
 def settle_chunk(parts, c):
     def rows(which):
         total = 0.0
@@ -317,46 +307,65 @@
     keep = lax.dynamic_slice_in_dim(turned, c * half, half)
     give = lax.dynamic_slice_in_dim(turned, (1 - c) * half, half)
     k_act, state = span_state(after(key_in, keep, give), value)
+    base = jnp.concatenate([keep, after(swap(give), state)], axis=1)
     level1 = [fetch_mixed(state, 1, offset) for offset in REL[1:]]
-    base = jnp.concatenate([keep, after(swap(give), state)], axis=1)
-    near_plus, near_minus = fetch_mixed(base, 1, 1), fetch_mixed(base, 1, 3)
-
-    heads = query.shape[1] // DH // 2
+    plus, minus = fetch_mixed(base, 1, 1), fetch_mixed(base, 1, 3)
+
+    width = query.shape[1] // 2
+    heads = width // DH
     early = local_attention(query, k_act, value, 0, heads)
-    level1 = [after(piece, early[0]) for piece in level1]
+    level1 = [after(piece, early[0], plus, minus) for piece in level1]
     sent = messages(table, state, level1)
     level2 = [fetch_mixed(piece, 2, offset) for piece, offset in zip(sent, REL[1:])]
-    far_weights = fetch_mixed(after(base, sent[0]), 1, 2)
+    far = fetch_mixed(after(base, sent[0]), 1, 2)
     late = local_attention(after(query, sent[0]), k_act, value, heads, heads)
     level2 = [after(piece, late[0]) for piece in level2]
-
-    g0a = jnp.concatenate([base, near_plus], axis=0)
-    ready = after(g0a, *level2)
-    g1a, g3a = fetch_mixed(ready, 2, 1), fetch_mixed(ready, 2, 3)
-    table = after(table, far_weights, near_plus, near_minus)
-    normed = norm(table, (early, late), head_gain.reshape(1, -1), level1, level2)
-    other = swap(normed)
-    g0b = jnp.concatenate([near_minus, far_weights], axis=0)
+    g0a = jnp.concatenate([base, plus], axis=0)
+    g0a = after(g0a, *level2)
+    g1a, g3a = fetch_mixed(g0a, 2, 1), fetch_mixed(g0a, 2, 3)
+    g0b = jnp.concatenate([minus, far], axis=0)
+
+    gain = head_gain.reshape(1, -1)
+    table = after(table, far)
+    norm_a = norm(table, early, 0, gain, level1, level2)
+    swap_a = swap(norm_a)
+    norm_b = norm(after(table, norm_a), late, heads, gain, level1, level2)
+    swap_b = swap(norm_b)
     core = c.astype(jnp.int32).reshape(1)
-    first = project(core, normed, other, [g0a, g0b], 384)
-    ready = after(g0b, g1a, g3a, first[0])
+    ready = after(g0b, g1a, g3a)
     g1b, g3b = fetch_mixed(ready, 2, 1), fetch_mixed(ready, 2, 3)
-    first = reduce_ring(first)
-    second = project(core, after(normed, first[0]), other, [g1a, g3a], 384)
+
+    def columns(weights, *others):
+        return project(core, [after(norm_a, *others), norm_b, swap_a, swap_b], weights, 384)
+
+    first = columns([g1a, g3a], norm_b)
+    second = columns([g0a, g0b], first[0])
+    first1 = push(first[0], 1)
+    second1 = push(after(second[0], first1), 1)
+    first2 = push(after(add(first1, first[1]), second[0]), 1)
     g2 = [
-        fetch_mixed(after(g1a, g1b, g3b, second[0]), 2, 1),
-        fetch_mixed(after(g3b, g1b, second[0]), 2, 3),
+        fetch_mixed(after(g1a, g1b, g3b, second[0], first1), 2, 1),
+        fetch_mixed(after(g3b, g1b, second[0], first1), 2, 3),
     ]
-    second = reduce_ring(second)
-    third = project(core, after(normed, second[0], *first), other, [g1b, g3b], 384)
-    third = reduce_ring(third)
-    fourth = project(core, after(normed, third[0], *second), other, g2, 384)
-    fourth = reduce_direct(fourth)
-    settled = [settle_chunk(parts, c) for parts in (first, second, third, fourth)]
+    second2 = push(add(second1, second[1]), 1)
+    third = columns([g1b, g3b], second[0], first1)
+    third1 = push(after(third[0], first2), 1)
+    first3 = push(add(first2, first[2]), 1)
+    second3 = push(add(second2, second[2]), 1)
+    third2 = push(add(third1, third[1]), 1)
+    third3 = push(add(third2, third[2]), 1)
+    fourth = columns(g2, third[0], first2, second2)
+    chunks = (
+        (first[3], first3),
+        (second[3], second3),
+        (third[3], third3),
+        (fourth[3], push(fourth[1], 2), push(fourth[2], 1), push(fourth[0], 3)),
+    )
+    settled = [settle_chunk(parts, c) for parts in chunks]
     spot = (
-        ((0, 0), (0, 1), (0, 2), (0, 3)),
-        ((1, 0), (1, 1), (2, 0), (2, 1)),
-        ((1, 2), (1, 3), (2, 2), (2, 3)),
+        ((1, 0), (1, 1), (1, 2), (1, 3)),
+        ((0, 0), (0, 1), (2, 0), (2, 1)),
+        ((0, 2), (0, 3), (2, 2), (2, 3)),
         ((3, 0), (3, 1), (3, 2), (3, 3)),
     )
     layout, shards = [], []

time: 176 us -> 168 us (0.955)
  waiting for transfers between devices: 52.8 us -> 36.1 us
  starting transfers between devices: 57.9 us -> 63.5 us
  Pallas kernels: 49.6 us -> 52.8 us
    ppermute x12, waiting for transfers between devices: 20.1 us -> 8.19 us  [push(): return lax.ppermute(array, ('y', 'c'), pairs)]
    ppermute x15, starting transfers between devices: 16.4 us -> 21.7 us  [fetch_mixed(): return lax.ppermute(array, ('x', 'z', 'c'), pairs)]
    ppermute x15, waiting for transfers between devices: 30.5 us -> 26.6 us  [fetch_mixed(): return lax.ppermute(array, ('x', 'z', 'c'), pairs)]
    pallas_call x4, Pallas kernels: 20.3 us -> 22.2 us  [project(): pl.pallas_call(functools.partial(project_body, counts), grid_spec=pltpu.P...]
    pallas_call x1 -> x2, Pallas kernels: 6.96 us -> 8.47 us  [norm(): pl.pallas_call(norm_body, grid_spec=pltpu.PrefetchScalarGridSpec(num_scal...]
    ppermute x6 -> x7, starting transfers between devices: 19.1 us -> 18.8 us  [swap(): return lax.ppermute(array, 'c', [(0, 1), (1, 0)])]
  transfers between devices with their start and end apart: 33 -> 34, of which waited for: 14 -> 14; matrix products, arithmetic and copies ran while one was open for 5% -> 6% of each run, Pallas kernels for 23% -> 28%
where the time goes in v3:
time: 168 us
  starting transfers between devices  63.5 us (38%)
  Pallas kernels  52.8 us (31%)
  waiting for transfers between devices  36.1 us (21%)
  other arithmetic  8.59 us (5%)
  local copies, waits for them, and re-layouts  6.26 us (4%)
    ppermute x15, waiting for transfers between devices, fetch_mixed(): return lax.ppermute(array, ('x', 'z', 'c'), pairs)  26.6 us
    ppermute x12, starting transfers between devices, push(): return lax.ppermute(array, ('y', 'c'), pairs)  23 us
    pallas_call x4, Pallas kernels, project(): pl.pallas_call(functools.partial(project_body, counts), grid_spec=pltpu.P...  22.2 us
    ppermute x15, starting transfers between devices, fetch_mixed(): return lax.ppermute(array, ('x', 'z', 'c'), pairs)  21.7 us
    ppermute x7, starting transfers between devices, swap(): return lax.ppermute(array, 'c', [(0, 1), (1, 0)])  18.8 us
    pallas_call x2, Pallas kernels, local_attention(): pl.pallas_call(local_body, grid=(heads,), in_specs=[source, source, sourc...  11.4 us
    pallas_call x2, Pallas kernels, norm(): pl.pallas_call(norm_body, grid_spec=pltpu.PrefetchScalarGridSpec(num_scal...  8.47 us
    ppermute x12, waiting for transfers between devices, push(): return lax.ppermute(array, ('y', 'c'), pairs)  8.19 us
  transfers between devices with their start and end apart: 34, of which 14 were waited for; matrix products, arithmetic and copies ran while one was open for 6% of the time, Pallas kernels for 28%

profile of v3, /device:TPU:1, one launch (start us, length us, event | category | flops | bytes accessed | tf_op | source)
XLA Modules:
  0.0 167.5 jit_solution(7107275799993366676)
XLA Ops:
  0.0 1.7 %constant_dynamic-slice_fusion.1 = (bf16[1024,192]{1,0:T(8,128)(2,1)S(1)}, bf16[1024,192]{1,0:T(8,128)(2,1)S(1)}) fusion(bf16[1024,384]{1,0:T(8,128)(2,1)} %param.10, s32[]{:T(128)S(6)} %select_n.187, s32[]{:T(128)S(6)} %select_n.188), kind=kLoop, calls=%fused_computation.19 | loop fusion | bytes 1572872 | tf_op jit(solution)/shard_map/dynamic-slice
  1.9 1.5 collective-permute-start
  3.6 4.7 %span_state.1 = (bf16[1024,1024]{1,0:T(8,128)(2,1)}, bf16[64,2048]{1,0:T(8,128)(2,1)}) custom-call(bf16[1024,1024]{1,0:T(8,128)(2,1)} %k_ref, bf16[1024,1024]{1,0:T(8,128)(2,1)} %v_ref.5), custom_call_target="tpu_custom_call" | custom-call | tf_op jit(solution)/shard_map/span_state/pallas_call | solution.py:45
  9.3 1.3 collective-permute-start.3
  10.6 1.4 collective-permute-start.2
  12.0 1.6 collective-permute-start.5
  13.9 2.4 %collective-permute-start.1 = (bf16[64,2048]{1,0:T(8,128)(2,1)S(1)}, bf16[64,2048]{1,0:T(8,128)(2,1)S(1)}, u32[]{:S(2)}, u32[]{:S(2)}) collective-permute-start(bf16[64,2048]{1,0:T(8,128)(2,1)S(1)} %copy-done.16), channel_id=1, source_target_pairs={{8,0},{33,1},{16,8},{41,9},{24,16},{49,17},{0,24},{57,25},{40,32},... | collective-permute-start | bytes 786440 | tf_op jit(solution)/shard_map/ppermute | solution.py:268
  16.3 5.7 %local_attention.2 = (bf16[1024,512]{1,0:T(8,128)(2,1)}, f32[1024,512]{1,0:T(8,128)}) custom-call(bf16[1024,1024]{1,0:T(8,128)(2,1)} %q_ref.2, bf16[1024,1024]{1,0:T(8,128)(2,1)} %get-tuple-element.56.kact_ref, bf16[1024,1024]{1,0:T(8,128)(2,1)} %v_ref.5), custom_call_target="tpu_custom_call" | custom-call | tf_op jit(solution)/shard_map/local_attention/pallas_call | solution.py:84
  22.6 3.2 %collective-permute-done.5.z3 = bf16[64,2048]{1,0:T(8,128)(2,1)S(1)} collective-permute-done((bf16[64,2048]{1,0:T(8,128)(2,1)S(1)}, bf16[64,2048]{1,0:T(8,128)(2,1)S(1)}, u32[]{:S(2)}, u32[]{:S(2)}) %collective-permute-start.5) | collective-permute-done | bytes 262176 | tf_op jit(solution)/shard_map/ppermute | solution.py:268
  25.8 1.7 %collective-permute-done.4.z2 = bf16[64,2048]{1,0:T(8,128)(2,1)S(1)} collective-permute-done((bf16[64,2048]{1,0:T(8,128)(2,1)S(1)}, bf16[64,2048]{1,0:T(8,128)(2,1)S(1)}, u32[]{:S(2)}, u32[]{:S(2)}) %collective-permute-start.4) | collective-permute-done | bytes 262176 | tf_op jit(solution)/shard_map/ppermute | solution.py:268
  28.9 2.9 %messages.1 = (bf16[64,2048]{1,0:T(8,128)(2,1)}, bf16[64,2048]{1,0:T(8,128)(2,1)}, bf16[64,2048]{1,0:T(8,128)(2,1)}) custom-call(s32[15]{0:T(128)} %stack.156.tab_ref, bf16[64,2048]{1,0:T(8,128)(2,1)} %get-tuple-element.54.state_ref, bf16[64,2048]{1,0:T(8,128)(2,1)} %copy-done.8, bf16[64,2048]{1,0:T(8,128)(2,1)} %copy-done.7, bf16[64,2048]{1,0:T(8,128)(2,1)} %copy-done.6), custom_call_target="tpu_custom_call" | custom-call | tf_op jit(solution)/shard_map/messages/pallas_call | solution.py:115
  31.9 3.8 %collective-permute-start.7 = (bf16[64,2048]{1,0:T(8,128)(2,1)}, bf16[64,2048]{1,0:T(8,128)(2,1)S(1)}, u32[]{:S(2)}, u32[]{:S(2)}) collective-permute-start(bf16[64,2048]{1,0:T(8,128)(2,1)} %get-tuple-element.61), channel_id=1, source_target_pairs={{32,0},{9,1},{40,8},{17,9},{48,16},{25,17},{56,24},{1,25},{64,32},... | collective-permute-start | bytes 786440 | tf_op jit(solution)/shard_map/ppermute | solution.py:268
  35.7 1.2 collective-permute-start.9
  37.0 5.7 %local_attention.3 = (bf16[1024,512]{1,0:T(8,128)(2,1)}, f32[1024,512]{1,0:T(8,128)}) custom-call(bf16[1024,1024]{1,0:T(8,128)(2,1)} %q_ref.2, bf16[1024,1024]{1,0:T(8,128)(2,1)} %get-tuple-element.56.kact_ref, bf16[1024,1024]{1,0:T(8,128)(2,1)} %v_ref.5), custom_call_target="tpu_custom_call" | custom-call | tf_op jit(solution)/shard_map/local_attention/pallas_call | solution.py:84
  42.7 1.2 pad_maximum_fusion.refs_4_
  44.1 1.4 collective-permute-done.8.x2
  46.1 2.1 %collective-permute-start.12 = (bf16[384,2048]{1,0:T(8,128)(2,1)S(1)}, bf16[384,2048]{1,0:T(8,128)(2,1)}, u32[]{:S(2)}, u32[]{:S(2)}) collective-permute-start(bf16[384,2048]{1,0:T(8,128)(2,1)S(1)} %pad_maximum_fusion.refs_4_), channel_id=1, source_target_pairs={{32,0},{9,1},{40,8},{17,9},{48,16},{25,17},{56,24},{1,25},{64,32},... | collective-permute-start | bytes 4718600 | tf_op jit(solution)/shard_map/ppermute | solution.py:268
  48.2 1.5 collective-permute-start.6
  49.7 20.0 %collective-permute-done.6 = bf16[192,2048]{1,0:T(8,128)(2,1)} collective-permute-done((bf16[192,2048]{1,0:T(8,128)(2,1)}, bf16[192,2048]{1,0:T(8,128)(2,1)}, u32[]{:S(2)}, u32[]{:S(2)}) %collective-permute-start.6) | collective-permute-done | bytes 786464 | tf_op jit(solution)/shard_map/ppermute | solution.py:268
  69.7 4.2 %norm.2.refs_0_ = bf16[1024,512]{1,0:T(8,128)(2,1)} custom-call(s32[15]{0:T(128)} %stack.156.tab_ref, bf16[1024,512]{1,0:T(8,128)(2,1)} %get-tuple-element.57.q_ref, f32[1024,512]{1,0:T(8,128)} %get-tuple-element.64.local_ref, f32[1,1024]{1,0:T(1,128)} %bitcast.37, bf16[64,2048]{1,0:T(8,128)(2,1)} %copy-done.8, bf16[64,2048]{1,0:T(8,128)(2,1)} %copy-done.7, ...), custom_call_target="tpu_custom_call" | custom-call | tf_op jit(solution)/shard_map/norm/pallas_call | solution.py:157
  73.8 3.0 %collective-permute-start.10 = (bf16[1024,512]{1,0:T(8,128)(2,1)}, bf16[1024,512]{1,0:T(8,128)(2,1)S(1)}, u32[]{:S(2)}, u32[]{:S(2)}) collective-permute-start(bf16[1024,512]{1,0:T(8,128)(2,1)} %norm.2.refs_0_), channel_id=1, source_target_pairs={{0,1},{1,0},{2,3},{3,2},{4,5},{5,4},{6,7},{7,6},{8,9},{9,8},{10,11... | collective-permute-start | bytes 3145736 | tf_op jit(solution)/shard_map/ppermute | solution.py:272
  76.8 4.3 %norm.3.refs_1_ = bf16[1024,512]{1,0:T(8,128)(2,1)} custom-call(s32[15]{0:T(128)} %stack.156.tab_ref, bf16[1024,512]{1,0:T(8,128)(2,1)} %get-tuple-element.66.q_ref, f32[1024,512]{1,0:T(8,128)} %get-tuple-element.73.local_ref, f32[1,1024]{1,0:T(1,128)} %bitcast.38, bf16[64,2048]{1,0:T(8,128)(2,1)} %copy-done.8, bf16[64,2048]{1,0:T(8,128)(2,1)} %copy-done.7, ...), custom_call_target="tpu_custom_call" | custom-call | tf_op jit(solution)/shard_map/norm/pallas_call | solution.py:157
  81.2 1.3 constant_dynamic-update-slice_fusion.refs_5_
  83.5 1.9 %collective-permute-start.20 = (bf16[384,2048]{1,0:T(8,128)(2,1)S(1)}, bf16[384,2048]{1,0:T(8,128)(2,1)S(1)}, u32[]{:S(2)}, u32[]{:S(2)}) collective-permute-start(bf16[384,2048]{1,0:T(8,128)(2,1)S(1)} %constant_dynamic-update-slice_fusion.refs_5_), channel_id=1, source_target_pairs={{32,0},{9,1},{40,8},{17,9},{48,16},{25,17},{56,24},{1,25},{64,32},... | collective-permute-start | bytes 4718600 | tf_op jit(solution)/shard_map/ppermute | solution.py:268
  85.4 6.8 %project.4 = (bf16[256,768]{1,0:T(8,128)(2,1)S(1)}, bf16[256,768]{1,0:T(8,128)(2,1)S(1)}, bf16[256,768]{1,0:T(8,128)(2,1)S(1)}, bf16[256,768]{1,0:T(8,128)(2,1)S(1)}) custom-call(s32[1]{0:T(128)} %bitcast.16.core_ref, bf16[1024,512]{1,0:T(8,128)(2,1)S(1)} %copy-done, bf16[1024,512]{1,0:T(8,128)(2,1)S(1)} %copy-done.1, ...), custom_call_target="tpu_custom_call" | custom-call | tf_op jit(solution)/shard_map/project/pallas_call | solution.py:212
  92.2 2.8 %collective-permute-start.14 = (bf16[256,768]{1,0:T(8,128)(2,1)S(1)}, bf16[256,768]{1,0:T(8,128)(2,1)S(1)}, u32[]{:S(2)}, u32[]{:S(2)}) collective-permute-start(bf16[256,768]{1,0:T(8,128)(2,1)S(1)} %get-tuple-element.77), channel_id=1, source_target_pairs={{0,2},{1,7},{2,4},{3,1},{4,6},{5,3},{6,0},{7,5},{8,10},{9,15},{10,... | collective-permute-start | bytes 1179656 | tf_op jit(solution)/shard_map/ppermute | solution.py:280
  95.0 4.9 %project.5 = (bf16[256,768]{1,0:T(8,128)(2,1)S(1)}, bf16[256,768]{1,0:T(8,128)(2,1)S(1)}, bf16[256,768]{1,0:T(8,128)(2,1)S(1)}, bf16[256,768]{1,0:T(8,128)(2,1)S(1)}) custom-call(s32[1]{0:T(128)} %bitcast.16.core_ref, bf16[1024,512]{1,0:T(8,128)(2,1)S(1)} %copy-done, bf16[1024,512]{1,0:T(8,128)(2,1)S(1)} %copy-done.1, ...), custom_call_target="tpu_custom_call" | custom-call | tf_op jit(solution)/shard_map/project/pallas_call | solution.py:212
  100.0 3.3 %collective-permute-start.15 = (bf16[256,768]{1,0:T(8,128)(2,1)S(1)}, bf16[256,768]{1,0:T(8,128)(2,1)S(1)}, u32[]{:S(2)}, u32[]{:S(2)}) collective-permute-start(bf16[256,768]{1,0:T(8,128)(2,1)S(1)} %add_convert_fusion.5), channel_id=1, source_target_pairs={{0,2},{1,7},{2,4},{3,1},{4,6},{5,3},{6,0},{7,5},{8,10},{9,15},{10,... | collective-permute-start | bytes 1179656 | tf_op jit(solution)/shard_map/ppermute | solution.py:280
  103.4 2.7 %collective-permute-start.25 = (bf16[384,2048]{1,0:T(8,128)(2,1)}, bf16[384,2048]{1,0:T(8,128)(2,1)S(1)}, u32[]{:S(2)}, u32[]{:S(2)}) collective-permute-start(bf16[384,2048]{1,0:T(8,128)(2,1)} %collective-permute-done.12.refs_4_), channel_id=1, source_target_pairs={{32,0},{9,1},{40,8},{17,9},{48,16},{25,17},{56,24},{1,25},{64,32},... | collective-permute-start | bytes 4718600 | tf_op jit(solution)/shard_map/ppermute | solution.py:268
  106.1 4.9 %project.6 = (bf16[256,768]{1,0:T(8,128)(2,1)S(1)}, bf16[256,768]{1,0:T(8,128)(2,1)S(1)}, bf16[256,768]{1,0:T(8,128)(2,1)S(1)}, bf16[256,768]{1,0:T(8,128)(2,1)S(1)}) custom-call(s32[1]{0:T(128)} %bitcast.16.core_ref, bf16[1024,512]{1,0:T(8,128)(2,1)S(1)} %copy-done, bf16[1024,512]{1,0:T(8,128)(2,1)S(1)} %copy-done.1, ...), custom_call_target="tpu_custom_call" | custom-call | tf_op jit(solution)/shard_map/project/pallas_call | solution.py:212
  111.0 2.8 %collective-permute-start.22 = (bf16[256,768]{1,0:T(8,128)(2,1)S(1)}, bf16[256,768]{1,0:T(8,128)(2,1)S(1)}, u32[]{:S(2)}, u32[]{:S(2)}) collective-permute-start(bf16[256,768]{1,0:T(8,128)(2,1)S(1)} %get-tuple-element.91), channel_id=1, source_target_pairs={{0,2},{1,7},{2,4},{3,1},{4,6},{5,3},{6,0},{7,5},{8,10},{9,15},{10,... | collective-permute-start | bytes 1179656 | tf_op jit(solution)/shard_map/ppermute | solution.py:280
  113.9 1.8 %collective-permute-start.18 = (bf16[256,768]{1,0:T(8,128)(2,1)S(1)}, bf16[256,768]{1,0:T(8,128)(2,1)S(1)}, u32[]{:S(2)}, u32[]{:S(2)}) collective-permute-start(bf16[256,768]{1,0:T(8,128)(2,1)S(1)} %add_convert_fusion.3), channel_id=1, source_target_pairs={{0,2},{1,7},{2,4},{3,1},{4,6},{5,3},{6,0},{7,5},{8,10},{9,15},{10,... | collective-permute-start | bytes 1179656 | tf_op jit(solution)/shard_map/ppermute | solution.py:280
  115.8 2.8 %collective-permute-done.22 = bf16[256,768]{1,0:T(8,128)(2,1)S(1)} collective-permute-done((bf16[256,768]{1,0:T(8,128)(2,1)S(1)}, bf16[256,768]{1,0:T(8,128)(2,1)S(1)}, u32[]{:S(2)}, u32[]{:S(2)}) %collective-permute-start.22) | collective-permute-done | bytes 393248 | tf_op jit(solution)/shard_map/ppermute | solution.py:280
  118.7 3.7 %collective-permute-start.23 = (bf16[256,768]{1,0:T(8,128)(2,1)S(1)}, bf16[256,768]{1,0:T(8,128)(2,1)S(1)}, u32[]{:S(2)}, u32[]{:S(2)}) collective-permute-start(bf16[256,768]{1,0:T(8,128)(2,1)S(1)} %add_convert_fusion.1), channel_id=1, source_target_pairs={{0,2},{1,7},{2,4},{3,1},{4,6},{5,3},{6,0},{7,5},{8,10},{9,15},{10,... | collective-permute-start | bytes 1179656 | tf_op jit(solution)/shard_map/ppermute | solution.py:280
  122.9 3.5 %collective-permute-start.19 = (bf16[256,768]{1,0:T(8,128)(2,1)S(1)}, bf16[256,768]{1,0:T(8,128)(2,1)S(1)}, u32[]{:S(2)}, u32[]{:S(2)}) collective-permute-start(bf16[256,768]{1,0:T(8,128)(2,1)S(1)} %add_convert_fusion.2), channel_id=1, source_target_pairs={{0,2},{1,7},{2,4},{3,1},{4,6},{5,3},{6,0},{7,5},{8,10},{9,15},{10,... | collective-permute-start | bytes 1179656 | tf_op jit(solution)/shard_map/ppermute | solution.py:280
  127.2 3.5 %collective-permute-start.24 = (bf16[256,768]{1,0:T(8,128)(2,1)S(1)}, bf16[256,768]{1,0:T(8,128)(2,1)}, u32[]{:S(2)}, u32[]{:S(2)}) collective-permute-start(bf16[256,768]{1,0:T(8,128)(2,1)S(1)} %add_convert_fusion), channel_id=1, source_target_pairs={{0,2},{1,7},{2,4},{3,1},{4,6},{5,3},{6,0},{7,5},{8,10},{9,15},{10,... | collective-permute-start | bytes 1179656 | tf_op jit(solution)/shard_map/ppermute | solution.py:280
  130.7 5.7 %project.7 = (bf16[256,768]{1,0:T(8,128)(2,1)}, bf16[256,768]{1,0:T(8,128)(2,1)}, bf16[256,768]{1,0:T(8,128)(2,1)}, bf16[256,768]{1,0:T(8,128)(2,1)S(1)}) custom-call(s32[1]{0:T(128)} %bitcast.16.core_ref, bf16[1024,512]{1,0:T(8,128)(2,1)S(1)} %copy-done, bf16[1024,512]{1,0:T(8,128)(2,1)S(1)} %copy-done.1, ...), custom_call_target="tpu_custom_call" | custom-call | tf_op jit(solution)/shard_map/project/pallas_call | solution.py:212
  137.5 1.0 collective-permute-start.29
  139.3 4.8 %collective-permute-start.30 = (bf16[128,768]{1,0:T(8,128)(2,1)}, bf16[128,768]{1,0:T(8,128)(2,1)S(1)}, u32[]{:S(2)}, u32[]{:S(2)}) collective-permute-start(bf16[128,768]{1,0:T(8,128)(2,1)} %get-tuple-element.107), channel_id=1, source_target_pairs={{0,1},{1,0},{2,3},{3,2},{4,5},{5,4},{6,7},{7,6},{8,9},{9,8},{10,11... | collective-permute-start | bytes 589832 | tf_op jit(solution)/shard_map/ppermute | solution.py:272
  144.9 1.3 collective-permute-done.24
  146.2 7.2 %collective-permute-start.31 = (bf16[128,768]{1,0:T(8,128)(2,1)}, bf16[128,768]{1,0:T(8,128)(2,1)S(1)}, u32[]{:S(2)}, u32[]{:S(2)}) collective-permute-start(bf16[128,768]{1,0:T(8,128)(2,1)} %get-tuple-element.105), channel_id=1, source_target_pairs={{0,1},{1,0},{2,3},{3,2},{4,5},{5,4},{6,7},{7,6},{8,9},{9,8},{10,11... | collective-permute-start | bytes 589832 | tf_op jit(solution)/shard_map/ppermute | solution.py:272
  153.4 2.1 %add_convert_fusion.7 = (bf16[128,768]{1,0:T(8,128)(2,1)}, f32[128,768]{1,0:T(8,128)S(1)}) fusion(bf16[256,768]{1,0:T(8,128)(2,1)} %collective-permute-done.24, s32[]{:T(128)S(6)} %select_n.190, bf16[256,768]{1,0:T(8,128)(2,1)} %copy-done.3, s32[]{:T(128)S(6)} %select_n.189), kind=kLoop, calls=%fused_computation.9 | loop fusion | flops 688128 | bytes 1376264 | tf_op jit(solution)/shard_map/convert_element_type | solution.py:294
  155.5 1.2 collective-permute-done.28
  156.7 2.0 %collective-permute-done.29 = bf16[256,768]{1,0:T(8,128)(2,1)} collective-permute-done((bf16[256,768]{1,0:T(8,128)(2,1)}, bf16[256,768]{1,0:T(8,128)(2,1)}, u32[]{:S(2)}, u32[]{:S(2)}) %collective-permute-start.29) | collective-permute-done | bytes 393248 | tf_op jit(solution)/shard_map/ppermute | solution.py:280
  158.7 2.2 %add_convert_fusion.6 = (bf16[128,768]{1,0:T(8,128)(2,1)}, f32[128,768]{1,0:T(8,128)S(1)}) fusion(bf16[256,768]{1,0:T(8,128)(2,1)} %collective-permute-done.29, s32[]{:T(128)S(6)} %select_n.190, bf16[256,768]{1,0:T(8,128)(2,1)} %collective-permute-done.28, bf16[256,768]{1,0:T(8,128)(2,1)} %collective-permute-done.27, bf16[256,768]{1,0:T(8,128)(2,1)S(1)} %copy-done.5, ...), kind=kLoop, calls=%fused_computation.8 | loop fusion | flops 1474560 | bytes 2162696 | tf_op jit(solution)/shard_map/convert_element_type | solution.py:294
  160.9 2.2 %collective-permute-start.33 = (bf16[128,768]{1,0:T(8,128)(2,1)}, bf16[128,768]{1,0:T(8,128)(2,1)}, u32[]{:S(2)}, u32[]{:S(2)}) collective-permute-start(bf16[128,768]{1,0:T(8,128)(2,1)} %get-tuple-element.101), channel_id=1, source_target_pairs={{0,1},{1,0},{2,3},{3,2},{4,5},{5,4},{6,7},{7,6},{8,9},{9,8},{10,11... | collective-permute-start | bytes 589832 | tf_op jit(solution)/shard_map/ppermute | solution.py:272
  163.2 1.3 collective-permute-done.33.refs_7_
  164.5 3.0 %finish.1 = bf16[128,6144]{1,0:T(8,128)(2,1)} custom-call(s32[17]{0:T(128)S(1)} %stack.135.tab_ref, bf16[128,6144]{1,0:T(8,128)(2,1)S(1)} %copy-done.2, f32[128,768]{1,0:T(8,128)S(1)} %get-tuple-element.108.refs_0_, f32[128,768]{1,0:T(8,128)S(1)} %get-tuple-element.106.refs_1_, f32[128,768]{1,0:T(8,128)S(1)} %get-tuple-element.104.refs_2_, ...), custom_call_target="tpu_custom_call" | custom-call | tf_op jit(solution)/shard_map/finish/pallas_call | solution.py:243
  (84 shorter events, 10.1 us)
Async XLA Ops:
  1.9 6.4 %collective-permute-start = (bf16[192,1024]{1,0:T(8,128)(2,1)S(1)}, bf16[192,1024]{1,0:T(8,128)(2,1)S(1)}, u32[]{:S(2)}, u32[]{:S(2)}) collective-permute-start(bf16[192,1024]{1,0:T(8,128)(2,1)S(1)} %bitcast.36), channel_id=1, source_target_pairs={{0,1},{1,0},{2,3},{3,2},{4,5},{5,4},{6,7},{7,6},{8,9},{9,8},{10,11... | collective-permute-start | bytes 1179656 | tf_op jit(solution)/shard_map/ppermute | solution.py:272
  8.4 3.7 %copy-start.16 = (bf16[64,2048]{1,0:T(8,128)(2,1)S(1)}, bf16[64,2048]{1,0:T(8,128)(2,1)}, u32[]{:S(2)}) copy-start(bf16[64,2048]{1,0:T(8,128)(2,1)} %get-tuple-element.54.state_ref) | copy-start | bytes 786436
  8.4 13.7 %copy-start.9 = (bf16[192,1024]{1,0:T(8,128)(2,1)}, bf16[192,1024]{1,0:T(8,128)(2,1)S(1)}, u32[]{:S(2)}) copy-start(bf16[192,1024]{1,0:T(8,128)(2,1)S(1)} %collective-permute-done) | copy-start | bytes 1179652
  9.3 16.5 %collective-permute-start.3 = (bf16[192,2048]{1,0:T(8,128)(2,1)}, bf16[192,2048]{1,0:T(8,128)(2,1)S(1)}, u32[]{:S(2)}, u32[]{:S(2)}) collective-permute-start(bf16[192,2048]{1,0:T(8,128)(2,1)} %pad_maximum_fusion.1), channel_id=1, source_target_pairs={{24,0},{97,1},{0,8},{105,9},{8,16},{113,17},{16,24},{121,25},{56,3... | collective-permute-start | bytes 2359304 | tf_op jit(solution)/shard_map/ppermute | solution.py:268
  10.6 15.2 %collective-permute-start.2 = (bf16[192,2048]{1,0:T(8,128)(2,1)}, bf16[192,2048]{1,0:T(8,128)(2,1)}, u32[]{:S(2)}, u32[]{:S(2)}) collective-permute-start(bf16[192,2048]{1,0:T(8,128)(2,1)} %pad_maximum_fusion.1), channel_id=1, source_target_pairs={{8,0},{33,1},{16,8},{41,9},{24,16},{49,17},{0,24},{57,25},{40,32},... | collective-permute-start | bytes 2359304 | tf_op jit(solution)/shard_map/ppermute | solution.py:268
  12.0 13.8 %collective-permute-start.5 = (bf16[64,2048]{1,0:T(8,128)(2,1)S(1)}, bf16[64,2048]{1,0:T(8,128)(2,1)S(1)}, u32[]{:S(2)}, u32[]{:S(2)}) collective-permute-start(bf16[64,2048]{1,0:T(8,128)(2,1)S(1)} %copy-done.16), channel_id=1, source_target_pairs={{16,0},{65,1},{24,8},{73,9},{0,16},{81,17},{8,24},{89,25},{48,32},... | collective-permute-start | bytes 786440 | tf_op jit(solution)/shard_map/ppermute | solution.py:268
  13.6 13.9 %collective-permute-start.4 = (bf16[64,2048]{1,0:T(8,128)(2,1)S(1)}, bf16[64,2048]{1,0:T(8,128)(2,1)S(1)}, u32[]{:S(2)}, u32[]{:S(2)}) collective-permute-start(bf16[64,2048]{1,0:T(8,128)(2,1)S(1)} %copy-done.16), channel_id=1, source_target_pairs={{24,0},{97,1},{0,8},{105,9},{8,16},{113,17},{16,24},{121,25},{56,3... | collective-permute-start | bytes 786440 | tf_op jit(solution)/shard_map/ppermute | solution.py:268
  13.9 13.7 %collective-permute-start.1 = (bf16[64,2048]{1,0:T(8,128)(2,1)S(1)}, bf16[64,2048]{1,0:T(8,128)(2,1)S(1)}, u32[]{:S(2)}, u32[]{:S(2)}) collective-permute-start(bf16[64,2048]{1,0:T(8,128)(2,1)S(1)} %copy-done.16), channel_id=1, source_target_pairs={{8,0},{33,1},{16,8},{41,9},{24,16},{49,17},{0,24},{57,25},{40,32},... | collective-permute-start | bytes 786440 | tf_op jit(solution)/shard_map/ppermute | solution.py:268
  25.8 1.8 %copy-start.6 = (bf16[64,2048]{1,0:T(8,128)(2,1)}, bf16[64,2048]{1,0:T(8,128)(2,1)S(1)}, u32[]{:S(2)}) copy-start(bf16[64,2048]{1,0:T(8,128)(2,1)S(1)} %collective-permute-done.5.z3) | copy-start | bytes 786436
  25.8 11.1 %copy-start.14 = (bf16[192,2048]{1,0:T(8,128)(2,1)}, bf16[192,2048]{1,0:T(8,128)(2,1)S(1)}, u32[]{:S(2)}) copy-start(bf16[192,2048]{1,0:T(8,128)(2,1)S(1)} %collective-permute-done.3) | copy-start | bytes 2359300
  31.9 13.6 %collective-permute-start.7 = (bf16[64,2048]{1,0:T(8,128)(2,1)}, bf16[64,2048]{1,0:T(8,128)(2,1)S(1)}, u32[]{:S(2)}, u32[]{:S(2)}) collective-permute-start(bf16[64,2048]{1,0:T(8,128)(2,1)} %get-tuple-element.61), channel_id=1, source_target_pairs={{32,0},{9,1},{40,8},{17,9},{48,16},{25,17},{56,24},{1,25},{64,32},... | collective-permute-start | bytes 786440 | tf_op jit(solution)/shard_map/ppermute | solution.py:268
  35.7 9.7 %collective-permute-start.8 = (bf16[64,2048]{1,0:T(8,128)(2,1)}, bf16[64,2048]{1,0:T(8,128)(2,1)S(1)}, u32[]{:S(2)}, u32[]{:S(2)}) collective-permute-start(bf16[64,2048]{1,0:T(8,128)(2,1)} %get-tuple-element.68), channel_id=1, source_target_pairs={{96,0},{25,1},{104,8},{1,9},{112,16},{9,17},{120,24},{17,25},{0,32... | collective-permute-start | bytes 786440 | tf_op jit(solution)/shard_map/ppermute | solution.py:268
  35.7 7.0 %copy-start.10 = (bf16[192,1024]{1,0:T(8,128)(2,1)S(1)}, bf16[192,1024]{1,0:T(8,128)(2,1)}, u32[]{:S(2)}) copy-start(bf16[192,1024]{1,0:T(8,128)(2,1)} %copy-done.9) | copy-start | bytes 1179652
  35.7 8.4 %collective-permute-start.9 = (bf16[64,2048]{1,0:T(8,128)(2,1)}, bf16[64,2048]{1,0:T(8,128)(2,1)S(1)}, u32[]{:S(2)}, u32[]{:S(2)}) collective-permute-start(bf16[64,2048]{1,0:T(8,128)(2,1)} %get-tuple-element.70), channel_id=1, source_target_pairs={{64,0},{17,1},{72,8},{25,9},{80,16},{1,17},{88,24},{9,25},{96,32},... | collective-permute-start | bytes 786440 | tf_op jit(solution)/shard_map/ppermute | solution.py:268
  44.1 25.6 %copy-start.13 = (bf16[64,2048]{1,0:T(8,128)(2,1)}, bf16[64,2048]{1,0:T(8,128)(2,1)S(1)}, u32[]{:S(2)}) copy-start(bf16[64,2048]{1,0:T(8,128)(2,1)S(1)} %collective-permute-done.9.x3) | copy-start | bytes 786436
  45.4 24.2 %copy-start.12 = (bf16[64,2048]{1,0:T(8,128)(2,1)}, bf16[64,2048]{1,0:T(8,128)(2,1)S(1)}, u32[]{:S(2)}) copy-start(bf16[64,2048]{1,0:T(8,128)(2,1)S(1)} %collective-permute-done.8.x2) | copy-start | bytes 786436
  45.5 24.2 %copy-start.11 = (bf16[64,2048]{1,0:T(8,128)(2,1)}, bf16[64,2048]{1,0:T(8,128)(2,1)S(1)}, u32[]{:S(2)}) copy-start(bf16[64,2048]{1,0:T(8,128)(2,1)S(1)} %collective-permute-done.7.x1) | copy-start | bytes 786436
  45.5 37.1 %collective-permute-start.13 = (bf16[384,2048]{1,0:T(8,128)(2,1)S(1)}, bf16[384,2048]{1,0:T(8,128)(2,1)}, u32[]{:S(2)}, u32[]{:S(2)}) collective-permute-start(bf16[384,2048]{1,0:T(8,128)(2,1)S(1)} %pad_maximum_fusion.refs_4_), channel_id=1, source_target_pairs={{96,0},{25,1},{104,8},{1,9},{112,16},{9,17},{120,24},{17,25},{0,32... | collective-permute-start | bytes 4718600 | tf_op jit(solution)/shard_map/ppermute | solution.py:268
  46.1 36.5 %collective-permute-start.12 = (bf16[384,2048]{1,0:T(8,128)(2,1)S(1)}, bf16[384,2048]{1,0:T(8,128)(2,1)}, u32[]{:S(2)}, u32[]{:S(2)}) collective-permute-start(bf16[384,2048]{1,0:T(8,128)(2,1)S(1)} %pad_maximum_fusion.refs_4_), channel_id=1, source_target_pairs={{32,0},{9,1},{40,8},{17,9},{48,16},{25,17},{56,24},{1,25},{64,32},... | collective-permute-start | bytes 4718600 | tf_op jit(solution)/shard_map/ppermute | solution.py:268
  48.2 21.4 %collective-permute-start.6 = (bf16[192,2048]{1,0:T(8,128)(2,1)}, bf16[192,2048]{1,0:T(8,128)(2,1)}, u32[]{:S(2)}, u32[]{:S(2)}) collective-permute-start(bf16[192,2048]{1,0:T(8,128)(2,1)} %pad_maximum_fusion.1), channel_id=1, source_target_pairs={{16,0},{65,1},{24,8},{73,9},{0,16},{81,17},{8,24},{89,25},{48,32},... | collective-permute-start | bytes 2359304 | tf_op jit(solution)/shard_map/ppermute | solution.py:268
  73.8 11.5 %collective-permute-start.10 = (bf16[1024,512]{1,0:T(8,128)(2,1)}, bf16[1024,512]{1,0:T(8,128)(2,1)S(1)}, u32[]{:S(2)}, u32[]{:S(2)}) collective-permute-start(bf16[1024,512]{1,0:T(8,128)(2,1)} %norm.2.refs_0_), channel_id=1, source_target_pairs={{0,1},{1,0},{2,3},{3,2},{4,5},{5,4},{6,7},{7,6},{8,9},{9,8},{10,11... | collective-permute-start | bytes 3145736 | tf_op jit(solution)/shard_map/ppermute | solution.py:272
  76.8 4.4 %copy-start.15 = (bf16[192,2048]{1,0:T(8,128)(2,1)S(1)}, bf16[192,2048]{1,0:T(8,128)(2,1)}, u32[]{:S(2)}) copy-start(bf16[192,2048]{1,0:T(8,128)(2,1)} %copy-done.14) | copy-start | bytes 2359300
  81.1 4.3 %copy-start = (bf16[1024,512]{1,0:T(8,128)(2,1)S(1)}, bf16[1024,512]{1,0:T(8,128)(2,1)}, u32[]{:S(2)}) copy-start(bf16[1024,512]{1,0:T(8,128)(2,1)} %norm.2.refs_0_) | copy-start | bytes 3145732
  81.1 4.3 %copy-start.1 = (bf16[1024,512]{1,0:T(8,128)(2,1)S(1)}, bf16[1024,512]{1,0:T(8,128)(2,1)}, u32[]{:S(2)}) copy-start(bf16[1024,512]{1,0:T(8,128)(2,1)} %norm.3.refs_1_) | copy-start | bytes 3145732
  81.1 4.3 %collective-permute-start.11 = (bf16[1024,512]{1,0:T(8,128)(2,1)}, bf16[1024,512]{1,0:T(8,128)(2,1)S(1)}, u32[]{:S(2)}, u32[]{:S(2)}) collective-permute-start(bf16[1024,512]{1,0:T(8,128)(2,1)} %norm.3.refs_1_), channel_id=1, source_target_pairs={{0,1},{1,0},{2,3},{3,2},{4,5},{5,4},{6,7},{7,6},{8,9},{9,8},{10,11... | collective-permute-start | bytes 3145736 | tf_op jit(solution)/shard_map/ppermute | solution.py:272
  82.6 20.8 %collective-permute-start.21 = (bf16[384,2048]{1,0:T(8,128)(2,1)S(1)}, bf16[384,2048]{1,0:T(8,128)(2,1)S(1)}, u32[]{:S(2)}, u32[]{:S(2)}) collective-permute-start(bf16[384,2048]{1,0:T(8,128)(2,1)S(1)} %constant_dynamic-update-slice_fusion.refs_5_), channel_id=1, source_target_pairs={{96,0},{25,1},{104,8},{1,9},{112,16},{9,17},{120,24},{17,25},{0,32... | collective-permute-start | bytes 4718600 | tf_op jit(solution)/shard_map/ppermute | solution.py:268
  83.5 20.0 %collective-permute-start.20 = (bf16[384,2048]{1,0:T(8,128)(2,1)S(1)}, bf16[384,2048]{1,0:T(8,128)(2,1)S(1)}, u32[]{:S(2)}, u32[]{:S(2)}) collective-permute-start(bf16[384,2048]{1,0:T(8,128)(2,1)S(1)} %constant_dynamic-update-slice_fusion.refs_5_), channel_id=1, source_target_pairs={{32,0},{9,1},{40,8},{17,9},{48,16},{25,17},{56,24},{1,25},{64,32},... | collective-permute-start | bytes 4718600 | tf_op jit(solution)/shard_map/ppermute | solution.py:268
  92.2 7.7 %collective-permute-start.14 = (bf16[256,768]{1,0:T(8,128)(2,1)S(1)}, bf16[256,768]{1,0:T(8,128)(2,1)S(1)}, u32[]{:S(2)}, u32[]{:S(2)}) collective-permute-start(bf16[256,768]{1,0:T(8,128)(2,1)S(1)} %get-tuple-element.77), channel_id=1, source_target_pairs={{0,2},{1,7},{2,4},{3,1},{4,6},{5,3},{6,0},{7,5},{8,10},{9,15},{10,... | collective-permute-start | bytes 1179656 | tf_op jit(solution)/shard_map/ppermute | solution.py:280
  100.0 11.0 %collective-permute-start.15 = (bf16[256,768]{1,0:T(8,128)(2,1)S(1)}, bf16[256,768]{1,0:T(8,128)(2,1)S(1)}, u32[]{:S(2)}, u32[]{:S(2)}) collective-permute-start(bf16[256,768]{1,0:T(8,128)(2,1)S(1)} %add_convert_fusion.5), channel_id=1, source_target_pairs={{0,2},{1,7},{2,4},{3,1},{4,6},{5,3},{6,0},{7,5},{8,10},{9,15},{10,... | collective-permute-start | bytes 1179656 | tf_op jit(solution)/shard_map/ppermute | solution.py:280
  103.3 10.6 %collective-permute-start.17 = (bf16[256,768]{1,0:T(8,128)(2,1)S(1)}, bf16[256,768]{1,0:T(8,128)(2,1)S(1)}, u32[]{:S(2)}, u32[]{:S(2)}) collective-permute-start(bf16[256,768]{1,0:T(8,128)(2,1)S(1)} %get-tuple-element.84), channel_id=1, source_target_pairs={{0,2},{1,7},{2,4},{3,1},{4,6},{5,3},{6,0},{7,5},{8,10},{9,15},{10,... | collective-permute-start | bytes 1179656 | tf_op jit(solution)/shard_map/ppermute | solution.py:280
  103.4 27.2 %collective-permute-start.25 = (bf16[384,2048]{1,0:T(8,128)(2,1)}, bf16[384,2048]{1,0:T(8,128)(2,1)S(1)}, u32[]{:S(2)}, u32[]{:S(2)}) collective-permute-start(bf16[384,2048]{1,0:T(8,128)(2,1)} %collective-permute-done.12.refs_4_), channel_id=1, source_target_pairs={{32,0},{9,1},{40,8},{17,9},{48,16},{25,17},{56,24},{1,25},{64,32},... | collective-permute-start | bytes 4718600 | tf_op jit(solution)/shard_map/ppermute | solution.py:268
  106.1 24.6 %collective-permute-start.26 = (bf16[384,2048]{1,0:T(8,128)(2,1)S(1)}, bf16[384,2048]{1,0:T(8,128)(2,1)S(1)}, u32[]{:S(2)}, u32[]{:S(2)}) collective-permute-start(bf16[384,2048]{1,0:T(8,128)(2,1)S(1)} %collective-permute-done.21.refs_5_), channel_id=1, source_target_pairs={{96,0},{25,1},{104,8},{1,9},{112,16},{9,17},{120,24},{17,25},{0,32... | collective-permute-start | bytes 4718600 | tf_op jit(solution)/shard_map/ppermute | solution.py:268
  111.0 19.7 %copy-start.3 = (bf16[256,768]{1,0:T(8,128)(2,1)}, bf16[256,768]{1,0:T(8,128)(2,1)S(1)}, u32[]{:S(2)}) copy-start(bf16[256,768]{1,0:T(8,128)(2,1)S(1)} %get-tuple-element.89) | copy-start | bytes 1179652
  111.0 7.5 %collective-permute-start.22 = (bf16[256,768]{1,0:T(8,128)(2,1)S(1)}, bf16[256,768]{1,0:T(8,128)(2,1)S(1)}, u32[]{:S(2)}, u32[]{:S(2)}) collective-permute-start(bf16[256,768]{1,0:T(8,128)(2,1)S(1)} %get-tuple-element.91), channel_id=1, source_target_pairs={{0,2},{1,7},{2,4},{3,1},{4,6},{5,3},{6,0},{7,5},{8,10},{9,15},{10,... | collective-permute-start | bytes 1179656 | tf_op jit(solution)/shard_map/ppermute | solution.py:280
  113.9 8.8 %collective-permute-start.18 = (bf16[256,768]{1,0:T(8,128)(2,1)S(1)}, bf16[256,768]{1,0:T(8,128)(2,1)S(1)}, u32[]{:S(2)}, u32[]{:S(2)}) collective-permute-start(bf16[256,768]{1,0:T(8,128)(2,1)S(1)} %add_convert_fusion.3), channel_id=1, source_target_pairs={{0,2},{1,7},{2,4},{3,1},{4,6},{5,3},{6,0},{7,5},{8,10},{9,15},{10,... | collective-permute-start | bytes 1179656 | tf_op jit(solution)/shard_map/ppermute | solution.py:280
  118.7 8.4 %collective-permute-start.23 = (bf16[256,768]{1,0:T(8,128)(2,1)S(1)}, bf16[256,768]{1,0:T(8,128)(2,1)S(1)}, u32[]{:S(2)}, u32[]{:S(2)}) collective-permute-start(bf16[256,768]{1,0:T(8,128)(2,1)S(1)} %add_convert_fusion.1), channel_id=1, source_target_pairs={{0,2},{1,7},{2,4},{3,1},{4,6},{5,3},{6,0},{7,5},{8,10},{9,15},{10,... | collective-permute-start | bytes 1179656 | tf_op jit(solution)/shard_map/ppermute | solution.py:280
  122.5 15.1 %collective-permute-start.16 = (bf16[256,768]{1,0:T(8,128)(2,1)S(1)}, bf16[256,768]{1,0:T(8,128)(2,1)S(1)}, u32[]{:S(2)}, u32[]{:S(2)}) collective-permute-start(bf16[256,768]{1,0:T(8,128)(2,1)S(1)} %add_convert_fusion.4), channel_id=1, source_target_pairs={{0,2},{1,7},{2,4},{3,1},{4,6},{5,3},{6,0},{7,5},{8,10},{9,15},{10,... | collective-permute-start | bytes 1179656 | tf_op jit(solution)/shard_map/ppermute | solution.py:280
  122.9 16.4 %collective-permute-start.19 = (bf16[256,768]{1,0:T(8,128)(2,1)S(1)}, bf16[256,768]{1,0:T(8,128)(2,1)S(1)}, u32[]{:S(2)}, u32[]{:S(2)}) collective-permute-start(bf16[256,768]{1,0:T(8,128)(2,1)S(1)} %add_convert_fusion.2), channel_id=1, source_target_pairs={{0,2},{1,7},{2,4},{3,1},{4,6},{5,3},{6,0},{7,5},{8,10},{9,15},{10,... | collective-permute-start | bytes 1179656 | tf_op jit(solution)/shard_map/ppermute | solution.py:280
  127.2 19.0 %collective-permute-start.24 = (bf16[256,768]{1,0:T(8,128)(2,1)S(1)}, bf16[256,768]{1,0:T(8,128)(2,1)}, u32[]{:S(2)}, u32[]{:S(2)}) collective-permute-start(bf16[256,768]{1,0:T(8,128)(2,1)S(1)} %add_convert_fusion), channel_id=1, source_target_pairs={{0,2},{1,7},{2,4},{3,1},{4,6},{5,3},{6,0},{7,5},{8,10},{9,15},{10,... | collective-permute-start | bytes 1179656 | tf_op jit(solution)/shard_map/ppermute | solution.py:280
  137.1 18.4 %collective-permute-start.27 = (bf16[256,768]{1,0:T(8,128)(2,1)}, bf16[256,768]{1,0:T(8,128)(2,1)}, u32[]{:S(2)}, u32[]{:S(2)}) collective-permute-start(bf16[256,768]{1,0:T(8,128)(2,1)} %get-tuple-element.98), channel_id=1, source_target_pairs={{0,4},{1,5},{2,6},{3,7},{4,0},{5,1},{6,2},{7,3},{8,12},{9,13},{10,... | collective-permute-start | bytes 1179656 | tf_op jit(solution)/shard_map/ppermute | solution.py:280
  137.1 19.6 %collective-permute-start.28 = (bf16[256,768]{1,0:T(8,128)(2,1)}, bf16[256,768]{1,0:T(8,128)(2,1)}, u32[]{:S(2)}, u32[]{:S(2)}) collective-permute-start(bf16[256,768]{1,0:T(8,128)(2,1)} %get-tuple-element.99), channel_id=1, source_target_pairs={{0,2},{1,7},{2,4},{3,1},{4,6},{5,3},{6,0},{7,5},{8,10},{9,15},{10,... | collective-permute-start | bytes 1179656 | tf_op jit(solution)/shard_map/ppermute | solution.py:280
  137.5 21.2 %collective-permute-start.29 = (bf16[256,768]{1,0:T(8,128)(2,1)}, bf16[256,768]{1,0:T(8,128)(2,1)}, u32[]{:S(2)}, u32[]{:S(2)}) collective-permute-start(bf16[256,768]{1,0:T(8,128)(2,1)} %get-tuple-element.100), channel_id=1, source_target_pairs={{0,6},{1,3},{2,0},{3,5},{4,2},{5,7},{6,4},{7,1},{8,14},{9,11},{10,... | collective-permute-start | bytes 1179656 | tf_op jit(solution)/shard_map/ppermute | solution.py:280
  139.3 19.4 %copy-start.5 = (bf16[256,768]{1,0:T(8,128)(2,1)S(1)}, bf16[256,768]{1,0:T(8,128)(2,1)}, u32[]{:S(2)}) copy-start(bf16[256,768]{1,0:T(8,128)(2,1)} %copy-done.4) | copy-start | bytes 1179652
  139.3 23.9 %collective-permute-start.30 = (bf16[128,768]{1,0:T(8,128)(2,1)}, bf16[128,768]{1,0:T(8,128)(2,1)S(1)}, u32[]{:S(2)}, u32[]{:S(2)}) collective-permute-start(bf16[128,768]{1,0:T(8,128)(2,1)} %get-tuple-element.107), channel_id=1, source_target_pairs={{0,1},{1,0},{2,3},{3,2},{4,5},{5,4},{6,7},{7,6},{8,9},{9,8},{10,11... | collective-permute-start | bytes 589832 | tf_op jit(solution)/shard_map/ppermute | solution.py:272
  146.2 17.0 %collective-permute-start.31 = (bf16[128,768]{1,0:T(8,128)(2,1)}, bf16[128,768]{1,0:T(8,128)(2,1)S(1)}, u32[]{:S(2)}, u32[]{:S(2)}) collective-permute-start(bf16[128,768]{1,0:T(8,128)(2,1)} %get-tuple-element.105), channel_id=1, source_target_pairs={{0,1},{1,0},{2,3},{3,2},{4,5},{5,4},{6,7},{7,6},{8,9},{9,8},{10,11... | collective-permute-start | bytes 589832 | tf_op jit(solution)/shard_map/ppermute | solution.py:272
  153.4 11.1 %copy-start.2 = (bf16[128,6144]{1,0:T(8,128)(2,1)S(1)}, bf16[128,6144]{1,0:T(8,128)(2,1)}, u32[]{:S(2)}) copy-start(bf16[128,6144]{1,0:T(8,128)(2,1)} %res_ref.1) | copy-start | bytes 4718596
  155.5 7.7 %collective-permute-start.32 = (bf16[128,768]{1,0:T(8,128)(2,1)}, bf16[128,768]{1,0:T(8,128)(2,1)}, u32[]{:S(2)}, u32[]{:S(2)}) collective-permute-start(bf16[128,768]{1,0:T(8,128)(2,1)} %get-tuple-element.103), channel_id=1, source_target_pairs={{0,1},{1,0},{2,3},{3,2},{4,5},{5,4},{6,7},{7,6},{8,9},{9,8},{10,11... | collective-permute-start | bytes 589832 | tf_op jit(solution)/shard_map/ppermute | solution.py:272
  160.9 3.6 %collective-permute-start.33 = (bf16[128,768]{1,0:T(8,128)(2,1)}, bf16[128,768]{1,0:T(8,128)(2,1)}, u32[]{:S(2)}, u32[]{:S(2)}) collective-permute-start(bf16[128,768]{1,0:T(8,128)(2,1)} %get-tuple-element.101), channel_id=1, source_target_pairs={{0,1},{1,0},{2,3},{3,2},{4,5},{5,4},{6,7},{7,6},{8,9},{9,8},{10,11... | collective-permute-start | bytes 589832 | tf_op jit(solution)/shard_map/ppermute | solution.py:272
  (3 other events, 2.2 us)

commit v4 on v3

--- a/solution.py
+++ b/solution.py
@@ -109,14 +109,11 @@
 
 
 def messages(table, state, pieces):
-    rows, columns = state.shape
-    own = pl.BlockSpec((rows, columns // 2), lambda g, t: (0, g))
-    last = pl.BlockSpec((rows, columns // 2), lambda g, t: (0, g))
     return pl.pallas_call(
         message_body,
-        grid_spec=pltpu.PrefetchScalarGridSpec(
-            num_scalar_prefetch=1, grid=(2,), in_specs=[own] + [last] * 3, out_specs=[own] * 3
-        ),
+        in_specs=[pl.BlockSpec(memory_space=pltpu.SMEM)]
+        + [pl.BlockSpec(memory_space=pltpu.VMEM)] * 4,
+        out_specs=[pl.BlockSpec(memory_space=pltpu.VMEM)] * 3,
         out_shape=[jax.ShapeDtypeStruct(state.shape, BF16)] * 3,
         name="messages",
     )(table, state, *pieces)
@@ -169,22 +166,21 @@
     )(table, *half, gain, *z_pieces, *x_pieces)
 
 
-def project_body(counts, core_ref, *refs):
-    tokens, weights, outs = refs[:4], refs[4 : 4 + len(counts)], refs[4 + len(counts) :]
+def project_body(core_ref, *refs):
+    tokens, (a_first, a_second, b_first, b_second), outs = refs[:4], refs[4:8], refs[8:]
     step = pl.program_id(0)
-    depth, rows = tokens[0].shape[1], outs[0].shape[0]
+    rows = outs[0].shape[0]
     first_core = core_ref[0] == 0
-    first = 0
-    for w_ref, count in zip(weights, counts):
-
-        @pl.when((step >= first) & (step < first + count))
-        def _(w_ref=w_ref):
-            total = 0.0
-            for index, t_ref in enumerate(tokens):
-                columns = slice(index * depth, (index + 1) * depth)
-                total = total + contract(t_ref[...], w_ref[:, columns], ((1,), (1,)))
+    pairs = ((a_first, a_second), (a_first, b_first), (b_first, b_second))
+    for index, (upper, lower) in enumerate(pairs):
+
+        @pl.when(step == index)
+        def _(upper=upper, lower=lower):
+            joined = jnp.concatenate([t_ref[...] for t_ref in tokens], axis=1)
+            weights = jnp.concatenate([upper[...], lower[...]], axis=0)
+            total = contract(joined, weights, ((1,), (1,)))
             far, right, left, own = (
-                total[index * rows : (index + 1) * rows].astype(BF16) for index in range(4)
+                total[place * rows : (place + 1) * rows].astype(BF16) for place in range(4)
             )
             for out, block in zip(
                 outs,
@@ -192,35 +188,35 @@
             ):
                 out[...] = block
 
-        first += count
-
-
-def project(core, tokens, weights, tile):
-    rows, depth = tokens[0].shape
-    counts = tuple(w.shape[0] // tile for w in weights)
-    columns = tile * sum(counts)
-    specs, first = [], 0
-    for count in counts:
-        specs.append(
-            pl.BlockSpec(
-                (tile, 4 * depth),
-                lambda g, t, first=first, count=count: (jnp.clip(g - first, 0, count - 1), 0),
-            )
-        )
-        first += count
-    whole = pl.BlockSpec((rows, depth), lambda g, t: (0, 0))
-    return pl.pallas_call(
-        functools.partial(project_body, counts),
+
+def project(core, tokens, weights):
+    rows = tokens[0].shape[0]
+    first, second = weights
+    tile, depth = first.shape[0] // 3, first.shape[1]
+    columns = 6 * tile
+
+    def piece(place):
+        return pl.BlockSpec((tile, depth), lambda g, t: (place(g), 0))
+
+    whole = pl.BlockSpec(memory_space=pltpu.VMEM)
+    return pl.pallas_call(
+        project_body,
         grid_spec=pltpu.PrefetchScalarGridSpec(
             num_scalar_prefetch=1,
-            grid=(sum(counts),),
-            in_specs=[whole] * 4 + specs,
-            out_specs=[pl.BlockSpec((rows // 4, tile), lambda g, t: (0, g))] * 4,
+            grid=(3,),
+            in_specs=[whole] * 4
+            + [
+                piece(lambda g: jnp.minimum(2 * g, 2)),
+                piece(lambda g: 1),
+                piece(lambda g: jnp.maximum(g - 1, 0)),
+                piece(lambda g: 2),
+            ],
+            out_specs=[pl.BlockSpec((rows // 4, 2 * tile), lambda g, t: (0, g))] * 4,
         ),
         out_shape=[jax.ShapeDtypeStruct((rows // 4, columns), BF16)] * 4,
-        compiler_params=pltpu.CompilerParams(vmem_limit_bytes=40 * 1024 * 1024),
+        compiler_params=pltpu.CompilerParams(vmem_limit_bytes=24 * 1024 * 1024),
         name="project",
-    )(core, *tokens, *weights)
+    )(core, *tokens, first, first, second, second)
 
 
 def finish_body(layout, tab_ref, res_ref, *refs):
@@ -317,16 +313,15 @@
     level1 = [after(piece, early[0], plus, minus) for piece in level1]
     sent = messages(table, state, level1)
     level2 = [fetch_mixed(piece, 2, offset) for piece, offset in zip(sent, REL[1:])]
-    far = fetch_mixed(after(base, sent[0]), 1, 2)
     late = local_attention(after(query, sent[0]), k_act, value, heads, heads)
     level2 = [after(piece, late[0]) for piece in level2]
     g0a = jnp.concatenate([base, plus], axis=0)
     g0a = after(g0a, *level2)
+    far = fetch_mixed(after(base, *level2), 1, 2)
     g1a, g3a = fetch_mixed(g0a, 2, 1), fetch_mixed(g0a, 2, 3)
     g0b = jnp.concatenate([minus, far], axis=0)
 
     gain = head_gain.reshape(1, -1)
-    table = after(table, far)
     norm_a = norm(table, early, 0, gain, level1, level2)
     swap_a = swap(norm_a)
     norm_b = norm(after(table, norm_a), late, heads, gain, level1, level2)
@@ -336,7 +331,7 @@
     g1b, g3b = fetch_mixed(ready, 2, 1), fetch_mixed(ready, 2, 3)
 
     def columns(weights, *others):
-        return project(core, [after(norm_a, *others), norm_b, swap_a, swap_b], weights, 384)
+        return project(core, [after(norm_a, *others), norm_b, swap_a, swap_b], weights)
 
     first = columns([g1a, g3a], norm_b)
     second = columns([g0a, g0b], first[0])

time: 168 us -> 161 us (0.958)
  waiting for transfers between devices: 36.1 us -> 25.8 us
  starting transfers between devices: 63.5 us -> 70.8 us
  Pallas kernels: 52.8 us -> 48.7 us
    ppermute x7, starting transfers between devices: 18.8 us -> 26.5 us  [swap(): return lax.ppermute(array, 'c', [(0, 1), (1, 0)])]
    ppermute x15, waiting for transfers between devices: 26.6 us -> 19.5 us  [fetch_mixed(): return lax.ppermute(array, ('x', 'z', 'c'), pairs)]
    pallas_call x5, Pallas kernels: 25.2 us -> 21 us  [the longest x4 18.6 us: project(): pl.pallas_call(project_body, grid_spec=pltpu.PrefetchScalarGridSpec(num_s...]
    ppermute x12, waiting for transfers between devices: 8.19 us -> 4.99 us  [push(): return lax.ppermute(array, ('y', 'c'), pairs)]
  transfers between devices with their start and end apart: 34 -> 34, of which waited for: 14 -> 13; matrix products, arithmetic and copies ran while one was open for 6% -> 6% of each run, Pallas kernels for 28% -> 27%
where the time goes in v4:
time: 161 us; the launch traced here: 160 us
  starting transfers between devices  70.8 us (44%)
  Pallas kernels  48.7 us (30%)
  waiting for transfers between devices  25.8 us (16%)
  other arithmetic  8.61 us (5%)
  local copies, waits for them, and re-layouts  6.19 us (4%)
    ppermute x7, starting transfers between devices, swap(): return lax.ppermute(array, 'c', [(0, 1), (1, 0)])  26.5 us
    ppermute x12, starting transfers between devices, push(): return lax.ppermute(array, ('y', 'c'), pairs)  22.7 us
    ppermute x15, starting transfers between devices, fetch_mixed(): return lax.ppermute(array, ('x', 'z', 'c'), pairs)  21.6 us
    ppermute x15, waiting for transfers between devices, fetch_mixed(): return lax.ppermute(array, ('x', 'z', 'c'), pairs)  19.5 us
    pallas_call x4, Pallas kernels, project(): pl.pallas_call(project_body, grid_spec=pltpu.PrefetchScalarGridSpec(num_s...  18.6 us
    pallas_call x2, Pallas kernels, local_attention(): pl.pallas_call(local_body, grid=(heads,), in_specs=[source, source, sourc...  11.4 us
    pallas_call x2, Pallas kernels, norm(): pl.pallas_call(norm_body, grid_spec=pltpu.PrefetchScalarGridSpec(num_scal...  8.46 us
    convert_element_type x4, other arithmetic, settle_chunk(): return (rows(c), swap(rows(1 - c).astype(BF16)))  5.82 us
  transfers between devices with their start and end apart: 34, of which 13 were waited for; matrix products, arithmetic and copies ran while one was open for 6% of the time, Pallas kernels for 27%

profile of v4, /device:TPU:1, one launch (start us, length us, event | category | flops | bytes accessed | tf_op | source)
XLA Modules:
  0.0 160.3 jit_solution(598026679491450288)
XLA Ops:
  0.0 1.7 %constant_dynamic-slice_fusion = (bf16[1024,192]{1,0:T(8,128)(2,1)S(1)}, bf16[1024,192]{1,0:T(8,128)(2,1)S(1)}) fusion(bf16[1024,384]{1,0:T(8,128)(2,1)} %param.10, s32[]{:T(128)S(6)} %select_n.188, s32[]{:T(128)S(6)} %select_n.187), kind=kLoop, calls=%fused_computation.18 | loop fusion | bytes 1572872 | tf_op jit(solution)/shard_map/dynamic-slice.1
  1.9 1.5 collective-permute-start.1
  3.6 4.7 %span_state.1 = (bf16[1024,1024]{1,0:T(8,128)(2,1)}, bf16[64,2048]{1,0:T(8,128)(2,1)}) custom-call(bf16[1024,1024]{1,0:T(8,128)(2,1)} %k_ref, bf16[1024,1024]{1,0:T(8,128)(2,1)} %v_ref.5), custom_call_target="tpu_custom_call" | custom-call | tf_op jit(solution)/shard_map/span_state/pallas_call | solution.py:45
  8.4 1.0 pad_maximum_fusion.1
  9.4 1.3 collective-permute-start.3
  10.6 1.4 collective-permute-start.2
  12.0 1.6 %collective-permute-start.5 = (bf16[64,2048]{1,0:T(8,128)(2,1)S(1)}, bf16[64,2048]{1,0:T(8,128)(2,1)S(1)}, u32[]{:S(2)}, u32[]{:S(2)}) collective-permute-start(bf16[64,2048]{1,0:T(8,128)(2,1)S(1)} %copy-done.16), channel_id=1, source_target_pairs={{16,0},{65,1},{24,8},{73,9},{0,16},{81,17},{8,24},{89,25},{48,32},... | collective-permute-start | bytes 786440 | tf_op jit(solution)/shard_map/ppermute | solution.py:264
  14.0 2.4 %collective-permute-start = (bf16[64,2048]{1,0:T(8,128)(2,1)S(1)}, bf16[64,2048]{1,0:T(8,128)(2,1)S(1)}, u32[]{:S(2)}, u32[]{:S(2)}) collective-permute-start(bf16[64,2048]{1,0:T(8,128)(2,1)S(1)} %copy-done.16), channel_id=1, source_target_pairs={{8,0},{33,1},{16,8},{41,9},{24,16},{49,17},{0,24},{57,25},{40,32},... | collective-permute-start | bytes 786440 | tf_op jit(solution)/shard_map/ppermute | solution.py:264
  16.3 5.7 %local_attention.2 = (bf16[1024,512]{1,0:T(8,128)(2,1)}, f32[1024,512]{1,0:T(8,128)}) custom-call(bf16[1024,1024]{1,0:T(8,128)(2,1)} %q_ref.2, bf16[1024,1024]{1,0:T(8,128)(2,1)} %get-tuple-element.53.kact_ref, bf16[1024,1024]{1,0:T(8,128)(2,1)} %v_ref.5), custom_call_target="tpu_custom_call" | custom-call | tf_op jit(solution)/shard_map/local_attention/pallas_call | solution.py:84
  22.7 3.1 %collective-permute-done.5.z3 = bf16[64,2048]{1,0:T(8,128)(2,1)S(1)} collective-permute-done((bf16[64,2048]{1,0:T(8,128)(2,1)S(1)}, bf16[64,2048]{1,0:T(8,128)(2,1)S(1)}, u32[]{:S(2)}, u32[]{:S(2)}) %collective-permute-start.5) | collective-permute-done | bytes 262176 | tf_op jit(solution)/shard_map/ppermute | solution.py:264
  25.8 1.7 %collective-permute-done.4.z2 = bf16[64,2048]{1,0:T(8,128)(2,1)S(1)} collective-permute-done((bf16[64,2048]{1,0:T(8,128)(2,1)S(1)}, bf16[64,2048]{1,0:T(8,128)(2,1)S(1)}, u32[]{:S(2)}, u32[]{:S(2)}) %collective-permute-start.4) | collective-permute-done | bytes 262176 | tf_op jit(solution)/shard_map/ppermute | solution.py:264
  28.9 2.4 %messages.1 = (bf16[64,2048]{1,0:T(8,128)(2,1)}, bf16[64,2048]{1,0:T(8,128)(2,1)}, bf16[64,2048]{1,0:T(8,128)(2,1)}) custom-call(s32[15]{0:T(128)} %stack.156.tab_ref, bf16[64,2048]{1,0:T(8,128)(2,1)} %get-tuple-element.56.state_ref, bf16[64,2048]{1,0:T(8,128)(2,1)} %copy-done.8, bf16[64,2048]{1,0:T(8,128)(2,1)} %copy-done.7, bf16[64,2048]{1,0:T(8,128)(2,1)} %copy-done.6), custom_call_target="tpu_custom_call" | custom-call | tf_op jit(solution)/shard_map/messages/pallas_call | solution.py:112
  31.3 3.8 %collective-permute-start.6 = (bf16[64,2048]{1,0:T(8,128)(2,1)}, bf16[64,2048]{1,0:T(8,128)(2,1)S(1)}, u32[]{:S(2)}, u32[]{:S(2)}) collective-permute-start(bf16[64,2048]{1,0:T(8,128)(2,1)} %get-tuple-element.61), channel_id=1, source_target_pairs={{32,0},{9,1},{40,8},{17,9},{48,16},{25,17},{56,24},{1,25},{64,32},... | collective-permute-start | bytes 786440 | tf_op jit(solution)/shard_map/ppermute | solution.py:264
  35.2 1.2 collective-permute-start.8
  36.4 5.7 %local_attention.3 = (bf16[1024,512]{1,0:T(8,128)(2,1)}, f32[1024,512]{1,0:T(8,128)}) custom-call(bf16[1024,1024]{1,0:T(8,128)(2,1)} %q_ref.2, bf16[1024,1024]{1,0:T(8,128)(2,1)} %get-tuple-element.53.kact_ref, bf16[1024,1024]{1,0:T(8,128)(2,1)} %v_ref.5), custom_call_target="tpu_custom_call" | custom-call | tf_op jit(solution)/shard_map/local_attention/pallas_call | solution.py:84
  42.1 1.2 pad_maximum_fusion.refs_4_.refs_5_
  43.5 1.4 collective-permute-done.7.x2
  45.5 2.1 %collective-permute-start.11 = (bf16[384,2048]{1,0:T(8,128)(2,1)S(1)}, bf16[384,2048]{1,0:T(8,128)(2,1)}, u32[]{:S(2)}, u32[]{:S(2)}) collective-permute-start(bf16[384,2048]{1,0:T(8,128)(2,1)S(1)} %pad_maximum_fusion.refs_4_.refs_5_), channel_id=1, source_target_pairs={{32,0},{9,1},{40,8},{17,9},{48,16},{25,17},{56,24},{1,25},{64,32},... | collective-permute-start | bytes 4718600 | tf_op jit(solution)/shard_map/ppermute | solution.py:264
  47.7 1.5 collective-permute-start.14
  49.2 4.2 %norm.2.refs_0_ = bf16[1024,512]{1,0:T(8,128)(2,1)} custom-call(s32[15]{0:T(128)} %stack.156.tab_ref, bf16[1024,512]{1,0:T(8,128)(2,1)} %get-tuple-element.54.q_ref, f32[1024,512]{1,0:T(8,128)} %get-tuple-element.55.local_ref, f32[1,1024]{1,0:T(1,128)} %bitcast.37, bf16[64,2048]{1,0:T(8,128)(2,1)} %copy-done.8, bf16[64,2048]{1,0:T(8,128)(2,1)} %copy-done.7, ...), custom_call_target="tpu_custom_call" | custom-call | tf_op jit(solution)/shard_map/norm/pallas_call | solution.py:154
  53.4 3.4 %collective-permute-start.9 = (bf16[1024,512]{1,0:T(8,128)(2,1)}, bf16[1024,512]{1,0:T(8,128)(2,1)S(1)}, u32[]{:S(2)}, u32[]{:S(2)}) collective-permute-start(bf16[1024,512]{1,0:T(8,128)(2,1)} %norm.2.refs_0_), channel_id=1, source_target_pairs={{0,1},{1,0},{2,3},{3,2},{4,5},{5,4},{6,7},{7,6},{8,9},{9,8},{10,11... | collective-permute-start | bytes 3145736 | tf_op jit(solution)/shard_map/ppermute | solution.py:268
  56.8 4.3 %norm.3.refs_1_ = bf16[1024,512]{1,0:T(8,128)(2,1)} custom-call(s32[15]{0:T(128)} %stack.156.tab_ref, bf16[1024,512]{1,0:T(8,128)(2,1)} %get-tuple-element.63.q_ref, f32[1024,512]{1,0:T(8,128)} %get-tuple-element.70.local_ref, f32[1,1024]{1,0:T(1,128)} %bitcast.38, bf16[64,2048]{1,0:T(8,128)(2,1)} %copy-done.8, bf16[64,2048]{1,0:T(8,128)(2,1)} %copy-done.7, ...), custom_call_target="tpu_custom_call" | custom-call | tf_op jit(solution)/shard_map/norm/pallas_call | solution.py:154
  61.3 7.9 %collective-permute-done.14 = bf16[192,2048]{1,0:T(8,128)(2,1)} collective-permute-done((bf16[192,2048]{1,0:T(8,128)(2,1)}, bf16[192,2048]{1,0:T(8,128)(2,1)}, u32[]{:S(2)}, u32[]{:S(2)}) %collective-permute-start.14) | collective-permute-done | bytes 786464 | tf_op jit(solution)/shard_map/ppermute | solution.py:264
  69.1 1.2 constant_dynamic-update-slice_fusion.refs_6_.refs_7_
  70.3 4.0 %collective-permute-done.12.refs_6_.refs_7_ = bf16[384,2048]{1,0:T(8,128)(2,1)} collective-permute-done((bf16[384,2048]{1,0:T(8,128)(2,1)S(1)}, bf16[384,2048]{1,0:T(8,128)(2,1)}, u32[]{:S(2)}, u32[]{:S(2)}) %collective-permute-start.12) | collective-permute-done | bytes 1572896 | tf_op jit(solution)/shard_map/ppermute | solution.py:264
  74.3 2.7 %collective-permute-start.20 = (bf16[384,2048]{1,0:T(8,128)(2,1)S(1)}, bf16[384,2048]{1,0:T(8,128)(2,1)S(1)}, u32[]{:S(2)}, u32[]{:S(2)}) collective-permute-start(bf16[384,2048]{1,0:T(8,128)(2,1)S(1)} %constant_dynamic-update-slice_fusion.refs_6_.refs_7_), channel_id=1, source_target_pairs={{32,0},{9,1},{40,8},{17,9},{48,16},{25,17},{56,24},{1,25},{64,32},... | collective-permute-start | bytes 4718600 | tf_op jit(solution)/shard_map/ppermute | solution.py:264
  77.0 5.7 %project.4 = (bf16[256,768]{1,0:T(8,128)(2,1)S(1)}, bf16[256,768]{1,0:T(8,128)(2,1)S(1)}, bf16[256,768]{1,0:T(8,128)(2,1)S(1)}, bf16[256,768]{1,0:T(8,128)(2,1)S(1)}) custom-call(s32[1]{0:T(128)} %bitcast.16.core_ref, bf16[1024,512]{1,0:T(8,128)(2,1)S(1)} %copy-done, bf16[1024,512]{1,0:T(8,128)(2,1)S(1)} %copy-done.1, ...), custom_call_target="tpu_custom_call" | custom-call | tf_op jit(solution)/shard_map/project/pallas_call | solution.py:202
  82.7 2.8 %collective-permute-start.13 = (bf16[256,768]{1,0:T(8,128)(2,1)S(1)}, bf16[256,768]{1,0:T(8,128)(2,1)S(1)}, u32[]{:S(2)}, u32[]{:S(2)}) collective-permute-start(bf16[256,768]{1,0:T(8,128)(2,1)S(1)} %get-tuple-element.74), channel_id=1, source_target_pairs={{0,2},{1,7},{2,4},{3,1},{4,6},{5,3},{6,0},{7,5},{8,10},{9,15},{10,... | collective-permute-start | bytes 1179656 | tf_op jit(solution)/shard_map/ppermute | solution.py:276
  85.5 4.0 %project.5 = (bf16[256,768]{1,0:T(8,128)(2,1)S(1)}, bf16[256,768]{1,0:T(8,128)(2,1)S(1)}, bf16[256,768]{1,0:T(8,128)(2,1)S(1)}, bf16[256,768]{1,0:T(8,128)(2,1)S(1)}) custom-call(s32[1]{0:T(128)} %bitcast.16.core_ref, bf16[1024,512]{1,0:T(8,128)(2,1)S(1)} %copy-done, bf16[1024,512]{1,0:T(8,128)(2,1)S(1)} %copy-done.1, ...), custom_call_target="tpu_custom_call" | custom-call | tf_op jit(solution)/shard_map/project/pallas_call | solution.py:202
  90.3 3.5 %collective-permute-start.15 = (bf16[256,768]{1,0:T(8,128)(2,1)S(1)}, bf16[256,768]{1,0:T(8,128)(2,1)S(1)}, u32[]{:S(2)}, u32[]{:S(2)}) collective-permute-start(bf16[256,768]{1,0:T(8,128)(2,1)S(1)} %add_convert_fusion.5), channel_id=1, source_target_pairs={{0,2},{1,7},{2,4},{3,1},{4,6},{5,3},{6,0},{7,5},{8,10},{9,15},{10,... | collective-permute-start | bytes 1179656 | tf_op jit(solution)/shard_map/ppermute | solution.py:276
  93.9 1.2 collective-permute-done.21.refs_6_.refs_7_
  95.1 2.7 %collective-permute-start.25 = (bf16[384,2048]{1,0:T(8,128)(2,1)}, bf16[384,2048]{1,0:T(8,128)(2,1)S(1)}, u32[]{:S(2)}, u32[]{:S(2)}) collective-permute-start(bf16[384,2048]{1,0:T(8,128)(2,1)} %collective-permute-done.11.refs_4_.refs_5_), channel_id=1, source_target_pairs={{32,0},{9,1},{40,8},{17,9},{48,16},{25,17},{56,24},{1,25},{64,32},... | collective-permute-start | bytes 4718600 | tf_op jit(solution)/shard_map/ppermute | solution.py:264
  97.8 4.0 %project.6 = (bf16[256,768]{1,0:T(8,128)(2,1)S(1)}, bf16[256,768]{1,0:T(8,128)(2,1)S(1)}, bf16[256,768]{1,0:T(8,128)(2,1)S(1)}, bf16[256,768]{1,0:T(8,128)(2,1)S(1)}) custom-call(s32[1]{0:T(128)} %bitcast.16.core_ref, bf16[1024,512]{1,0:T(8,128)(2,1)S(1)} %copy-done, bf16[1024,512]{1,0:T(8,128)(2,1)S(1)} %copy-done.1, ...), custom_call_target="tpu_custom_call" | custom-call | tf_op jit(solution)/shard_map/project/pallas_call | solution.py:202
  101.8 2.8 %collective-permute-start.22 = (bf16[256,768]{1,0:T(8,128)(2,1)S(1)}, bf16[256,768]{1,0:T(8,128)(2,1)S(1)}, u32[]{:S(2)}, u32[]{:S(2)}) collective-permute-start(bf16[256,768]{1,0:T(8,128)(2,1)S(1)} %get-tuple-element.89), channel_id=1, source_target_pairs={{0,2},{1,7},{2,4},{3,1},{4,6},{5,3},{6,0},{7,5},{8,10},{9,15},{10,... | collective-permute-start | bytes 1179656 | tf_op jit(solution)/shard_map/ppermute | solution.py:276
  104.7 1.3 collective-permute-start.18
  106.0 3.3 %collective-permute-done.22 = bf16[256,768]{1,0:T(8,128)(2,1)S(1)} collective-permute-done((bf16[256,768]{1,0:T(8,128)(2,1)S(1)}, bf16[256,768]{1,0:T(8,128)(2,1)S(1)}, u32[]{:S(2)}, u32[]{:S(2)}) %collective-permute-start.22) | collective-permute-done | bytes 393248 | tf_op jit(solution)/shard_map/ppermute | solution.py:276
  109.5 3.7 %collective-permute-start.23 = (bf16[256,768]{1,0:T(8,128)(2,1)S(1)}, bf16[256,768]{1,0:T(8,128)(2,1)S(1)}, u32[]{:S(2)}, u32[]{:S(2)}) collective-permute-start(bf16[256,768]{1,0:T(8,128)(2,1)S(1)} %add_convert_fusion.1), channel_id=1, source_target_pairs={{0,2},{1,7},{2,4},{3,1},{4,6},{5,3},{6,0},{7,5},{8,10},{9,15},{10,... | collective-permute-start | bytes 1179656 | tf_op jit(solution)/shard_map/ppermute | solution.py:276
  113.7 3.5 %collective-permute-start.19 = (bf16[256,768]{1,0:T(8,128)(2,1)S(1)}, bf16[256,768]{1,0:T(8,128)(2,1)S(1)}, u32[]{:S(2)}, u32[]{:S(2)}) collective-permute-start(bf16[256,768]{1,0:T(8,128)(2,1)S(1)} %add_convert_fusion.2), channel_id=1, source_target_pairs={{0,2},{1,7},{2,4},{3,1},{4,6},{5,3},{6,0},{7,5},{8,10},{9,15},{10,... | collective-permute-start | bytes 1179656 | tf_op jit(solution)/shard_map/ppermute | solution.py:276
  118.0 3.5 %collective-permute-start.24 = (bf16[256,768]{1,0:T(8,128)(2,1)S(1)}, bf16[256,768]{1,0:T(8,128)(2,1)}, u32[]{:S(2)}, u32[]{:S(2)}) collective-permute-start(bf16[256,768]{1,0:T(8,128)(2,1)S(1)} %add_convert_fusion), channel_id=1, source_target_pairs={{0,2},{1,7},{2,4},{3,1},{4,6},{5,3},{6,0},{7,5},{8,10},{9,15},{10,... | collective-permute-start | bytes 1179656 | tf_op jit(solution)/shard_map/ppermute | solution.py:276
  121.5 4.8 %project.7 = (bf16[256,768]{1,0:T(8,128)(2,1)}, bf16[256,768]{1,0:T(8,128)(2,1)}, bf16[256,768]{1,0:T(8,128)(2,1)}, bf16[256,768]{1,0:T(8,128)(2,1)S(1)}) custom-call(s32[1]{0:T(128)} %bitcast.16.core_ref, bf16[1024,512]{1,0:T(8,128)(2,1)S(1)} %copy-done, bf16[1024,512]{1,0:T(8,128)(2,1)S(1)} %copy-done.1, ...), custom_call_target="tpu_custom_call" | custom-call | tf_op jit(solution)/shard_map/project/pallas_call | solution.py:202
  127.7 0.8 collective-permute-start.29
  129.3 6.8 %collective-permute-start.30 = (bf16[128,768]{1,0:T(8,128)(2,1)}, bf16[128,768]{1,0:T(8,128)(2,1)S(1)}, u32[]{:S(2)}, u32[]{:S(2)}) collective-permute-start(bf16[128,768]{1,0:T(8,128)(2,1)} %get-tuple-element.105), channel_id=1, source_target_pairs={{0,1},{1,0},{2,3},{3,2},{4,5},{5,4},{6,7},{7,6},{8,9},{9,8},{10,11... | collective-permute-start | bytes 589832 | tf_op jit(solution)/shard_map/ppermute | solution.py:268
  136.9 11.4 %collective-permute-start.31 = (bf16[128,768]{1,0:T(8,128)(2,1)}, bf16[128,768]{1,0:T(8,128)(2,1)S(1)}, u32[]{:S(2)}, u32[]{:S(2)}) collective-permute-start(bf16[128,768]{1,0:T(8,128)(2,1)} %get-tuple-element.103), channel_id=1, source_target_pairs={{0,1},{1,0},{2,3},{3,2},{4,5},{5,4},{6,7},{7,6},{8,9},{9,8},{10,11... | collective-permute-start | bytes 589832 | tf_op jit(solution)/shard_map/ppermute | solution.py:268
  148.3 2.1 %add_convert_fusion.7 = (bf16[128,768]{1,0:T(8,128)(2,1)}, f32[128,768]{1,0:T(8,128)S(1)}) fusion(bf16[256,768]{1,0:T(8,128)(2,1)} %collective-permute-done.24, s32[]{:T(128)S(6)} %select_n.190, bf16[256,768]{1,0:T(8,128)(2,1)} %copy-done.3, s32[]{:T(128)S(6)} %select_n.189), kind=kLoop, calls=%fused_computation.9 | loop fusion | flops 688128 | bytes 1376264 | tf_op jit(solution)/shard_map/convert_element_type | solution.py:290
  150.4 2.2 %add_convert_fusion.6 = (bf16[128,768]{1,0:T(8,128)(2,1)}, f32[128,768]{1,0:T(8,128)S(1)}) fusion(bf16[256,768]{1,0:T(8,128)(2,1)} %collective-permute-done.29, s32[]{:T(128)S(6)} %select_n.190, bf16[256,768]{1,0:T(8,128)(2,1)} %collective-permute-done.28, bf16[256,768]{1,0:T(8,128)(2,1)} %collective-permute-done.27, bf16[256,768]{1,0:T(8,128)(2,1)S(1)} %copy-done.5, ...), kind=kLoop, calls=%fused_computation.8 | loop fusion | flops 1474560 | bytes 2162696 | tf_op jit(solution)/shard_map/convert_element_type | solution.py:290
  152.7 3.2 %collective-permute-start.33 = (bf16[128,768]{1,0:T(8,128)(2,1)}, bf16[128,768]{1,0:T(8,128)(2,1)}, u32[]{:S(2)}, u32[]{:S(2)}) collective-permute-start(bf16[128,768]{1,0:T(8,128)(2,1)} %get-tuple-element.99), channel_id=1, source_target_pairs={{0,1},{1,0},{2,3},{3,2},{4,5},{5,4},{6,7},{7,6},{8,9},{9,8},{10,11... | collective-permute-start | bytes 589832 | tf_op jit(solution)/shard_map/ppermute | solution.py:268
  156.0 1.3 collective-permute-done.33.refs_7_
  157.3 3.0 %finish.1 = bf16[128,6144]{1,0:T(8,128)(2,1)} custom-call(s32[17]{0:T(128)S(1)} %stack.135.tab_ref, bf16[128,6144]{1,0:T(8,128)(2,1)S(1)} %copy-done.2, f32[128,768]{1,0:T(8,128)S(1)} %get-tuple-element.106.refs_0_, f32[128,768]{1,0:T(8,128)S(1)} %get-tuple-element.104.refs_1_, f32[128,768]{1,0:T(8,128)S(1)} %get-tuple-element.102.refs_2_, ...), custom_call_target="tpu_custom_call" | custom-call | tf_op jit(solution)/shard_map/finish/pallas_call | solution.py:239
  (84 shorter events, 9.2 us)
Async XLA Ops:
  1.9 6.4 %collective-permute-start.1 = (bf16[192,1024]{1,0:T(8,128)(2,1)S(1)}, bf16[192,1024]{1,0:T(8,128)(2,1)S(1)}, u32[]{:S(2)}, u32[]{:S(2)}) collective-permute-start(bf16[192,1024]{1,0:T(8,128)(2,1)S(1)} %bitcast.36), channel_id=1, source_target_pairs={{0,1},{1,0},{2,3},{3,2},{4,5},{5,4},{6,7},{7,6},{8,9},{9,8},{10,11... | collective-permute-start | bytes 1179656 | tf_op jit(solution)/shard_map/ppermute | solution.py:268
  8.4 3.7 %copy-start.16 = (bf16[64,2048]{1,0:T(8,128)(2,1)S(1)}, bf16[64,2048]{1,0:T(8,128)(2,1)}, u32[]{:S(2)}) copy-start(bf16[64,2048]{1,0:T(8,128)(2,1)} %get-tuple-element.56.state_ref) | copy-start | bytes 786436
  8.4 13.7 %copy-start.9 = (bf16[192,1024]{1,0:T(8,128)(2,1)}, bf16[192,1024]{1,0:T(8,128)(2,1)S(1)}, u32[]{:S(2)}) copy-start(bf16[192,1024]{1,0:T(8,128)(2,1)S(1)} %collective-permute-done.1) | copy-start | bytes 1179652
  9.4 16.5 %collective-permute-start.3 = (bf16[192,2048]{1,0:T(8,128)(2,1)}, bf16[192,2048]{1,0:T(8,128)(2,1)S(1)}, u32[]{:S(2)}, u32[]{:S(2)}) collective-permute-start(bf16[192,2048]{1,0:T(8,128)(2,1)} %pad_maximum_fusion.1), channel_id=1, source_target_pairs={{24,0},{97,1},{0,8},{105,9},{8,16},{113,17},{16,24},{121,25},{56,3... | collective-permute-start | bytes 2359304 | tf_op jit(solution)/shard_map/ppermute | solution.py:264
  10.6 15.2 %collective-permute-start.2 = (bf16[192,2048]{1,0:T(8,128)(2,1)}, bf16[192,2048]{1,0:T(8,128)(2,1)}, u32[]{:S(2)}, u32[]{:S(2)}) collective-permute-start(bf16[192,2048]{1,0:T(8,128)(2,1)} %pad_maximum_fusion.1), channel_id=1, source_target_pairs={{8,0},{33,1},{16,8},{41,9},{24,16},{49,17},{0,24},{57,25},{40,32},... | collective-permute-start | bytes 2359304 | tf_op jit(solution)/shard_map/ppermute | solution.py:264
  12.0 13.8 %collective-permute-start.5 = (bf16[64,2048]{1,0:T(8,128)(2,1)S(1)}, bf16[64,2048]{1,0:T(8,128)(2,1)S(1)}, u32[]{:S(2)}, u32[]{:S(2)}) collective-permute-start(bf16[64,2048]{1,0:T(8,128)(2,1)S(1)} %copy-done.16), channel_id=1, source_target_pairs={{16,0},{65,1},{24,8},{73,9},{0,16},{81,17},{8,24},{89,25},{48,32},... | collective-permute-start | bytes 786440 | tf_op jit(solution)/shard_map/ppermute | solution.py:264
  13.7 13.9 %collective-permute-start.4 = (bf16[64,2048]{1,0:T(8,128)(2,1)S(1)}, bf16[64,2048]{1,0:T(8,128)(2,1)S(1)}, u32[]{:S(2)}, u32[]{:S(2)}) collective-permute-start(bf16[64,2048]{1,0:T(8,128)(2,1)S(1)} %copy-done.16), channel_id=1, source_target_pairs={{24,0},{97,1},{0,8},{105,9},{8,16},{113,17},{16,24},{121,25},{56,3... | collective-permute-start | bytes 786440 | tf_op jit(solution)/shard_map/ppermute | solution.py:264
  14.0 13.7 %collective-permute-start = (bf16[64,2048]{1,0:T(8,128)(2,1)S(1)}, bf16[64,2048]{1,0:T(8,128)(2,1)S(1)}, u32[]{:S(2)}, u32[]{:S(2)}) collective-permute-start(bf16[64,2048]{1,0:T(8,128)(2,1)S(1)} %copy-done.16), channel_id=1, source_target_pairs={{8,0},{33,1},{16,8},{41,9},{24,16},{49,17},{0,24},{57,25},{40,32},... | collective-permute-start | bytes 786440 | tf_op jit(solution)/shard_map/ppermute | solution.py:264
  25.8 1.8 %copy-start.6 = (bf16[64,2048]{1,0:T(8,128)(2,1)}, bf16[64,2048]{1,0:T(8,128)(2,1)S(1)}, u32[]{:S(2)}) copy-start(bf16[64,2048]{1,0:T(8,128)(2,1)S(1)} %collective-permute-done.5.z3) | copy-start | bytes 786436
  25.8 10.5 %copy-start.14 = (bf16[192,2048]{1,0:T(8,128)(2,1)}, bf16[192,2048]{1,0:T(8,128)(2,1)S(1)}, u32[]{:S(2)}) copy-start(bf16[192,2048]{1,0:T(8,128)(2,1)S(1)} %collective-permute-done.3) | copy-start | bytes 2359300
  31.3 13.6 %collective-permute-start.6 = (bf16[64,2048]{1,0:T(8,128)(2,1)}, bf16[64,2048]{1,0:T(8,128)(2,1)S(1)}, u32[]{:S(2)}, u32[]{:S(2)}) collective-permute-start(bf16[64,2048]{1,0:T(8,128)(2,1)} %get-tuple-element.61), channel_id=1, source_target_pairs={{32,0},{9,1},{40,8},{17,9},{48,16},{25,17},{56,24},{1,25},{64,32},... | collective-permute-start | bytes 786440 | tf_op jit(solution)/shard_map/ppermute | solution.py:264
  35.2 9.7 %collective-permute-start.7 = (bf16[64,2048]{1,0:T(8,128)(2,1)}, bf16[64,2048]{1,0:T(8,128)(2,1)S(1)}, u32[]{:S(2)}, u32[]{:S(2)}) collective-permute-start(bf16[64,2048]{1,0:T(8,128)(2,1)} %get-tuple-element.65), channel_id=1, source_target_pairs={{96,0},{25,1},{104,8},{1,9},{112,16},{9,17},{120,24},{17,25},{0,32... | collective-permute-start | bytes 786440 | tf_op jit(solution)/shard_map/ppermute | solution.py:264
  35.2 6.9 %copy-start.10 = (bf16[192,1024]{1,0:T(8,128)(2,1)S(1)}, bf16[192,1024]{1,0:T(8,128)(2,1)}, u32[]{:S(2)}) copy-start(bf16[192,1024]{1,0:T(8,128)(2,1)} %copy-done.9) | copy-start | bytes 1179652
  35.2 8.3 %collective-permute-start.8 = (bf16[64,2048]{1,0:T(8,128)(2,1)}, bf16[64,2048]{1,0:T(8,128)(2,1)S(1)}, u32[]{:S(2)}, u32[]{:S(2)}) collective-permute-start(bf16[64,2048]{1,0:T(8,128)(2,1)} %get-tuple-element.67), channel_id=1, source_target_pairs={{64,0},{17,1},{72,8},{25,9},{80,16},{1,17},{88,24},{9,25},{96,32},... | collective-permute-start | bytes 786440 | tf_op jit(solution)/shard_map/ppermute | solution.py:264
  43.5 5.7 %copy-start.13 = (bf16[64,2048]{1,0:T(8,128)(2,1)}, bf16[64,2048]{1,0:T(8,128)(2,1)S(1)}, u32[]{:S(2)}) copy-start(bf16[64,2048]{1,0:T(8,128)(2,1)S(1)} %collective-permute-done.8.x3) | copy-start | bytes 786436
  44.9 4.3 %copy-start.12 = (bf16[64,2048]{1,0:T(8,128)(2,1)}, bf16[64,2048]{1,0:T(8,128)(2,1)S(1)}, u32[]{:S(2)}) copy-start(bf16[64,2048]{1,0:T(8,128)(2,1)S(1)} %collective-permute-done.7.x2) | copy-start | bytes 786436
  44.9 4.3 %copy-start.11 = (bf16[64,2048]{1,0:T(8,128)(2,1)}, bf16[64,2048]{1,0:T(8,128)(2,1)S(1)}, u32[]{:S(2)}) copy-start(bf16[64,2048]{1,0:T(8,128)(2,1)S(1)} %collective-permute-done.6.x1) | copy-start | bytes 786436
  44.9 29.4 %collective-permute-start.12 = (bf16[384,2048]{1,0:T(8,128)(2,1)S(1)}, bf16[384,2048]{1,0:T(8,128)(2,1)}, u32[]{:S(2)}, u32[]{:S(2)}) collective-permute-start(bf16[384,2048]{1,0:T(8,128)(2,1)S(1)} %pad_maximum_fusion.refs_4_.refs_5_), channel_id=1, source_target_pairs={{96,0},{25,1},{104,8},{1,9},{112,16},{9,17},{120,24},{17,25},{0,32... | collective-permute-start | bytes 4718600 | tf_op jit(solution)/shard_map/ppermute | solution.py:264
  45.5 28.8 %collective-permute-start.11 = (bf16[384,2048]{1,0:T(8,128)(2,1)S(1)}, bf16[384,2048]{1,0:T(8,128)(2,1)}, u32[]{:S(2)}, u32[]{:S(2)}) collective-permute-start(bf16[384,2048]{1,0:T(8,128)(2,1)S(1)} %pad_maximum_fusion.refs_4_.refs_5_), channel_id=1, source_target_pairs={{32,0},{9,1},{40,8},{17,9},{48,16},{25,17},{56,24},{1,25},{64,32},... | collective-permute-start | bytes 4718600 | tf_op jit(solution)/shard_map/ppermute | solution.py:264
  47.7 21.4 %collective-permute-start.14 = (bf16[192,2048]{1,0:T(8,128)(2,1)}, bf16[192,2048]{1,0:T(8,128)(2,1)}, u32[]{:S(2)}, u32[]{:S(2)}) collective-permute-start(bf16[192,2048]{1,0:T(8,128)(2,1)} %pad_maximum_fusion.1), channel_id=1, source_target_pairs={{16,0},{65,1},{24,8},{73,9},{0,16},{81,17},{8,24},{89,25},{48,32},... | collective-permute-start | bytes 2359304 | tf_op jit(solution)/shard_map/ppermute | solution.py:264
  53.4 23.6 %collective-permute-start.9 = (bf16[1024,512]{1,0:T(8,128)(2,1)}, bf16[1024,512]{1,0:T(8,128)(2,1)S(1)}, u32[]{:S(2)}, u32[]{:S(2)}) collective-permute-start(bf16[1024,512]{1,0:T(8,128)(2,1)} %norm.2.refs_0_), channel_id=1, source_target_pairs={{0,1},{1,0},{2,3},{3,2},{4,5},{5,4},{6,7},{7,6},{8,9},{9,8},{10,11... | collective-permute-start | bytes 3145736 | tf_op jit(solution)/shard_map/ppermute | solution.py:268
  56.8 4.4 %copy-start.15 = (bf16[192,2048]{1,0:T(8,128)(2,1)S(1)}, bf16[192,2048]{1,0:T(8,128)(2,1)}, u32[]{:S(2)}) copy-start(bf16[192,2048]{1,0:T(8,128)(2,1)} %copy-done.14) | copy-start | bytes 2359300
  61.1 15.9 %copy-start = (bf16[1024,512]{1,0:T(8,128)(2,1)S(1)}, bf16[1024,512]{1,0:T(8,128)(2,1)}, u32[]{:S(2)}) copy-start(bf16[1024,512]{1,0:T(8,128)(2,1)} %norm.2.refs_0_) | copy-start | bytes 3145732
  61.1 15.9 %copy-start.1 = (bf16[1024,512]{1,0:T(8,128)(2,1)S(1)}, bf16[1024,512]{1,0:T(8,128)(2,1)}, u32[]{:S(2)}) copy-start(bf16[1024,512]{1,0:T(8,128)(2,1)} %norm.3.refs_1_) | copy-start | bytes 3145732
  61.1 15.9 %collective-permute-start.10 = (bf16[1024,512]{1,0:T(8,128)(2,1)}, bf16[1024,512]{1,0:T(8,128)(2,1)S(1)}, u32[]{:S(2)}, u32[]{:S(2)}) collective-permute-start(bf16[1024,512]{1,0:T(8,128)(2,1)} %norm.3.refs_1_), channel_id=1, source_target_pairs={{0,1},{1,0},{2,3},{3,2},{4,5},{5,4},{6,7},{7,6},{8,9},{9,8},{10,11... | collective-permute-start | bytes 3145736 | tf_op jit(solution)/shard_map/ppermute | solution.py:268
  74.3 20.8 %collective-permute-start.21 = (bf16[384,2048]{1,0:T(8,128)(2,1)S(1)}, bf16[384,2048]{1,0:T(8,128)(2,1)S(1)}, u32[]{:S(2)}, u32[]{:S(2)}) collective-permute-start(bf16[384,2048]{1,0:T(8,128)(2,1)S(1)} %constant_dynamic-update-slice_fusion.refs_6_.refs_7_), channel_id=1, source_target_pairs={{96,0},{25,1},{104,8},{1,9},{112,16},{9,17},{120,24},{17,25},{0,32... | collective-permute-start | bytes 4718600 | tf_op jit(solution)/shard_map/ppermute | solution.py:264
  74.3 20.8 %collective-permute-start.20 = (bf16[384,2048]{1,0:T(8,128)(2,1)S(1)}, bf16[384,2048]{1,0:T(8,128)(2,1)S(1)}, u32[]{:S(2)}, u32[]{:S(2)}) collective-permute-start(bf16[384,2048]{1,0:T(8,128)(2,1)S(1)} %constant_dynamic-update-slice_fusion.refs_6_.refs_7_), channel_id=1, source_target_pairs={{32,0},{9,1},{40,8},{17,9},{48,16},{25,17},{56,24},{1,25},{64,32},... | collective-permute-start | bytes 4718600 | tf_op jit(solution)/shard_map/ppermute | solution.py:264
  82.7 7.5 %collective-permute-start.13 = (bf16[256,768]{1,0:T(8,128)(2,1)S(1)}, bf16[256,768]{1,0:T(8,128)(2,1)S(1)}, u32[]{:S(2)}, u32[]{:S(2)}) collective-permute-start(bf16[256,768]{1,0:T(8,128)(2,1)S(1)} %get-tuple-element.74), channel_id=1, source_target_pairs={{0,2},{1,7},{2,4},{3,1},{4,6},{5,3},{6,0},{7,5},{8,10},{9,15},{10,... | collective-permute-start | bytes 1179656 | tf_op jit(solution)/shard_map/ppermute | solution.py:276
  90.3 11.5 %collective-permute-start.15 = (bf16[256,768]{1,0:T(8,128)(2,1)S(1)}, bf16[256,768]{1,0:T(8,128)(2,1)S(1)}, u32[]{:S(2)}, u32[]{:S(2)}) collective-permute-start(bf16[256,768]{1,0:T(8,128)(2,1)S(1)} %add_convert_fusion.5), channel_id=1, source_target_pairs={{0,2},{1,7},{2,4},{3,1},{4,6},{5,3},{6,0},{7,5},{8,10},{9,15},{10,... | collective-permute-start | bytes 1179656 | tf_op jit(solution)/shard_map/ppermute | solution.py:276
  93.8 10.8 %collective-permute-start.17 = (bf16[256,768]{1,0:T(8,128)(2,1)S(1)}, bf16[256,768]{1,0:T(8,128)(2,1)S(1)}, u32[]{:S(2)}, u32[]{:S(2)}) collective-permute-start(bf16[256,768]{1,0:T(8,128)(2,1)S(1)} %get-tuple-element.82), channel_id=1, source_target_pairs={{0,2},{1,7},{2,4},{3,1},{4,6},{5,3},{6,0},{7,5},{8,10},{9,15},{10,... | collective-permute-start | bytes 1179656 | tf_op jit(solution)/shard_map/ppermute | solution.py:276
  95.1 26.4 %collective-permute-start.25 = (bf16[384,2048]{1,0:T(8,128)(2,1)}, bf16[384,2048]{1,0:T(8,128)(2,1)S(1)}, u32[]{:S(2)}, u32[]{:S(2)}) collective-permute-start(bf16[384,2048]{1,0:T(8,128)(2,1)} %collective-permute-done.11.refs_4_.refs_5_), channel_id=1, source_target_pairs={{32,0},{9,1},{40,8},{17,9},{48,16},{25,17},{56,24},{1,25},{64,32},... | collective-permute-start | bytes 4718600 | tf_op jit(solution)/shard_map/ppermute | solution.py:264
  97.8 23.7 %collective-permute-start.26 = (bf16[384,2048]{1,0:T(8,128)(2,1)S(1)}, bf16[384,2048]{1,0:T(8,128)(2,1)S(1)}, u32[]{:S(2)}, u32[]{:S(2)}) collective-permute-start(bf16[384,2048]{1,0:T(8,128)(2,1)S(1)} %collective-permute-done.21.refs_6_.refs_7_), channel_id=1, source_target_pairs={{96,0},{25,1},{104,8},{1,9},{112,16},{9,17},{120,24},{17,25},{0,32... | collective-permute-start | bytes 4718600 | tf_op jit(solution)/shard_map/ppermute | solution.py:264
  101.8 19.7 %copy-start.3 = (bf16[256,768]{1,0:T(8,128)(2,1)}, bf16[256,768]{1,0:T(8,128)(2,1)S(1)}, u32[]{:S(2)}) copy-start(bf16[256,768]{1,0:T(8,128)(2,1)S(1)} %get-tuple-element.87) | copy-start | bytes 1179652
  101.8 7.5 %collective-permute-start.22 = (bf16[256,768]{1,0:T(8,128)(2,1)S(1)}, bf16[256,768]{1,0:T(8,128)(2,1)S(1)}, u32[]{:S(2)}, u32[]{:S(2)}) collective-permute-start(bf16[256,768]{1,0:T(8,128)(2,1)S(1)} %get-tuple-element.89), channel_id=1, source_target_pairs={{0,2},{1,7},{2,4},{3,1},{4,6},{5,3},{6,0},{7,5},{8,10},{9,15},{10,... | collective-permute-start | bytes 1179656 | tf_op jit(solution)/shard_map/ppermute | solution.py:276
  104.7 8.8 %collective-permute-start.18 = (bf16[256,768]{1,0:T(8,128)(2,1)S(1)}, bf16[256,768]{1,0:T(8,128)(2,1)S(1)}, u32[]{:S(2)}, u32[]{:S(2)}) collective-permute-start(bf16[256,768]{1,0:T(8,128)(2,1)S(1)} %add_convert_fusion.3), channel_id=1, source_target_pairs={{0,2},{1,7},{2,4},{3,1},{4,6},{5,3},{6,0},{7,5},{8,10},{9,15},{10,... | collective-permute-start | bytes 1179656 | tf_op jit(solution)/shard_map/ppermute | solution.py:276
  109.5 8.4 %collective-permute-start.23 = (bf16[256,768]{1,0:T(8,128)(2,1)S(1)}, bf16[256,768]{1,0:T(8,128)(2,1)S(1)}, u32[]{:S(2)}, u32[]{:S(2)}) collective-permute-start(bf16[256,768]{1,0:T(8,128)(2,1)S(1)} %add_convert_fusion.1), channel_id=1, source_target_pairs={{0,2},{1,7},{2,4},{3,1},{4,6},{5,3},{6,0},{7,5},{8,10},{9,15},{10,... | collective-permute-start | bytes 1179656 | tf_op jit(solution)/shard_map/ppermute | solution.py:276
  113.3 14.5 %collective-permute-start.16 = (bf16[256,768]{1,0:T(8,128)(2,1)S(1)}, bf16[256,768]{1,0:T(8,128)(2,1)S(1)}, u32[]{:S(2)}, u32[]{:S(2)}) collective-permute-start(bf16[256,768]{1,0:T(8,128)(2,1)S(1)} %add_convert_fusion.4), channel_id=1, source_target_pairs={{0,2},{1,7},{2,4},{3,1},{4,6},{5,3},{6,0},{7,5},{8,10},{9,15},{10,... | collective-permute-start | bytes 1179656 | tf_op jit(solution)/shard_map/ppermute | solution.py:276
  113.7 15.6 %collective-permute-start.19 = (bf16[256,768]{1,0:T(8,128)(2,1)S(1)}, bf16[256,768]{1,0:T(8,128)(2,1)S(1)}, u32[]{:S(2)}, u32[]{:S(2)}) collective-permute-start(bf16[256,768]{1,0:T(8,128)(2,1)S(1)} %add_convert_fusion.2), channel_id=1, source_target_pairs={{0,2},{1,7},{2,4},{3,1},{4,6},{5,3},{6,0},{7,5},{8,10},{9,15},{10,... | collective-permute-start | bytes 1179656 | tf_op jit(solution)/shard_map/ppermute | solution.py:276
  118.0 18.9 %collective-permute-start.24 = (bf16[256,768]{1,0:T(8,128)(2,1)S(1)}, bf16[256,768]{1,0:T(8,128)(2,1)}, u32[]{:S(2)}, u32[]{:S(2)}) collective-permute-start(bf16[256,768]{1,0:T(8,128)(2,1)S(1)} %add_convert_fusion), channel_id=1, source_target_pairs={{0,2},{1,7},{2,4},{3,1},{4,6},{5,3},{6,0},{7,5},{8,10},{9,15},{10,... | collective-permute-start | bytes 1179656 | tf_op jit(solution)/shard_map/ppermute | solution.py:276
  127.0 23.4 %collective-permute-start.27 = (bf16[256,768]{1,0:T(8,128)(2,1)}, bf16[256,768]{1,0:T(8,128)(2,1)}, u32[]{:S(2)}, u32[]{:S(2)}) collective-permute-start(bf16[256,768]{1,0:T(8,128)(2,1)} %get-tuple-element.96), channel_id=1, source_target_pairs={{0,4},{1,5},{2,6},{3,7},{4,0},{5,1},{6,2},{7,3},{8,12},{9,13},{10,... | collective-permute-start | bytes 1179656 | tf_op jit(solution)/shard_map/ppermute | solution.py:276
  127.0 23.4 %collective-permute-start.28 = (bf16[256,768]{1,0:T(8,128)(2,1)}, bf16[256,768]{1,0:T(8,128)(2,1)}, u32[]{:S(2)}, u32[]{:S(2)}) collective-permute-start(bf16[256,768]{1,0:T(8,128)(2,1)} %get-tuple-element.97), channel_id=1, source_target_pairs={{0,2},{1,7},{2,4},{3,1},{4,6},{5,3},{6,0},{7,5},{8,10},{9,15},{10,... | collective-permute-start | bytes 1179656 | tf_op jit(solution)/shard_map/ppermute | solution.py:276
  127.7 22.7 %collective-permute-start.29 = (bf16[256,768]{1,0:T(8,128)(2,1)}, bf16[256,768]{1,0:T(8,128)(2,1)}, u32[]{:S(2)}, u32[]{:S(2)}) collective-permute-start(bf16[256,768]{1,0:T(8,128)(2,1)} %get-tuple-element.98), channel_id=1, source_target_pairs={{0,6},{1,3},{2,0},{3,5},{4,2},{5,7},{6,4},{7,1},{8,14},{9,11},{10,... | collective-permute-start | bytes 1179656 | tf_op jit(solution)/shard_map/ppermute | solution.py:276
  129.3 21.2 %copy-start.5 = (bf16[256,768]{1,0:T(8,128)(2,1)S(1)}, bf16[256,768]{1,0:T(8,128)(2,1)}, u32[]{:S(2)}) copy-start(bf16[256,768]{1,0:T(8,128)(2,1)} %copy-done.4) | copy-start | bytes 1179652
  129.3 26.7 %collective-permute-start.30 = (bf16[128,768]{1,0:T(8,128)(2,1)}, bf16[128,768]{1,0:T(8,128)(2,1)S(1)}, u32[]{:S(2)}, u32[]{:S(2)}) collective-permute-start(bf16[128,768]{1,0:T(8,128)(2,1)} %get-tuple-element.105), channel_id=1, source_target_pairs={{0,1},{1,0},{2,3},{3,2},{4,5},{5,4},{6,7},{7,6},{8,9},{9,8},{10,11... | collective-permute-start | bytes 589832 | tf_op jit(solution)/shard_map/ppermute | solution.py:268
  136.9 19.1 %collective-permute-start.31 = (bf16[128,768]{1,0:T(8,128)(2,1)}, bf16[128,768]{1,0:T(8,128)(2,1)S(1)}, u32[]{:S(2)}, u32[]{:S(2)}) collective-permute-start(bf16[128,768]{1,0:T(8,128)(2,1)} %get-tuple-element.103), channel_id=1, source_target_pairs={{0,1},{1,0},{2,3},{3,2},{4,5},{5,4},{6,7},{7,6},{8,9},{9,8},{10,11... | collective-permute-start | bytes 589832 | tf_op jit(solution)/shard_map/ppermute | solution.py:268
  148.3 9.0 %copy-start.2 = (bf16[128,6144]{1,0:T(8,128)(2,1)S(1)}, bf16[128,6144]{1,0:T(8,128)(2,1)}, u32[]{:S(2)}) copy-start(bf16[128,6144]{1,0:T(8,128)(2,1)} %res_ref.1) | copy-start | bytes 4718596
  150.4 5.6 %collective-permute-start.32 = (bf16[128,768]{1,0:T(8,128)(2,1)}, bf16[128,768]{1,0:T(8,128)(2,1)}, u32[]{:S(2)}, u32[]{:S(2)}) collective-permute-start(bf16[128,768]{1,0:T(8,128)(2,1)} %get-tuple-element.101), channel_id=1, source_target_pairs={{0,1},{1,0},{2,3},{3,2},{4,5},{5,4},{6,7},{7,6},{8,9},{9,8},{10,11... | collective-permute-start | bytes 589832 | tf_op jit(solution)/shard_map/ppermute | solution.py:268
  152.7 4.6 %collective-permute-start.33 = (bf16[128,768]{1,0:T(8,128)(2,1)}, bf16[128,768]{1,0:T(8,128)(2,1)}, u32[]{:S(2)}, u32[]{:S(2)}) collective-permute-start(bf16[128,768]{1,0:T(8,128)(2,1)} %get-tuple-element.99), channel_id=1, source_target_pairs={{0,1},{1,0},{2,3},{3,2},{4,5},{5,4},{6,7},{7,6},{8,9},{9,8},{10,11... | collective-permute-start | bytes 589832 | tf_op jit(solution)/shard_map/ppermute | solution.py:268
  (3 other events, 2.1 us)

commit v5 on v4

--- a/solution.py
+++ b/solution.py
@@ -317,9 +317,10 @@
     level2 = [after(piece, late[0]) for piece in level2]
     g0a = jnp.concatenate([base, plus], axis=0)
     g0a = after(g0a, *level2)
-    far = fetch_mixed(after(base, *level2), 1, 2)
+    upper = fetch_mixed(after(plus[: half // 2], *level2), 1, 1)
+    lower = fetch_mixed(after(minus[half // 2 :], *level2), 1, 3)
     g1a, g3a = fetch_mixed(g0a, 2, 1), fetch_mixed(g0a, 2, 3)
-    g0b = jnp.concatenate([minus, far], axis=0)
+    g0b = jnp.concatenate([minus, upper, lower], axis=0)
 
     gain = head_gain.reshape(1, -1)
     norm_a = norm(table, early, 0, gain, level1, level2)

time: 161 us -> 157 us (0.975)
  starting transfers between devices: 70.8 us -> 60.9 us
  local copies, waits for them, and re-layouts: 6.19 us -> 9.51 us
    ppermute x7, starting transfers between devices: 26.5 us -> 16.1 us  [swap(): return lax.ppermute(array, 'c', [(0, 1), (1, 0)])]
    ppermute x12, waiting for transfers between devices: 4.99 us -> 11.8 us  [push(): return lax.ppermute(array, ('y', 'c'), pairs)]
    ppermute x15 -> x16, waiting for transfers between devices: 19.5 us -> 14.2 us  [fetch_mixed(): return lax.ppermute(array, ('x', 'z', 'c'), pairs)]
    slice x0 -> x2, local copies, waits for them, and re-layouts: none -> 2.54 us  [the longest x1 1.76 us: per_device(): upper = fetch_mixed(after(plus[:half // 2], *level2), 1, 1)]
    unnamed x37 -> x30, local copies, waits for them, and re-layouts: 2.48 us -> 3.5 us
    ppermute x15 -> x16, starting transfers between devices: 21.6 us -> 21.6 us  [fetch_mixed(): return lax.ppermute(array, ('x', 'z', 'c'), pairs)]
  transfers between devices with their start and end apart: 34 -> 35, of which waited for: 13 -> 15; matrix products, arithmetic and copies ran while one was open for 6% -> 9% of each run, Pallas kernels for 27% -> 28%
where the time goes in v5:
time: 157 us; the launch traced here: 156 us
  starting transfers between devices  60.9 us (39%)
  Pallas kernels  48.6 us (31%)
  waiting for transfers between devices  27.3 us (17%)
  other arithmetic  9.61 us (6%)
  local copies, waits for them, and re-layouts  9.51 us (6%)
    ppermute x12, starting transfers between devices, push(): return lax.ppermute(array, ('y', 'c'), pairs)  23.2 us
    ppermute x16, starting transfers between devices, fetch_mixed(): return lax.ppermute(array, ('x', 'z', 'c'), pairs)  21.6 us
    pallas_call x4, Pallas kernels, project(): pl.pallas_call(project_body, grid_spec=pltpu.PrefetchScalarGridSpec(num_s...  18.6 us
    ppermute x7, starting transfers between devices, swap(): return lax.ppermute(array, 'c', [(0, 1), (1, 0)])  16.1 us
    ppermute x16, waiting for transfers between devices, fetch_mixed(): return lax.ppermute(array, ('x', 'z', 'c'), pairs)  14.2 us
    ppermute x12, waiting for transfers between devices, push(): return lax.ppermute(array, ('y', 'c'), pairs)  11.8 us
    pallas_call x2, Pallas kernels, local_attention(): pl.pallas_call(local_body, grid=(heads,), in_specs=[source, source, sourc...  11.4 us
    pallas_call x2, Pallas kernels, norm(): pl.pallas_call(norm_body, grid_spec=pltpu.PrefetchScalarGridSpec(num_scal...  8.37 us
  transfers between devices with their start and end apart: 35, of which 15 were waited for; matrix products, arithmetic and copies ran while one was open for 9% of the time, Pallas kernels for 28%

profile of v5, /device:TPU:1, one launch (start us, length us, event | category | flops | bytes accessed | tf_op | source)
XLA Modules:
  0.0 156.1 jit_solution(15599846922913974523)
XLA Ops:
  0.0 1.7 %constant_dynamic-slice_fusion = (bf16[1024,192]{1,0:T(8,128)(2,1)S(1)}, bf16[1024,192]{1,0:T(8,128)(2,1)S(1)}) fusion(bf16[1024,384]{1,0:T(8,128)(2,1)} %param.10, s32[]{:T(128)S(6)} %select_n.188, s32[]{:T(128)S(6)} %select_n.187), kind=kLoop, calls=%fused_computation.19 | loop fusion | bytes 1572872 | tf_op jit(solution)/shard_map/dynamic-slice.1
  1.9 1.5 collective-permute-start.1
  3.6 4.8 %span_state.1 = (bf16[1024,1024]{1,0:T(8,128)(2,1)}, bf16[64,2048]{1,0:T(8,128)(2,1)}) custom-call(bf16[1024,1024]{1,0:T(8,128)(2,1)} %k_ref, bf16[1024,1024]{1,0:T(8,128)(2,1)} %v_ref.5), custom_call_target="tpu_custom_call" | custom-call | tf_op jit(solution)/shard_map/span_state/pallas_call | solution.py:45
  8.4 1.1 pad_maximum_fusion.1
  9.5 1.4 collective-permute-start.3
  10.9 1.4 collective-permute-start.2
  12.3 1.6 %collective-permute-start.5 = (bf16[64,2048]{1,0:T(8,128)(2,1)S(1)}, bf16[64,2048]{1,0:T(8,128)(2,1)S(1)}, u32[]{:S(2)}, u32[]{:S(2)}) collective-permute-start(bf16[64,2048]{1,0:T(8,128)(2,1)S(1)} %copy-done.12), channel_id=1, source_target_pairs={{16,0},{65,1},{24,8},{73,9},{0,16},{81,17},{8,24},{89,25},{48,32},... | collective-permute-start | bytes 786440 | tf_op jit(solution)/shard_map/ppermute | solution.py:264
  14.2 2.4 %collective-permute-start = (bf16[64,2048]{1,0:T(8,128)(2,1)S(1)}, bf16[64,2048]{1,0:T(8,128)(2,1)S(1)}, u32[]{:S(2)}, u32[]{:S(2)}) collective-permute-start(bf16[64,2048]{1,0:T(8,128)(2,1)S(1)} %copy-done.12), channel_id=1, source_target_pairs={{8,0},{33,1},{16,8},{41,9},{24,16},{49,17},{0,24},{57,25},{40,32},... | collective-permute-start | bytes 786440 | tf_op jit(solution)/shard_map/ppermute | solution.py:264
  16.6 5.7 %local_attention.2 = (bf16[1024,512]{1,0:T(8,128)(2,1)}, f32[1024,512]{1,0:T(8,128)}) custom-call(bf16[1024,1024]{1,0:T(8,128)(2,1)} %q_ref.2, bf16[1024,1024]{1,0:T(8,128)(2,1)} %get-tuple-element.54.kact_ref, bf16[1024,1024]{1,0:T(8,128)(2,1)} %v_ref.5), custom_call_target="tpu_custom_call" | custom-call | tf_op jit(solution)/shard_map/local_attention/pallas_call | solution.py:84
  22.9 3.0 %collective-permute-done.5.z3 = bf16[64,2048]{1,0:T(8,128)(2,1)S(1)} collective-permute-done((bf16[64,2048]{1,0:T(8,128)(2,1)S(1)}, bf16[64,2048]{1,0:T(8,128)(2,1)S(1)}, u32[]{:S(2)}, u32[]{:S(2)}) %collective-permute-start.5) | collective-permute-done | bytes 262176 | tf_op jit(solution)/shard_map/ppermute | solution.py:264
  25.9 1.7 %collective-permute-done.4.z2 = bf16[64,2048]{1,0:T(8,128)(2,1)S(1)} collective-permute-done((bf16[64,2048]{1,0:T(8,128)(2,1)S(1)}, bf16[64,2048]{1,0:T(8,128)(2,1)S(1)}, u32[]{:S(2)}, u32[]{:S(2)}) %collective-permute-start.4) | collective-permute-done | bytes 262176 | tf_op jit(solution)/shard_map/ppermute | solution.py:264
  28.9 2.4 %messages.1 = (bf16[64,2048]{1,0:T(8,128)(2,1)}, bf16[64,2048]{1,0:T(8,128)(2,1)}, bf16[64,2048]{1,0:T(8,128)(2,1)}) custom-call(s32[15]{0:T(128)} %stack.156.tab_ref, bf16[64,2048]{1,0:T(8,128)(2,1)} %get-tuple-element.57.state_ref, bf16[64,2048]{1,0:T(8,128)(2,1)} %copy-done.8, bf16[64,2048]{1,0:T(8,128)(2,1)} %copy-done.7, bf16[64,2048]{1,0:T(8,128)(2,1)} %copy-done.6), custom_call_target="tpu_custom_call" | custom-call | tf_op jit(solution)/shard_map/messages/pallas_call | solution.py:112
  31.3 3.8 %collective-permute-start.6 = (bf16[64,2048]{1,0:T(8,128)(2,1)}, bf16[64,2048]{1,0:T(8,128)(2,1)}, u32[]{:S(2)}, u32[]{:S(2)}) collective-permute-start(bf16[64,2048]{1,0:T(8,128)(2,1)} %get-tuple-element.62), channel_id=1, source_target_pairs={{32,0},{9,1},{40,8},{17,9},{48,16},{25,17},{56,24},{1,25},{64,32},... | collective-permute-start | bytes 786440 | tf_op jit(solution)/shard_map/ppermute | solution.py:264
  35.1 1.2 collective-permute-start.8
  36.3 5.7 %local_attention.3 = (bf16[1024,512]{1,0:T(8,128)(2,1)}, f32[1024,512]{1,0:T(8,128)}) custom-call(bf16[1024,1024]{1,0:T(8,128)(2,1)} %q_ref.2, bf16[1024,1024]{1,0:T(8,128)(2,1)} %get-tuple-element.54.kact_ref, bf16[1024,1024]{1,0:T(8,128)(2,1)} %v_ref.5), custom_call_target="tpu_custom_call" | custom-call | tf_op jit(solution)/shard_map/local_attention/pallas_call | solution.py:84
  42.1 1.4 pad_maximum_fusion.refs_4_.refs_5_
  43.5 1.4 collective-permute-done.7.x2
  45.6 2.0 %collective-permute-start.11 = (bf16[384,2048]{1,0:T(8,128)(2,1)S(1)}, bf16[384,2048]{1,0:T(8,128)(2,1)}, u32[]{:S(2)}, u32[]{:S(2)}) collective-permute-start(bf16[384,2048]{1,0:T(8,128)(2,1)S(1)} %pad_maximum_fusion.refs_4_.refs_5_), channel_id=1, source_target_pairs={{32,0},{9,1},{40,8},{17,9},{48,16},{25,17},{56,24},{1,25},{64,32},... | collective-permute-start | bytes 4718600 | tf_op jit(solution)/shard_map/ppermute | solution.py:264
  47.7 1.8 %slice.8 = bf16[96,2048]{1,0:T(8,128)(2,1)} slice(bf16[192,2048]{1,0:T(8,128)(2,1)} %collective-permute-done.2), slice={[0:96], [0:2048]} | slice | bytes 786432 | tf_op jit(solution)/shard_map/slice | solution.py:320
  49.4 1.7 %collective-permute-start.14 = (bf16[96,2048]{1,0:T(8,128)(2,1)}, bf16[96,2048]{1,0:T(8,128)(2,1)}, u32[]{:S(2)}, u32[]{:S(2)}) collective-permute-start(bf16[96,2048]{1,0:T(8,128)(2,1)} %slice.8), channel_id=1, source_target_pairs={{8,0},{33,1},{16,8},{41,9},{24,16},{49,17},{0,24},{57,25},{40,32},... | collective-permute-start | bytes 1179656 | tf_op jit(solution)/shard_map/ppermute | solution.py:264
  51.9 4.2 %norm.2.refs_0_ = bf16[1024,512]{1,0:T(8,128)(2,1)} custom-call(s32[15]{0:T(128)} %stack.156.tab_ref, bf16[1024,512]{1,0:T(8,128)(2,1)} %get-tuple-element.55.q_ref, f32[1024,512]{1,0:T(8,128)} %get-tuple-element.56.local_ref, f32[1,1024]{1,0:T(1,128)} %bitcast.37, bf16[64,2048]{1,0:T(8,128)(2,1)} %copy-done.8, bf16[64,2048]{1,0:T(8,128)(2,1)} %copy-done.7, ...), custom_call_target="tpu_custom_call" | custom-call | tf_op jit(solution)/shard_map/norm/pallas_call | solution.py:154
  56.1 3.0 %collective-permute-start.9 = (bf16[1024,512]{1,0:T(8,128)(2,1)}, bf16[1024,512]{1,0:T(8,128)(2,1)S(1)}, u32[]{:S(2)}, u32[]{:S(2)}) collective-permute-start(bf16[1024,512]{1,0:T(8,128)(2,1)} %norm.2.refs_0_), channel_id=1, source_target_pairs={{0,1},{1,0},{2,3},{3,2},{4,5},{5,4},{6,7},{7,6},{8,9},{9,8},{10,11... | collective-permute-start | bytes 3145736 | tf_op jit(solution)/shard_map/ppermute | solution.py:268
  59.1 4.2 %norm.3.refs_1_ = bf16[1024,512]{1,0:T(8,128)(2,1)} custom-call(s32[15]{0:T(128)} %stack.156.tab_ref, bf16[1024,512]{1,0:T(8,128)(2,1)} %get-tuple-element.64.q_ref, f32[1024,512]{1,0:T(8,128)} %get-tuple-element.71.local_ref, f32[1,1024]{1,0:T(1,128)} %bitcast.38, bf16[64,2048]{1,0:T(8,128)(2,1)} %copy-done.8, bf16[64,2048]{1,0:T(8,128)(2,1)} %copy-done.7, ...), custom_call_target="tpu_custom_call" | custom-call | tf_op jit(solution)/shard_map/norm/pallas_call | solution.py:154
  65.1 6.7 %collective-permute-done.15 = bf16[96,2048]{1,0:T(8,128)(2,1)} collective-permute-done((bf16[96,2048]{1,0:T(8,128)(2,1)}, bf16[96,2048]{1,0:T(8,128)(2,1)}, u32[]{:S(2)}, u32[]{:S(2)}) %collective-permute-start.15) | collective-permute-done | bytes 393248 | tf_op jit(solution)/shard_map/ppermute | solution.py:264
  73.0 2.7 %collective-permute-start.21 = (bf16[384,2048]{1,0:T(8,128)(2,1)S(1)}, bf16[384,2048]{1,0:T(8,128)(2,1)S(1)}, u32[]{:S(2)}, u32[]{:S(2)}) collective-permute-start(bf16[384,2048]{1,0:T(8,128)(2,1)S(1)} %constant_dynamic-update-slice_fusion.refs_6_.refs_7_), channel_id=1, source_target_pairs={{32,0},{9,1},{40,8},{17,9},{48,16},{25,17},{56,24},{1,25},{64,32},... | collective-permute-start | bytes 4718600 | tf_op jit(solution)/shard_map/ppermute | solution.py:264
  75.6 5.7 %project.4 = (bf16[256,768]{1,0:T(8,128)(2,1)S(1)}, bf16[256,768]{1,0:T(8,128)(2,1)S(1)}, bf16[256,768]{1,0:T(8,128)(2,1)S(1)}, bf16[256,768]{1,0:T(8,128)(2,1)S(1)}) custom-call(s32[1]{0:T(128)} %bitcast.16.core_ref, bf16[1024,512]{1,0:T(8,128)(2,1)S(1)} %copy-done, bf16[1024,512]{1,0:T(8,128)(2,1)S(1)} %copy-done.1, ...), custom_call_target="tpu_custom_call" | custom-call | tf_op jit(solution)/shard_map/project/pallas_call | solution.py:202
  81.3 2.8 %collective-permute-start.13 = (bf16[256,768]{1,0:T(8,128)(2,1)S(1)}, bf16[256,768]{1,0:T(8,128)(2,1)S(1)}, u32[]{:S(2)}, u32[]{:S(2)}) collective-permute-start(bf16[256,768]{1,0:T(8,128)(2,1)S(1)} %get-tuple-element.75), channel_id=1, source_target_pairs={{0,2},{1,7},{2,4},{3,1},{4,6},{5,3},{6,0},{7,5},{8,10},{9,15},{10,... | collective-permute-start | bytes 1179656 | tf_op jit(solution)/shard_map/ppermute | solution.py:276
  84.2 4.0 %project.5 = (bf16[256,768]{1,0:T(8,128)(2,1)S(1)}, bf16[256,768]{1,0:T(8,128)(2,1)S(1)}, bf16[256,768]{1,0:T(8,128)(2,1)S(1)}, bf16[256,768]{1,0:T(8,128)(2,1)S(1)}) custom-call(s32[1]{0:T(128)} %bitcast.16.core_ref, bf16[1024,512]{1,0:T(8,128)(2,1)S(1)} %copy-done, bf16[1024,512]{1,0:T(8,128)(2,1)S(1)} %copy-done.1, ...), custom_call_target="tpu_custom_call" | custom-call | tf_op jit(solution)/shard_map/project/pallas_call | solution.py:202
  89.0 3.5 %collective-permute-start.16 = (bf16[256,768]{1,0:T(8,128)(2,1)S(1)}, bf16[256,768]{1,0:T(8,128)(2,1)S(1)}, u32[]{:S(2)}, u32[]{:S(2)}) collective-permute-start(bf16[256,768]{1,0:T(8,128)(2,1)S(1)} %add_convert_fusion.5), channel_id=1, source_target_pairs={{0,2},{1,7},{2,4},{3,1},{4,6},{5,3},{6,0},{7,5},{8,10},{9,15},{10,... | collective-permute-start | bytes 1179656 | tf_op jit(solution)/shard_map/ppermute | solution.py:276
  92.5 1.2 collective-permute-done.22.refs_6_.refs_7_
  93.7 2.4 %collective-permute-start.26 = (bf16[384,2048]{1,0:T(8,128)(2,1)}, bf16[384,2048]{1,0:T(8,128)(2,1)S(1)}, u32[]{:S(2)}, u32[]{:S(2)}) collective-permute-start(bf16[384,2048]{1,0:T(8,128)(2,1)} %collective-permute-done.11.refs_4_.refs_5_), channel_id=1, source_target_pairs={{32,0},{9,1},{40,8},{17,9},{48,16},{25,17},{56,24},{1,25},{64,32},... | collective-permute-start | bytes 4718600 | tf_op jit(solution)/shard_map/ppermute | solution.py:264
  96.1 4.0 %project.6 = (bf16[256,768]{1,0:T(8,128)(2,1)S(1)}, bf16[256,768]{1,0:T(8,128)(2,1)S(1)}, bf16[256,768]{1,0:T(8,128)(2,1)S(1)}, bf16[256,768]{1,0:T(8,128)(2,1)S(1)}) custom-call(s32[1]{0:T(128)} %bitcast.16.core_ref, bf16[1024,512]{1,0:T(8,128)(2,1)S(1)} %copy-done, bf16[1024,512]{1,0:T(8,128)(2,1)S(1)} %copy-done.1, ...), custom_call_target="tpu_custom_call" | custom-call | tf_op jit(solution)/shard_map/project/pallas_call | solution.py:202
  100.2 2.8 %collective-permute-start.23 = (bf16[256,768]{1,0:T(8,128)(2,1)S(1)}, bf16[256,768]{1,0:T(8,128)(2,1)S(1)}, u32[]{:S(2)}, u32[]{:S(2)}) collective-permute-start(bf16[256,768]{1,0:T(8,128)(2,1)S(1)} %get-tuple-element.91), channel_id=1, source_target_pairs={{0,2},{1,7},{2,4},{3,1},{4,6},{5,3},{6,0},{7,5},{8,10},{9,15},{10,... | collective-permute-start | bytes 1179656 | tf_op jit(solution)/shard_map/ppermute | solution.py:276
  103.1 1.9 %collective-permute-start.19 = (bf16[256,768]{1,0:T(8,128)(2,1)S(1)}, bf16[256,768]{1,0:T(8,128)(2,1)S(1)}, u32[]{:S(2)}, u32[]{:S(2)}) collective-permute-start(bf16[256,768]{1,0:T(8,128)(2,1)S(1)} %add_convert_fusion.3), channel_id=1, source_target_pairs={{0,2},{1,7},{2,4},{3,1},{4,6},{5,3},{6,0},{7,5},{8,10},{9,15},{10,... | collective-permute-start | bytes 1179656 | tf_op jit(solution)/shard_map/ppermute | solution.py:276
  105.0 2.7 %collective-permute-done.23 = bf16[256,768]{1,0:T(8,128)(2,1)S(1)} collective-permute-done((bf16[256,768]{1,0:T(8,128)(2,1)S(1)}, bf16[256,768]{1,0:T(8,128)(2,1)S(1)}, u32[]{:S(2)}, u32[]{:S(2)}) %collective-permute-start.23) | collective-permute-done | bytes 393248 | tf_op jit(solution)/shard_map/ppermute | solution.py:276
  107.8 3.7 %collective-permute-start.24 = (bf16[256,768]{1,0:T(8,128)(2,1)S(1)}, bf16[256,768]{1,0:T(8,128)(2,1)S(1)}, u32[]{:S(2)}, u32[]{:S(2)}) collective-permute-start(bf16[256,768]{1,0:T(8,128)(2,1)S(1)} %add_convert_fusion.1), channel_id=1, source_target_pairs={{0,2},{1,7},{2,4},{3,1},{4,6},{5,3},{6,0},{7,5},{8,10},{9,15},{10,... | collective-permute-start | bytes 1179656 | tf_op jit(solution)/shard_map/ppermute | solution.py:276
  112.7 3.4 %collective-permute-start.20 = (bf16[256,768]{1,0:T(8,128)(2,1)}, bf16[256,768]{1,0:T(8,128)(2,1)S(1)}, u32[]{:S(2)}, u32[]{:S(2)}) collective-permute-start(bf16[256,768]{1,0:T(8,128)(2,1)} %add_convert_fusion.2), channel_id=1, source_target_pairs={{0,2},{1,7},{2,4},{3,1},{4,6},{5,3},{6,0},{7,5},{8,10},{9,15},{10,... | collective-permute-start | bytes 1179656 | tf_op jit(solution)/shard_map/ppermute | solution.py:276
  116.3 3.5 %collective-permute-start.25 = (bf16[256,768]{1,0:T(8,128)(2,1)S(1)}, bf16[256,768]{1,0:T(8,128)(2,1)S(1)}, u32[]{:S(2)}, u32[]{:S(2)}) collective-permute-start(bf16[256,768]{1,0:T(8,128)(2,1)S(1)} %add_convert_fusion), channel_id=1, source_target_pairs={{0,2},{1,7},{2,4},{3,1},{4,6},{5,3},{6,0},{7,5},{8,10},{9,15},{10,... | collective-permute-start | bytes 1179656 | tf_op jit(solution)/shard_map/ppermute | solution.py:276
  119.8 4.8 %project.7 = (bf16[256,768]{1,0:T(8,128)(2,1)}, bf16[256,768]{1,0:T(8,128)(2,1)}, bf16[256,768]{1,0:T(8,128)(2,1)}, bf16[256,768]{1,0:T(8,128)(2,1)S(1)}) custom-call(s32[1]{0:T(128)} %bitcast.16.core_ref, bf16[1024,512]{1,0:T(8,128)(2,1)S(1)} %copy-done, bf16[1024,512]{1,0:T(8,128)(2,1)S(1)} %copy-done.1, ...), custom_call_target="tpu_custom_call" | custom-call | tf_op jit(solution)/shard_map/project/pallas_call | solution.py:202
  127.6 4.3 %collective-permute-start.31 = (bf16[128,768]{1,0:T(8,128)(2,1)}, bf16[128,768]{1,0:T(8,128)(2,1)S(1)}, u32[]{:S(2)}, u32[]{:S(2)}) collective-permute-start(bf16[128,768]{1,0:T(8,128)(2,1)} %get-tuple-element.107), channel_id=1, source_target_pairs={{0,1},{1,0},{2,3},{3,2},{4,5},{5,4},{6,7},{7,6},{8,9},{9,8},{10,11... | collective-permute-start | bytes 589832 | tf_op jit(solution)/shard_map/ppermute | solution.py:268
  132.7 5.8 %collective-permute-done.25 = bf16[256,768]{1,0:T(8,128)(2,1)S(1)} collective-permute-done((bf16[256,768]{1,0:T(8,128)(2,1)S(1)}, bf16[256,768]{1,0:T(8,128)(2,1)S(1)}, u32[]{:S(2)}, u32[]{:S(2)}) %collective-permute-start.25) | collective-permute-done | bytes 393248 | tf_op jit(solution)/shard_map/ppermute | solution.py:276
  138.5 3.5 %collective-permute-start.32 = (bf16[128,768]{1,0:T(8,128)(2,1)}, bf16[128,768]{1,0:T(8,128)(2,1)S(1)}, u32[]{:S(2)}, u32[]{:S(2)}) collective-permute-start(bf16[128,768]{1,0:T(8,128)(2,1)} %get-tuple-element.105), channel_id=1, source_target_pairs={{0,1},{1,0},{2,3},{3,2},{4,5},{5,4},{6,7},{7,6},{8,9},{9,8},{10,11... | collective-permute-start | bytes 589832 | tf_op jit(solution)/shard_map/ppermute | solution.py:268
  142.0 2.1 %add_convert_fusion.7 = (bf16[128,768]{1,0:T(8,128)(2,1)}, f32[128,768]{1,0:T(8,128)S(1)}) fusion(bf16[256,768]{1,0:T(8,128)(2,1)} %copy-done.11, s32[]{:T(128)S(6)} %select_n.190, bf16[256,768]{1,0:T(8,128)(2,1)} %copy-done.3, s32[]{:T(128)S(6)} %select_n.189), kind=kLoop, calls=%fused_computation.9 | loop fusion | flops 688128 | bytes 1376264 | tf_op jit(solution)/shard_map/convert_element_type | solution.py:290
  145.8 1.3 collective-permute-done.30
  147.1 2.2 %add_convert_fusion.6 = (bf16[128,768]{1,0:T(8,128)(2,1)}, f32[128,768]{1,0:T(8,128)S(1)}) fusion(bf16[256,768]{1,0:T(8,128)(2,1)} %collective-permute-done.30, s32[]{:T(128)S(6)} %select_n.190, bf16[256,768]{1,0:T(8,128)(2,1)} %collective-permute-done.29, bf16[256,768]{1,0:T(8,128)(2,1)} %collective-permute-done.28, bf16[256,768]{1,0:T(8,128)(2,1)S(1)} %copy-done.5, ...), kind=kLoop, calls=%fused_computation.8 | loop fusion | flops 1474560 | bytes 2162696 | tf_op jit(solution)/shard_map/convert_element_type | solution.py:290
  149.3 2.4 %collective-permute-start.34 = (bf16[128,768]{1,0:T(8,128)(2,1)}, bf16[128,768]{1,0:T(8,128)(2,1)}, u32[]{:S(2)}, u32[]{:S(2)}) collective-permute-start(bf16[128,768]{1,0:T(8,128)(2,1)} %get-tuple-element.101), channel_id=1, source_target_pairs={{0,1},{1,0},{2,3},{3,2},{4,5},{5,4},{6,7},{7,6},{8,9},{9,8},{10,11... | collective-permute-start | bytes 589832 | tf_op jit(solution)/shard_map/ppermute | solution.py:268
  151.8 1.3 collective-permute-done.34.refs_7_
  153.1 3.0 %finish.1 = bf16[128,6144]{1,0:T(8,128)(2,1)} custom-call(s32[17]{0:T(128)S(1)} %stack.135.tab_ref, bf16[128,6144]{1,0:T(8,128)(2,1)S(1)} %copy-done.2, f32[128,768]{1,0:T(8,128)S(1)} %get-tuple-element.108.refs_0_, f32[128,768]{1,0:T(8,128)S(1)} %get-tuple-element.106.refs_1_, f32[128,768]{1,0:T(8,128)S(1)} %get-tuple-element.104.refs_2_, ...), custom_call_target="tpu_custom_call" | custom-call | tf_op jit(solution)/shard_map/finish/pallas_call | solution.py:239
  (81 shorter events, 15.2 us)
Async XLA Ops:
  1.9 6.5 %collective-permute-start.1 = (bf16[192,1024]{1,0:T(8,128)(2,1)S(1)}, bf16[192,1024]{1,0:T(8,128)(2,1)}, u32[]{:S(2)}, u32[]{:S(2)}) collective-permute-start(bf16[192,1024]{1,0:T(8,128)(2,1)S(1)} %bitcast.36), channel_id=1, source_target_pairs={{0,1},{1,0},{2,3},{3,2},{4,5},{5,4},{6,7},{7,6},{8,9},{9,8},{10,11... | collective-permute-start | bytes 1179656 | tf_op jit(solution)/shard_map/ppermute | solution.py:268
  8.4 3.9 %copy-start.12 = (bf16[64,2048]{1,0:T(8,128)(2,1)S(1)}, bf16[64,2048]{1,0:T(8,128)(2,1)}, u32[]{:S(2)}) copy-start(bf16[64,2048]{1,0:T(8,128)(2,1)} %get-tuple-element.57.state_ref) | copy-start | bytes 786436
  9.5 16.3 %collective-permute-start.3 = (bf16[192,2048]{1,0:T(8,128)(2,1)S(1)}, bf16[192,2048]{1,0:T(8,128)(2,1)S(1)}, u32[]{:S(2)}, u32[]{:S(2)}) collective-permute-start(bf16[192,2048]{1,0:T(8,128)(2,1)S(1)} %pad_maximum_fusion.1), channel_id=1, source_target_pairs={{24,0},{97,1},{0,8},{105,9},{8,16},{113,17},{16,24},{121,25},{56,3... | collective-permute-start | bytes 2359304 | tf_op jit(solution)/shard_map/ppermute | solution.py:264
  10.9 15.0 %collective-permute-start.2 = (bf16[192,2048]{1,0:T(8,128)(2,1)S(1)}, bf16[192,2048]{1,0:T(8,128)(2,1)}, u32[]{:S(2)}, u32[]{:S(2)}) collective-permute-start(bf16[192,2048]{1,0:T(8,128)(2,1)S(1)} %pad_maximum_fusion.1), channel_id=1, source_target_pairs={{8,0},{33,1},{16,8},{41,9},{24,16},{49,17},{0,24},{57,25},{40,32},... | collective-permute-start | bytes 2359304 | tf_op jit(solution)/shard_map/ppermute | solution.py:264
  12.3 13.6 %collective-permute-start.5 = (bf16[64,2048]{1,0:T(8,128)(2,1)S(1)}, bf16[64,2048]{1,0:T(8,128)(2,1)S(1)}, u32[]{:S(2)}, u32[]{:S(2)}) collective-permute-start(bf16[64,2048]{1,0:T(8,128)(2,1)S(1)} %copy-done.12), channel_id=1, source_target_pairs={{16,0},{65,1},{24,8},{73,9},{0,16},{81,17},{8,24},{89,25},{48,32},... | collective-permute-start | bytes 786440 | tf_op jit(solution)/shard_map/ppermute | solution.py:264
  13.9 13.7 %collective-permute-start.4 = (bf16[64,2048]{1,0:T(8,128)(2,1)S(1)}, bf16[64,2048]{1,0:T(8,128)(2,1)S(1)}, u32[]{:S(2)}, u32[]{:S(2)}) collective-permute-start(bf16[64,2048]{1,0:T(8,128)(2,1)S(1)} %copy-done.12), channel_id=1, source_target_pairs={{24,0},{97,1},{0,8},{105,9},{8,16},{113,17},{16,24},{121,25},{56,3... | collective-permute-start | bytes 786440 | tf_op jit(solution)/shard_map/ppermute | solution.py:264
  14.2 13.5 %collective-permute-start = (bf16[64,2048]{1,0:T(8,128)(2,1)S(1)}, bf16[64,2048]{1,0:T(8,128)(2,1)S(1)}, u32[]{:S(2)}, u32[]{:S(2)}) collective-permute-start(bf16[64,2048]{1,0:T(8,128)(2,1)S(1)} %copy-done.12), channel_id=1, source_target_pairs={{8,0},{33,1},{16,8},{41,9},{24,16},{49,17},{0,24},{57,25},{40,32},... | collective-permute-start | bytes 786440 | tf_op jit(solution)/shard_map/ppermute | solution.py:264
  25.8 1.8 %copy-start.6 = (bf16[64,2048]{1,0:T(8,128)(2,1)}, bf16[64,2048]{1,0:T(8,128)(2,1)S(1)}, u32[]{:S(2)}) copy-start(bf16[64,2048]{1,0:T(8,128)(2,1)S(1)} %collective-permute-done.5.z3) | copy-start | bytes 786436
  25.9 10.5 %copy-start.9 = (bf16[192,2048]{1,0:T(8,128)(2,1)}, bf16[192,2048]{1,0:T(8,128)(2,1)S(1)}, u32[]{:S(2)}) copy-start(bf16[192,2048]{1,0:T(8,128)(2,1)S(1)} %collective-permute-done.3) | copy-start | bytes 2359300
  27.5 0.7 copy-start.7
  28.2 0.7 copy-start.8
  31.3 13.7 %collective-permute-start.6 = (bf16[64,2048]{1,0:T(8,128)(2,1)}, bf16[64,2048]{1,0:T(8,128)(2,1)}, u32[]{:S(2)}, u32[]{:S(2)}) collective-permute-start(bf16[64,2048]{1,0:T(8,128)(2,1)} %get-tuple-element.62), channel_id=1, source_target_pairs={{32,0},{9,1},{40,8},{17,9},{48,16},{25,17},{56,24},{1,25},{64,32},... | collective-permute-start | bytes 786440 | tf_op jit(solution)/shard_map/ppermute | solution.py:264
  35.1 9.9 %collective-permute-start.7 = (bf16[64,2048]{1,0:T(8,128)(2,1)}, bf16[64,2048]{1,0:T(8,128)(2,1)}, u32[]{:S(2)}, u32[]{:S(2)}) collective-permute-start(bf16[64,2048]{1,0:T(8,128)(2,1)} %get-tuple-element.66), channel_id=1, source_target_pairs={{96,0},{25,1},{104,8},{1,9},{112,16},{9,17},{120,24},{17,25},{0,32... | collective-permute-start | bytes 786440 | tf_op jit(solution)/shard_map/ppermute | solution.py:264
  35.1 8.4 %collective-permute-start.8 = (bf16[64,2048]{1,0:T(8,128)(2,1)}, bf16[64,2048]{1,0:T(8,128)(2,1)}, u32[]{:S(2)}, u32[]{:S(2)}) collective-permute-start(bf16[64,2048]{1,0:T(8,128)(2,1)} %get-tuple-element.68), channel_id=1, source_target_pairs={{64,0},{17,1},{72,8},{25,9},{80,16},{1,17},{88,24},{9,25},{96,32},... | collective-permute-start | bytes 786440 | tf_op jit(solution)/shard_map/ppermute | solution.py:264
  42.1 9.1 %copy-start.10 = (bf16[192,2048]{1,0:T(8,128)(2,1)S(1)}, bf16[192,2048]{1,0:T(8,128)(2,1)}, u32[]{:S(2)}) copy-start(bf16[192,2048]{1,0:T(8,128)(2,1)} %copy-done.9) | copy-start | bytes 2359300
  45.0 27.9 %collective-permute-start.12 = (bf16[384,2048]{1,0:T(8,128)(2,1)S(1)}, bf16[384,2048]{1,0:T(8,128)(2,1)}, u32[]{:S(2)}, u32[]{:S(2)}) collective-permute-start(bf16[384,2048]{1,0:T(8,128)(2,1)S(1)} %pad_maximum_fusion.refs_4_.refs_5_), channel_id=1, source_target_pairs={{96,0},{25,1},{104,8},{1,9},{112,16},{9,17},{120,24},{17,25},{0,32... | collective-permute-start | bytes 4718600 | tf_op jit(solution)/shard_map/ppermute | solution.py:264
  45.6 27.2 %collective-permute-start.11 = (bf16[384,2048]{1,0:T(8,128)(2,1)S(1)}, bf16[384,2048]{1,0:T(8,128)(2,1)}, u32[]{:S(2)}, u32[]{:S(2)}) collective-permute-start(bf16[384,2048]{1,0:T(8,128)(2,1)S(1)} %pad_maximum_fusion.refs_4_.refs_5_), channel_id=1, source_target_pairs={{32,0},{9,1},{40,8},{17,9},{48,16},{25,17},{56,24},{1,25},{64,32},... | collective-permute-start | bytes 4718600 | tf_op jit(solution)/shard_map/ppermute | solution.py:264
  49.4 13.9 %collective-permute-start.14 = (bf16[96,2048]{1,0:T(8,128)(2,1)}, bf16[96,2048]{1,0:T(8,128)(2,1)}, u32[]{:S(2)}, u32[]{:S(2)}) collective-permute-start(bf16[96,2048]{1,0:T(8,128)(2,1)} %slice.8), channel_id=1, source_target_pairs={{8,0},{33,1},{16,8},{41,9},{24,16},{49,17},{0,24},{57,25},{40,32},... | collective-permute-start | bytes 1179656 | tf_op jit(solution)/shard_map/ppermute | solution.py:264
  56.1 19.5 %collective-permute-start.9 = (bf16[1024,512]{1,0:T(8,128)(2,1)}, bf16[1024,512]{1,0:T(8,128)(2,1)S(1)}, u32[]{:S(2)}, u32[]{:S(2)}) collective-permute-start(bf16[1024,512]{1,0:T(8,128)(2,1)} %norm.2.refs_0_), channel_id=1, source_target_pairs={{0,1},{1,0},{2,3},{3,2},{4,5},{5,4},{6,7},{7,6},{8,9},{9,8},{10,11... | collective-permute-start | bytes 3145736 | tf_op jit(solution)/shard_map/ppermute | solution.py:268
  59.1 12.7 %collective-permute-start.15 = (bf16[96,2048]{1,0:T(8,128)(2,1)}, bf16[96,2048]{1,0:T(8,128)(2,1)}, u32[]{:S(2)}, u32[]{:S(2)}) collective-permute-start(bf16[96,2048]{1,0:T(8,128)(2,1)} %slice.9), channel_id=1, source_target_pairs={{24,0},{97,1},{0,8},{105,9},{8,16},{113,17},{16,24},{121,25},{56,3... | collective-permute-start | bytes 1179656 | tf_op jit(solution)/shard_map/ppermute | solution.py:264
  63.3 12.3 %copy-start = (bf16[1024,512]{1,0:T(8,128)(2,1)S(1)}, bf16[1024,512]{1,0:T(8,128)(2,1)}, u32[]{:S(2)}) copy-start(bf16[1024,512]{1,0:T(8,128)(2,1)} %norm.2.refs_0_) | copy-start | bytes 3145732
  63.3 12.3 %copy-start.1 = (bf16[1024,512]{1,0:T(8,128)(2,1)S(1)}, bf16[1024,512]{1,0:T(8,128)(2,1)}, u32[]{:S(2)}) copy-start(bf16[1024,512]{1,0:T(8,128)(2,1)} %norm.3.refs_1_) | copy-start | bytes 3145732
  63.3 12.3 %collective-permute-start.10 = (bf16[1024,512]{1,0:T(8,128)(2,1)}, bf16[1024,512]{1,0:T(8,128)(2,1)S(1)}, u32[]{:S(2)}, u32[]{:S(2)}) collective-permute-start(bf16[1024,512]{1,0:T(8,128)(2,1)} %norm.3.refs_1_), channel_id=1, source_target_pairs={{0,1},{1,0},{2,3},{3,2},{4,5},{5,4},{6,7},{7,6},{8,9},{9,8},{10,11... | collective-permute-start | bytes 3145736 | tf_op jit(solution)/shard_map/ppermute | solution.py:268
  72.9 20.8 %collective-permute-start.22 = (bf16[384,2048]{1,0:T(8,128)(2,1)S(1)}, bf16[384,2048]{1,0:T(8,128)(2,1)S(1)}, u32[]{:S(2)}, u32[]{:S(2)}) collective-permute-start(bf16[384,2048]{1,0:T(8,128)(2,1)S(1)} %constant_dynamic-update-slice_fusion.refs_6_.refs_7_), channel_id=1, source_target_pairs={{96,0},{25,1},{104,8},{1,9},{112,16},{9,17},{120,24},{17,25},{0,32... | collective-permute-start | bytes 4718600 | tf_op jit(solution)/shard_map/ppermute | solution.py:264
  73.0 20.7 %collective-permute-start.21 = (bf16[384,2048]{1,0:T(8,128)(2,1)S(1)}, bf16[384,2048]{1,0:T(8,128)(2,1)S(1)}, u32[]{:S(2)}, u32[]{:S(2)}) collective-permute-start(bf16[384,2048]{1,0:T(8,128)(2,1)S(1)} %constant_dynamic-update-slice_fusion.refs_6_.refs_7_), channel_id=1, source_target_pairs={{32,0},{9,1},{40,8},{17,9},{48,16},{25,17},{56,24},{1,25},{64,32},... | collective-permute-start | bytes 4718600 | tf_op jit(solution)/shard_map/ppermute | solution.py:264
  81.3 7.5 %collective-permute-start.13 = (bf16[256,768]{1,0:T(8,128)(2,1)S(1)}, bf16[256,768]{1,0:T(8,128)(2,1)S(1)}, u32[]{:S(2)}, u32[]{:S(2)}) collective-permute-start(bf16[256,768]{1,0:T(8,128)(2,1)S(1)} %get-tuple-element.75), channel_id=1, source_target_pairs={{0,2},{1,7},{2,4},{3,1},{4,6},{5,3},{6,0},{7,5},{8,10},{9,15},{10,... | collective-permute-start | bytes 1179656 | tf_op jit(solution)/shard_map/ppermute | solution.py:276
  89.0 11.2 %collective-permute-start.16 = (bf16[256,768]{1,0:T(8,128)(2,1)S(1)}, bf16[256,768]{1,0:T(8,128)(2,1)S(1)}, u32[]{:S(2)}, u32[]{:S(2)}) collective-permute-start(bf16[256,768]{1,0:T(8,128)(2,1)S(1)} %add_convert_fusion.5), channel_id=1, source_target_pairs={{0,2},{1,7},{2,4},{3,1},{4,6},{5,3},{6,0},{7,5},{8,10},{9,15},{10,... | collective-permute-start | bytes 1179656 | tf_op jit(solution)/shard_map/ppermute | solution.py:276
  92.5 10.5 %collective-permute-start.18 = (bf16[256,768]{1,0:T(8,128)(2,1)S(1)}, bf16[256,768]{1,0:T(8,128)(2,1)S(1)}, u32[]{:S(2)}, u32[]{:S(2)}) collective-permute-start(bf16[256,768]{1,0:T(8,128)(2,1)S(1)} %get-tuple-element.84), channel_id=1, source_target_pairs={{0,2},{1,7},{2,4},{3,1},{4,6},{5,3},{6,0},{7,5},{8,10},{9,15},{10,... | collective-permute-start | bytes 1179656 | tf_op jit(solution)/shard_map/ppermute | solution.py:276
  93.7 26.1 %collective-permute-start.26 = (bf16[384,2048]{1,0:T(8,128)(2,1)}, bf16[384,2048]{1,0:T(8,128)(2,1)S(1)}, u32[]{:S(2)}, u32[]{:S(2)}) collective-permute-start(bf16[384,2048]{1,0:T(8,128)(2,1)} %collective-permute-done.11.refs_4_.refs_5_), channel_id=1, source_target_pairs={{32,0},{9,1},{40,8},{17,9},{48,16},{25,17},{56,24},{1,25},{64,32},... | collective-permute-start | bytes 4718600 | tf_op jit(solution)/shard_map/ppermute | solution.py:264
  96.1 23.7 %collective-permute-start.27 = (bf16[384,2048]{1,0:T(8,128)(2,1)S(1)}, bf16[384,2048]{1,0:T(8,128)(2,1)S(1)}, u32[]{:S(2)}, u32[]{:S(2)}) collective-permute-start(bf16[384,2048]{1,0:T(8,128)(2,1)S(1)} %collective-permute-done.22.refs_6_.refs_7_), channel_id=1, source_target_pairs={{96,0},{25,1},{104,8},{1,9},{112,16},{9,17},{120,24},{17,25},{0,32... | collective-permute-start | bytes 4718600 | tf_op jit(solution)/shard_map/ppermute | solution.py:264
  100.1 19.6 %copy-start.3 = (bf16[256,768]{1,0:T(8,128)(2,1)}, bf16[256,768]{1,0:T(8,128)(2,1)S(1)}, u32[]{:S(2)}) copy-start(bf16[256,768]{1,0:T(8,128)(2,1)S(1)} %get-tuple-element.89) | copy-start | bytes 1179652
  100.2 7.5 %collective-permute-start.23 = (bf16[256,768]{1,0:T(8,128)(2,1)S(1)}, bf16[256,768]{1,0:T(8,128)(2,1)S(1)}, u32[]{:S(2)}, u32[]{:S(2)}) collective-permute-start(bf16[256,768]{1,0:T(8,128)(2,1)S(1)} %get-tuple-element.91), channel_id=1, source_target_pairs={{0,2},{1,7},{2,4},{3,1},{4,6},{5,3},{6,0},{7,5},{8,10},{9,15},{10,... | collective-permute-start | bytes 1179656 | tf_op jit(solution)/shard_map/ppermute | solution.py:276
  103.1 8.8 %collective-permute-start.19 = (bf16[256,768]{1,0:T(8,128)(2,1)S(1)}, bf16[256,768]{1,0:T(8,128)(2,1)S(1)}, u32[]{:S(2)}, u32[]{:S(2)}) collective-permute-start(bf16[256,768]{1,0:T(8,128)(2,1)S(1)} %add_convert_fusion.3), channel_id=1, source_target_pairs={{0,2},{1,7},{2,4},{3,1},{4,6},{5,3},{6,0},{7,5},{8,10},{9,15},{10,... | collective-permute-start | bytes 1179656 | tf_op jit(solution)/shard_map/ppermute | solution.py:276
  107.8 8.4 %collective-permute-start.24 = (bf16[256,768]{1,0:T(8,128)(2,1)S(1)}, bf16[256,768]{1,0:T(8,128)(2,1)S(1)}, u32[]{:S(2)}, u32[]{:S(2)}) collective-permute-start(bf16[256,768]{1,0:T(8,128)(2,1)S(1)} %add_convert_fusion.1), channel_id=1, source_target_pairs={{0,2},{1,7},{2,4},{3,1},{4,6},{5,3},{6,0},{7,5},{8,10},{9,15},{10,... | collective-permute-start | bytes 1179656 | tf_op jit(solution)/shard_map/ppermute | solution.py:276
  111.6 14.5 %collective-permute-start.17 = (bf16[256,768]{1,0:T(8,128)(2,1)S(1)}, bf16[256,768]{1,0:T(8,128)(2,1)S(1)}, u32[]{:S(2)}, u32[]{:S(2)}) collective-permute-start(bf16[256,768]{1,0:T(8,128)(2,1)S(1)} %add_convert_fusion.4), channel_id=1, source_target_pairs={{0,2},{1,7},{2,4},{3,1},{4,6},{5,3},{6,0},{7,5},{8,10},{9,15},{10,... | collective-permute-start | bytes 1179656 | tf_op jit(solution)/shard_map/ppermute | solution.py:276
  112.7 14.9 %collective-permute-start.20 = (bf16[256,768]{1,0:T(8,128)(2,1)}, bf16[256,768]{1,0:T(8,128)(2,1)S(1)}, u32[]{:S(2)}, u32[]{:S(2)}) collective-permute-start(bf16[256,768]{1,0:T(8,128)(2,1)} %add_convert_fusion.2), channel_id=1, source_target_pairs={{0,2},{1,7},{2,4},{3,1},{4,6},{5,3},{6,0},{7,5},{8,10},{9,15},{10,... | collective-permute-start | bytes 1179656 | tf_op jit(solution)/shard_map/ppermute | solution.py:276
  116.3 22.2 %collective-permute-start.25 = (bf16[256,768]{1,0:T(8,128)(2,1)S(1)}, bf16[256,768]{1,0:T(8,128)(2,1)S(1)}, u32[]{:S(2)}, u32[]{:S(2)}) collective-permute-start(bf16[256,768]{1,0:T(8,128)(2,1)S(1)} %add_convert_fusion), channel_id=1, source_target_pairs={{0,2},{1,7},{2,4},{3,1},{4,6},{5,3},{6,0},{7,5},{8,10},{9,15},{10,... | collective-permute-start | bytes 1179656 | tf_op jit(solution)/shard_map/ppermute | solution.py:276
  124.6 0.7 copy-start.4
  125.4 18.7 %collective-permute-start.28 = (bf16[256,768]{1,0:T(8,128)(2,1)}, bf16[256,768]{1,0:T(8,128)(2,1)}, u32[]{:S(2)}, u32[]{:S(2)}) collective-permute-start(bf16[256,768]{1,0:T(8,128)(2,1)} %get-tuple-element.98), channel_id=1, source_target_pairs={{0,4},{1,5},{2,6},{3,7},{4,0},{5,1},{6,2},{7,3},{8,12},{9,13},{10,... | collective-permute-start | bytes 1179656 | tf_op jit(solution)/shard_map/ppermute | solution.py:276
  125.4 20.4 %collective-permute-start.29 = (bf16[256,768]{1,0:T(8,128)(2,1)}, bf16[256,768]{1,0:T(8,128)(2,1)}, u32[]{:S(2)}, u32[]{:S(2)}) collective-permute-start(bf16[256,768]{1,0:T(8,128)(2,1)} %get-tuple-element.99), channel_id=1, source_target_pairs={{0,2},{1,7},{2,4},{3,1},{4,6},{5,3},{6,0},{7,5},{8,10},{9,15},{10,... | collective-permute-start | bytes 1179656 | tf_op jit(solution)/shard_map/ppermute | solution.py:276
  126.1 21.0 %collective-permute-start.30 = (bf16[256,768]{1,0:T(8,128)(2,1)}, bf16[256,768]{1,0:T(8,128)(2,1)}, u32[]{:S(2)}, u32[]{:S(2)}) collective-permute-start(bf16[256,768]{1,0:T(8,128)(2,1)} %get-tuple-element.100), channel_id=1, source_target_pairs={{0,6},{1,3},{2,0},{3,5},{4,2},{5,7},{6,4},{7,1},{8,14},{9,11},{10,... | collective-permute-start | bytes 1179656 | tf_op jit(solution)/shard_map/ppermute | solution.py:276
  127.6 19.5 %copy-start.5 = (bf16[256,768]{1,0:T(8,128)(2,1)S(1)}, bf16[256,768]{1,0:T(8,128)(2,1)}, u32[]{:S(2)}) copy-start(bf16[256,768]{1,0:T(8,128)(2,1)} %copy-done.4) | copy-start | bytes 1179652
  127.6 24.1 %collective-permute-start.31 = (bf16[128,768]{1,0:T(8,128)(2,1)}, bf16[128,768]{1,0:T(8,128)(2,1)S(1)}, u32[]{:S(2)}, u32[]{:S(2)}) collective-permute-start(bf16[128,768]{1,0:T(8,128)(2,1)} %get-tuple-element.107), channel_id=1, source_target_pairs={{0,1},{1,0},{2,3},{3,2},{4,5},{5,4},{6,7},{7,6},{8,9},{9,8},{10,11... | collective-permute-start | bytes 589832 | tf_op jit(solution)/shard_map/ppermute | solution.py:268
  138.5 3.5 %copy-start.11 = (bf16[256,768]{1,0:T(8,128)(2,1)}, bf16[256,768]{1,0:T(8,128)(2,1)S(1)}, u32[]{:S(2)}) copy-start(bf16[256,768]{1,0:T(8,128)(2,1)S(1)} %collective-permute-done.25) | copy-start | bytes 1179652
  138.5 13.2 %collective-permute-start.32 = (bf16[128,768]{1,0:T(8,128)(2,1)}, bf16[128,768]{1,0:T(8,128)(2,1)S(1)}, u32[]{:S(2)}, u32[]{:S(2)}) collective-permute-start(bf16[128,768]{1,0:T(8,128)(2,1)} %get-tuple-element.105), channel_id=1, source_target_pairs={{0,1},{1,0},{2,3},{3,2},{4,5},{5,4},{6,7},{7,6},{8,9},{9,8},{10,11... | collective-permute-start | bytes 589832 | tf_op jit(solution)/shard_map/ppermute | solution.py:268
  142.0 11.1 %copy-start.2 = (bf16[128,6144]{1,0:T(8,128)(2,1)S(1)}, bf16[128,6144]{1,0:T(8,128)(2,1)}, u32[]{:S(2)}) copy-start(bf16[128,6144]{1,0:T(8,128)(2,1)} %res_ref.1) | copy-start | bytes 4718596
  144.1 7.7 %collective-permute-start.33 = (bf16[128,768]{1,0:T(8,128)(2,1)}, bf16[128,768]{1,0:T(8,128)(2,1)}, u32[]{:S(2)}, u32[]{:S(2)}) collective-permute-start(bf16[128,768]{1,0:T(8,128)(2,1)} %get-tuple-element.103), channel_id=1, source_target_pairs={{0,1},{1,0},{2,3},{3,2},{4,5},{5,4},{6,7},{7,6},{8,9},{9,8},{10,11... | collective-permute-start | bytes 589832 | tf_op jit(solution)/shard_map/ppermute | solution.py:268
  149.3 3.8 %collective-permute-start.34 = (bf16[128,768]{1,0:T(8,128)(2,1)}, bf16[128,768]{1,0:T(8,128)(2,1)}, u32[]{:S(2)}, u32[]{:S(2)}) collective-permute-start(bf16[128,768]{1,0:T(8,128)(2,1)} %get-tuple-element.101), channel_id=1, source_target_pairs={{0,1},{1,0},{2,3},{3,2},{4,5},{5,4},{6,7},{7,6},{8,9},{9,8},{10,11... | collective-permute-start | bytes 589832 | tf_op jit(solution)/shard_map/ppermute | solution.py:268
